TPU v7x, 512 devices: a whole 4x4x16 slice. The times are simulated.
512 devices in a mesh: seq: 128 (over z, y, core), mp: 4 (over x).
Axes of the slice: x: 4, y: 4, z: 16, core: 2. Of those that a mesh axis runs over, the one named last changes fastest.
Arguments:
- queries: bfloat16 [8192, 2048], P('seq', 'mp'), may hold values from -14 to 14
- keys: bfloat16 [8192, 2048], P('seq', 'mp'), may hold values from -14 to 14
- values: bfloat16 [8192, 2048], P('seq', 'mp'), may hold values from -6 to 6
- stream: bfloat16 [8192, 2048], P('seq', 'mp'), may hold values from -6 to 6
- seg_lengths: int32 [64], replicated, may hold values from 1 to 256, 8192 in all
- gain: float32 [2048], replicated, may hold values from 0.5 to 1.5
- w_out: bfloat16 [2048, 2048], P('mp', 'seq'), may hold values from -0.125 to 0.125
- w_gate: bfloat16 [2048, 3072], P('seq', 'mp'), may hold values from -0.125 to 0.125
- w_up: bfloat16 [2048, 3072], P('seq', 'mp'), may hold values from -0.125 to 0.125
- w_down: bfloat16 [3072, 2048], P('mp', 'seq'), may hold values from -0.109375 to 0.109375
Outputs:
- mixed: bfloat16 [8192, 2048], P('seq', 'mp')
Inputs may be any that keep to these rules, and one draw needn't show every extreme that they name: `seg_lengths`: the segments of landmarks 0 to 63 follow one another and cover the document's 8192 tokens.
All inputs are finite; a program needn't handle non-finite values.
Results may differ from a plain program's by a relative error of at most 0.014.
Values may be sent and summed in bfloat16 or wider, within the bound.
No kernel may reach another device: no remote copies, remote signals or barrier semaphores. Data moves between devices by JAX's collectives and lax.ppermute only.
A program may use at most 64 MiB of HBM per device.

v0:
```python
import math

import jax
import jax.numpy as jnp
from jax import lax
from jax.sharding import PartitionSpec as P

PINV_ITERS = 6
HEAD = 128


HIGH_ACCURACY = lax.Precision.HIGHEST
EPS = 1e-05


def inverse_rounds(anchor_block):
    eye = jnp.eye(anchor_block.shape[-1], dtype=jnp.float32)
    col_most = jnp.max(jnp.sum(anchor_block, axis=1), axis=-1)
    row_most = jnp.max(jnp.sum(anchor_block, axis=2), axis=-1)
    approx = jnp.swapaxes(anchor_block, 1, 2) / (col_most * row_most)[:, None, None]
    for step in range(PINV_ITERS):
        prod = jnp.einsum("hij,hjk->hik", anchor_block, approx, precision=HIGH_ACCURACY)
        inner = 7.0 * eye - prod
        inner = 15.0 * eye - jnp.einsum("hij,hjk->hik", prod, inner, precision=HIGH_ACCURACY)
        inner = 13.0 * eye - jnp.einsum("hij,hjk->hik", prod, inner, precision=HIGH_ACCURACY)
        approx = 0.25 * jnp.einsum("hij,hjk->hik", approx, inner, precision=HIGH_ACCURACY)
    return approx


def on_device(queries, keys, values, stream, seg_lengths, gain, w_out, w_gate, w_up, w_down):
    tok = queries.shape[0]
    width = queries.shape[1]
    heads = width // HEAD
    marks = seg_lengths.shape[0]
    score_scale = 1.0 / math.sqrt(HEAD)
    ends = jnp.cumsum(seg_lengths)
    starts = ends - seg_lengths
    place = lax.axis_index("seq") * tok + jnp.arange(tok, dtype=jnp.int32)
    member = ((place[:, None] >= starts[None, :]) & (place[:, None] < ends[None, :])).astype(
        jnp.bfloat16
    )
    query_part = jnp.dot(member.T, queries, preferred_element_type=jnp.float32)
    key_part = jnp.dot(member.T, keys, preferred_element_type=jnp.float32)
    query_sum, key_sum = lax.psum((query_part, key_part), "seq")
    counts = seg_lengths.astype(jnp.float32)[:, None]
    query_anchors = (query_sum / counts).reshape(marks, heads, HEAD)
    key_anchors = (key_sum / counts).reshape(marks, heads, HEAD)
    query_slice = queries.astype(jnp.float32).reshape(tok, heads, HEAD)
    key_slice = keys.astype(jnp.float32).reshape(tok, heads, HEAD)
    value_slice = values.astype(jnp.float32).reshape(tok, heads, HEAD)
    nearby_scores = jax.nn.softmax(
        jnp.einsum("brc,xrc->rbx", query_slice, key_anchors, precision=HIGH_ACCURACY) * score_scale,
        axis=-1,
    )
    anchor_block = jax.nn.softmax(
        jnp.einsum("oqc,bqc->qob", query_anchors, key_anchors, precision=HIGH_ACCURACY)
        * score_scale,
        axis=-1,
    )
    distant_scores = (
        jnp.einsum("gvb,lvb->vgl", query_anchors, key_slice, precision=HIGH_ACCURACY) * score_scale
    )
    local_peak = jnp.max(distant_scores, axis=-1)
    peak = lax.pmax(local_peak, "seq")
    layer_weights = jnp.exp(distant_scores - peak[..., None])
    local_mass = jnp.sum(layer_weights, axis=-1)
    slice_sum = jnp.einsum("vqb,bvn->vqn", layer_weights, value_slice, precision=HIGH_ACCURACY)
    mass, weighted = lax.psum((local_mass, slice_sum), "seq")
    collected_rows = weighted / mass[..., None]
    token_mixer = jnp.einsum(
        "svy,syc->svc", inverse_rounds(anchor_block), collected_rows, precision=HIGH_ACCURACY
    )
    attn = (
        jnp.einsum("ljz,lzx->jlx", nearby_scores, token_mixer, precision=HIGH_ACCURACY)
        .reshape(tok, width)
        .astype(jnp.bfloat16)
    )
    full_out = lax.all_gather(w_out, "seq", axis=1, tiled=True)
    out_terms = jnp.dot(attn, full_out, preferred_element_type=jnp.float32)
    proj = lax.psum_scatter(
        out_terms.astype(jnp.bfloat16), "mp", scatter_dimension=1, tiled=True
    ).astype(jnp.float32)
    resid = (stream.astype(jnp.float32) + proj).astype(jnp.bfloat16)
    whole = lax.all_gather(resid, "mp", axis=1, tiled=True)
    whole32 = whole.astype(jnp.float32)
    meansq = jnp.mean(whole32 * whole32, axis=-1, keepdims=True)
    normed = (whole32 * lax.rsqrt(meansq + EPS) * gain[None, :]).astype(jnp.bfloat16)
    full_gate, full_up = (
        lax.all_gather(w_gate, "seq", axis=0, tiled=True),
        lax.all_gather(w_up, "seq", axis=0, tiled=True),
    )
    gate = jnp.dot(normed, full_gate, preferred_element_type=jnp.float32)
    upper = jnp.dot(normed, full_up, preferred_element_type=jnp.float32)
    hidden = (jax.nn.silu(gate) * upper).astype(jnp.bfloat16)
    full_down = lax.all_gather(w_down, "seq", axis=1, tiled=True)
    down_terms = jnp.dot(hidden, full_down, preferred_element_type=jnp.float32)
    ffn = lax.psum_scatter(
        down_terms.astype(jnp.bfloat16), "mp", scatter_dimension=1, tiled=True
    ).astype(jnp.float32)
    return (resid.astype(jnp.float32) + ffn).astype(jnp.bfloat16)


def solution(mesh):
    return jax.shard_map(
        on_device,
        mesh=mesh,
        in_specs=(
            P("seq", "mp"),
            P("seq", "mp"),
            P("seq", "mp"),
            P("seq", "mp"),
            P(),
            P(),
            P("mp", "seq"),
            P("seq", "mp"),
            P("seq", "mp"),
            P("mp", "seq"),
        ),
        out_specs=P("seq", "mp"),
        check_vma=False,
    )
```

profile of v0, /device:TPU:1, one launch (start us, length us, event | category | flops | bytes accessed | tf_op | source)
XLA Modules:
  0.0 1537.7 jit_solution(13063598890913038582)
XLA Ops:
  6.5 0.8 copy.40
  7.3 0.1 reduce-window.8
  7.4 0.1 reduce
  7.5 0.7 fusion.82
  8.3 1.8 fusion.60
  10.1 0.0 all-reduce.6.cloned.1.call-start
  10.1 0.9 fusion.59
  11.0 322.9 %all-reduce.4.cloned.1.call-done = f32[64,512]{1,0:T(8,128)} async-done(((f32[64,512]{1,0:T(8,128)}), f32[64,512]{1,0:T(8,128)}) %all-reduce.4.cloned.1.call-update) | async-done | bytes 131088 | tf_op jit(solution)/shard_map/psum | solution.py:44
  333.9 1.2 fusion.83
  335.1 248.6 %pmax.7 = f32[4,64]{1,0:T(4,128)S(1)} all-reduce(f32[4,64]{1,0:T(4,128)S(1)} %get-tuple-element.11), channel_id=1, replica_groups=mesh['seq'=128,'mp'=4] {'seq'}, use_global_device_ids=true, to_apply=%region_10.11 | all-reduce | flops 256 | bytes 2048 | tf_op jit(solution)/shard_map/pmax | solution.py:64
  583.7 1.8 fusion.29
  585.5 0.0 all-gather.5.cloned.1.call-start
  585.6 0.7 all-gather.5.cloned.1.call-update
  586.4 248.3 %psum.31 = f32[4,64]{1,0:T(4,128)S(1)} all-reduce(f32[4,64]{1,0:T(4,128)S(1)} %fusion.28), channel_id=1, replica_groups=mesh['seq'=128,'mp'=4] {'seq'}, use_global_device_ids=true, to_apply=%region_13.14 | all-reduce | flops 256 | bytes 2048 | tf_op jit(solution)/shard_map/psum | solution.py:68
  834.7 72.6 %all-reduce.6.cloned.1.call-done = (f32[64,512]{1,0:T(8,128)}, f32[4,64,128]{2,1,0:T(8,128)}) async-done(((f32[64,512]{1,0:T(8,128)}, f32[4,64,128]{2,1,0:T(8,128)}), (f32[64,512]{1,0:T(8,128)}, f32[4,64,128]{2,1,0:T(8,128)})) %all-reduce.6.cloned.1.call-update) | async-done | bytes 262160 | tf_op jit(solution)/shard_map/psum | solution.py:44
  907.2 1.3 fusion.85
  908.6 1.4 fusion.84
  910.0 0.1 fusion.80
  910.1 0.1 reduce_max.46
  910.3 0.1 reduce_max.47
  910.4 0.4 fusion.68
  910.8 0.3 convolution_subtract_fusion.11
  911.1 0.3 convolution_subtract_fusion.10
  911.4 0.3 convolution_multiply_fusion.8
  911.7 0.4 fusion.77
  912.1 0.3 convolution_subtract_fusion.9
  912.4 0.3 convolution_subtract_fusion.8
  912.6 0.3 convolution_multiply_fusion.7
  912.9 0.2 fusion.30
  913.1 0.4 fusion.75
  913.5 0.3 convolution_subtract_fusion.7
  913.8 0.3 convolution_subtract_fusion.6
  914.0 0.3 convolution_multiply_fusion.6
  914.3 0.4 fusion.73
  914.7 0.3 convolution_subtract_fusion.5
  915.0 0.3 convolution_subtract_fusion.4
  915.2 0.3 convolution_multiply_fusion.5
  915.5 0.4 fusion.71
  915.9 0.3 convolution_subtract_fusion.3
  916.2 0.3 convolution_subtract_fusion.2
  916.4 0.3 convolution_multiply_fusion.4
  916.7 0.4 fusion.69
  917.1 0.3 convolution_subtract_fusion.1
  917.4 0.3 convolution_subtract_fusion
  917.6 0.3 convolution_multiply_fusion.3
  917.9 0.4 fusion.22
  918.3 0.4 fusion.2
  918.6 129.7 %all-gather.5.cloned.1.call-done = bf16[512,2048]{0,1:T(8,128)(2,1)} async-done(((bf16[512,16]{0,1:T(8,128)(2,1)}), bf16[512,2048]{0,1:T(8,128)(2,1)}) %all-gather.5.cloned.1.call-update) | async-done | bytes 2097168 | tf_op jit(solution)/shard_map/all_gather | solution.py:78
  1048.3 3.0 convolution_convert_fusion.1
  1051.4 0.0 all-gather.7.cloned.1.call-start
  1051.5 0.5 all-gather.7.cloned.1.call-update
  1052.0 0.5 all-gather.11.cloned.1.call-update
  1052.6 0.7 all-gather.9.cloned.1.call-update
  1053.4 20.0 %reduce-scatter.3.cloned.1.call-done = bf16[64,512]{1,0:T(8,128)(2,1)} async-done(((bf16[64,2048]{1,0:T(8,128)(2,1)}), bf16[64,512]{1,0:T(8,128)(2,1)}) %reduce-scatter.3.cloned.1.call-update) | async-done | bytes 65552 | tf_op jit(solution)/shard_map/reduce_scatter | solution.py:80
  1073.3 0.9 add_convert_fusion.1
  1074.2 9.4 all_gather.16
  1083.6 0.2 fusion.3
  1083.7 136.8 %all-gather.7.cloned.1.call-done = bf16[2048,768]{1,0:T(8,128)(2,1)} async-done(((bf16[16,768]{1,0:T(8,128)(2,1)}), bf16[2048,768]{1,0:T(8,128)(2,1)}) %all-gather.7.cloned.1.call-update) | async-done | bytes 3145744 | tf_op jit(solution)/shard_map/all_gather | solution.py:89
  1220.6 2.6 fusion.36
  1223.2 138.2 %all-gather.11.cloned.1.call-done = bf16[768,2048]{0,1:T(8,128)(2,1)} async-done(((bf16[768,16]{0,1:T(8,128)(2,1)}), bf16[768,2048]{0,1:T(8,128)(2,1)}) %all-gather.11.cloned.1.call-update) | async-done | bytes 3145744 | tf_op jit(solution)/shard_map/all_gather | solution.py:95
  1361.4 140.9 %all-gather.9.cloned.1.call-done = bf16[2048,768]{1,0:T(8,128)(2,1)} async-done(((bf16[16,768]{1,0:T(8,128)(2,1)}), bf16[2048,768]{1,0:T(8,128)(2,1)}) %all-gather.9.cloned.1.call-update) | async-done | bytes 3145744 | tf_op jit(solution)/shard_map/all_gather | solution.py:90
  1502.2 5.3 convolution_convert_fusion
  1507.6 21.8 %reduce-scatter.5.cloned.1.call-done = bf16[64,512]{1,0:T(8,128)(2,1)} async-done(((bf16[64,2048]{1,0:T(8,128)(2,1)}), bf16[64,512]{1,0:T(8,128)(2,1)}) %reduce-scatter.5.cloned.1.call-update) | async-done | bytes 65552 | tf_op jit(solution)/shard_map/reduce_scatter | solution.py:97
  1529.3 1.5 add_convert_fusion
  (23 shorter events, 0.4 us)
Async XLA Ops:
  6.5 3.6 copy-start
  6.5 327.4 %all-reduce.4.cloned.1.call-start = ((), (), s32[]{:S(2)}) async-start(), calls=%async_computation.2 | async-start | bytes 262144 | tf_op jit(solution)/shard_map/psum | solution.py:44
  10.1 897.2 %all-reduce.6.cloned.1.call-start = ((), (), s32[]{:S(2)}) async-start(), calls=%async_computation.9 | async-start | bytes 524288 | tf_op jit(solution)/shard_map/psum | solution.py:44
  585.5 462.8 %all-gather.5.cloned.1.call-start = ((), (), s32[]{:S(2)}) async-start(), calls=%async_computation.3 | async-start | bytes 2113536 | tf_op jit(solution)/shard_map/all_gather | solution.py:78
  586.3 487.1 %reduce-scatter.3.cloned.1.call-start = ((), (), s32[]{:S(2)}) async-start(), calls=%async_computation.4 | async-start | bytes 327680 | tf_op jit(solution)/shard_map/reduce_scatter | solution.py:80
  913.8 4.2 copy-start.3
  916.2 157.2 %copy-start.1 = (bf16[64,512]{1,0:T(8,128)(2,1)S(1)}, bf16[64,512]{1,0:T(8,128)(2,1)}, u32[]{:S(2)}) copy-start(bf16[64,512]{1,0:T(8,128)(2,1)} %param.13) | copy-start | bytes 196612
  916.7 303.9 %copy-start.2 = (f32[2048]{0:T(1024)S(1)}, f32[2048]{0:T(1024)}, u32[]{:S(2)}) copy-start(f32[2048]{0:T(1024)} %param.15) | copy-start | bytes 24580
  1051.4 169.2 %all-gather.7.cloned.1.call-start = ((), (), s32[]{:S(2)}) async-start(), calls=%async_computation.5 | async-start | bytes 3170304 | tf_op jit(solution)/shard_map/all_gather | solution.py:89
  1052.0 309.4 %all-gather.11.cloned.1.call-start = ((), (), s32[]{:S(2)}) async-start(), calls=%async_computation.7 | async-start | bytes 3170304 | tf_op jit(solution)/shard_map/all_gather | solution.py:95
  1052.6 449.6 %all-gather.9.cloned.1.call-start = ((), (), s32[]{:S(2)}) async-start(), calls=%async_computation.6 | async-start | bytes 3170304 | tf_op jit(solution)/shard_map/all_gather | solution.py:90
  1053.3 476.0 %reduce-scatter.5.cloned.1.call-start = ((), (), s32[]{:S(2)}) async-start(), calls=%async_computation.8 | async-start | bytes 327680 | tf_op jit(solution)/shard_map/reduce_scatter | solution.py:97
Sparse Core Ops, SparseCore 0:
  10.8 323.0 all-reduce.3
  585.7 321.5 all-reduce.5
  910.4 137.9 all-gather.4
  1051.5 21.7 reduce-scatter.2
  1076.8 143.7 all-gather.6
  1224.0 137.2 all-gather.10
  1364.9 137.2 all-gather.8
  1507.7 21.6 reduce-scatter.4
where the time goes:
time: 1540 us
  waiting for transfers between devices  985 us (64%)
  blocking collectives  506 us (33%)
  matrix products  27.2 us (2%)
    psum x2, waiting for transfers between devices, on_device(): query_sum, key_sum = lax.psum((query_part, key_part), 'seq')  395 us
    pmax x1, blocking collectives, on_device(): peak = lax.pmax(local_peak, 'seq')  249 us
    psum x1, blocking collectives, on_device(): mass, weighted = lax.psum((local_mass, slice_sum), 'seq')  248 us
    all_gather x1, waiting for transfers between devices, on_device(): lax.all_gather(w_up, 'seq', axis=0, tiled=True)  141 us
    all_gather x1, waiting for transfers between devices, on_device(): full_down = lax.all_gather(w_down, 'seq', axis=1, tiled=True)  138 us
    all_gather x1, waiting for transfers between devices, on_device(): lax.all_gather(w_gate, 'seq', axis=0, tiled=True)  137 us
    all_gather x1, waiting for transfers between devices, on_device(): full_out = lax.all_gather(w_out, 'seq', axis=1, tiled=True)  130 us
  transfers between devices with their start and end apart: 8, of which 8 were waited for; matrix products, arithmetic and copies ran while one was open for 1% of the time, Pallas kernels for 0%

commit v1 on v0

v1 whole, which is shorter than its diff:
```python
import math

import jax
import jax.numpy as jnp
from jax import lax
from jax.sharding import Mesh
from jax.sharding import PartitionSpec as P

PINV_ITERS = 6
HEAD = 128
EPS = 1e-05
HI = lax.Precision.HIGHEST
F32 = jnp.float32
BF16 = jnp.bfloat16


def mm(spec, a, b):
    return jnp.einsum(spec, a, b, precision=HI, preferred_element_type=F32)


def inverse_rounds(land):
    eye = jnp.eye(land.shape[-1], dtype=F32)
    col_most = jnp.max(jnp.sum(land, axis=0))
    row_most = jnp.max(jnp.sum(land, axis=1))
    approx = land.T / (col_most * row_most)
    for _ in range(PINV_ITERS):
        prod = mm("ij,jk->ik", land, approx)
        inner = 7.0 * eye - prod
        inner = 15.0 * eye - mm("ij,jk->ik", prod, inner)
        inner = 13.0 * eye - mm("ij,jk->ik", prod, inner)
        approx = 0.25 * mm("ij,jk->ik", approx, inner)
    return approx


def tiles(a):
    return a[:, :512].reshape(a.shape[0], 4, 128).transpose(1, 0, 2)


def halves(a):
    return a[:, 512:].reshape(a.shape[0], 4, 64).transpose(1, 0, 2)


def on_device(queries, keys, values, stream, seg_lengths, gain, w_out, w_gate, w_up, w_down):
    scale = 1.0 / math.sqrt(HEAD)
    z, c = lax.axis_index("z"), lax.axis_index("c")
    down_t, out_t = w_down.T, w_out.T
    mixed_half = jnp.concatenate([halves(w_gate), halves(w_up)], axis=-1)
    down_half = jnp.pad(halves(down_t), ((0, 0), (0, 0), (0, 64)))
    pack = jnp.concatenate(
        [
            tiles(queries),
            tiles(keys),
            tiles(values),
            tiles(w_gate),
            tiles(w_up),
            mixed_half,
            tiles(down_t),
            down_half,
            tiles(out_t),
        ],
        axis=1,
    )
    got = lax.all_to_all(pack, "y", 0, 0)
    q = got[:, 0:64].reshape(256, HEAD)
    k = got[:, 64:128].reshape(256, HEAD)
    v = got[:, 128:192].reshape(256, HEAD)
    weights = lax.all_gather(got[:, 192:], ("z", "c"), axis=0)
    weights = (
        weights.reshape(16, 2, 4, 6, 16, 128).transpose(3, 0, 2, 1, 4, 5).reshape(6, 2048, 128)
    )

    ends = jnp.cumsum(seg_lengths)
    starts = ends - seg_lengths
    block = jnp.arange(4, dtype=jnp.int32)[:, None] * 2 + z * 8 + c
    place = (block * 64 + jnp.arange(64, dtype=jnp.int32)[None, :]).reshape(256)
    member = ((place[:, None] >= starts[None, :]) & (place[:, None] < ends[None, :])).astype(BF16)
    sums = jnp.stack(
        [
            jnp.dot(member.T, q, preferred_element_type=F32),
            jnp.dot(member.T, k, preferred_element_type=F32),
        ]
    )
    mine = jnp.sum(lax.all_to_all(sums, "c", 0, 0), axis=0)
    mine = jnp.sum(lax.all_gather(mine, "z", axis=0), axis=0)
    marks = lax.all_gather(mine / seg_lengths.astype(F32)[:, None], "c", axis=0)
    qm, km = marks[0], marks[1]

    q32, k32, v32 = q.astype(F32), k.astype(F32), v.astype(F32)
    far = mm("jd,td->jt", qm, k32) * scale
    peak = jnp.max(far, axis=-1, keepdims=True)
    far = jnp.exp(far - peak)
    mass = jnp.sum(far, axis=-1, keepdims=True)
    part = mm("jt,td->jd", far, v32)
    stats = jnp.concatenate([peak.reshape(32, 1, 2), mass.reshape(32, 1, 2)], axis=-1)
    send = jnp.concatenate(
        [part.reshape(32, 2, HEAD), jnp.pad(stats, ((0, 0), (0, 0), (0, 124)))], axis=1
    )
    parts = lax.all_to_all(send, ("z", "c"), 0, 0)
    peaks, masses = parts[:, 2, 0:2], parts[:, 2, 2:4]
    factor = jnp.exp(peaks - jnp.max(peaks, axis=0, keepdims=True))
    total = jnp.sum(factor * masses, axis=0)
    gathered = jnp.sum(factor[:, :, None] * parts[:, 0:2], axis=0) / total[:, None]
    gathered = lax.all_to_all(
        jnp.broadcast_to(gathered[None], (32, 2, HEAD)), ("z", "c"), 0, 0
    ).reshape(64, HEAD)

    near = jax.nn.softmax(mm("td,jd->tj", q32, km) * scale, axis=-1)
    land = jax.nn.softmax(mm("id,jd->ij", qm, km) * scale, axis=-1)
    mixer = mm("ij,jd->id", inverse_rounds(land), gathered)
    attn = mm("tj,jd->td", near, mixer).astype(BF16)

    def scatter(terms):
        terms = terms.astype(BF16).reshape(4, 64, 4, 512).transpose(0, 2, 1, 3).reshape(16, 64, 512)
        return jnp.sum(lax.all_to_all(terms, ("y", "x"), 0, 0).astype(F32), axis=0)

    proj = scatter(jnp.einsum("td,ed->te", attn, weights[5], preferred_element_type=F32))
    resid = (stream.astype(F32) + proj).astype(BF16)
    whole = lax.all_to_all(jnp.broadcast_to(resid[None], (16, 64, 512)), ("y", "x"), 0, 0)
    whole = whole.reshape(4, 4, 64, 512).transpose(0, 2, 1, 3).reshape(256, 2048).astype(F32)
    meansq = jnp.mean(whole * whole, axis=-1, keepdims=True)
    normed = (whole * lax.rsqrt(meansq + EPS) * gain[None, :]).astype(BF16)
    first = jnp.einsum("tk,jkl->jtl", normed, weights[0:3], preferred_element_type=F32)
    gate = jnp.concatenate([first[0], first[2][:, :64]], axis=-1)
    up = jnp.concatenate([first[1], first[2][:, 64:]], axis=-1)
    hidden = (jax.nn.silu(gate) * up).astype(BF16)
    down = jnp.concatenate([weights[3], weights[4][:, :64]], axis=-1)
    ffn = scatter(jnp.einsum("th,eh->te", hidden, down, preferred_element_type=F32))
    return (resid.astype(F32) + ffn).astype(BF16)


def solution(mesh):
    fine = Mesh(mesh.devices.reshape(16, 4, 2, 4), ("z", "y", "c", "x"))
    seq = ("z", "y", "c")
    return jax.shard_map(
        on_device,
        mesh=fine,
        in_specs=(
            P(seq, "x"),
            P(seq, "x"),
            P(seq, "x"),
            P(seq, "x"),
            P(),
            P(),
            P("x", seq),
            P(seq, "x"),
            P(seq, "x"),
            P("x", seq),
        ),
        out_specs=P(seq, "x"),
        check_vma=False,
    )
```

time: 1540 us -> 228 us (0.15)
  waiting for transfers between devices: 985 us -> 62.1 us
  blocking collectives: 506 us -> 90.4 us
  local copies, waits for them, and re-layouts: 0.8 us -> 25.8 us
  starting transfers between devices: 0.28 us -> 20.2 us
  matrix products: 27.2 us -> 7.97 us
    all_gather x4 -> x1, waiting for transfers between devices: 546 us -> 22.2 us  [on_device(): weights = lax.all_gather(got[:, 192:], ('z', 'c'), axis=0)]
    psum x2 -> x0, waiting for transfers between devices: 395 us -> none  [on_device(): query_sum, key_sum = lax.psum((query_part, key_part), 'seq')]
    pmax x1 -> x0, blocking collectives: 249 us -> none  [on_device(): peak = lax.pmax(local_peak, 'seq')]
    psum x1 -> x0, blocking collectives: 248 us -> none  [on_device(): mass, weighted = lax.psum((local_mass, slice_sum), 'seq')]
    all_to_all x0 -> x3, blocking collectives: none -> 54.6 us  [the longest x2 44.7 us: scatter(): return jnp.sum(lax.all_to_all(terms, ('y', 'x'), 0, 0).astype(F32), axis=0)]
    reduce_scatter x2 -> x0, waiting for transfers between devices: 41.7 us -> none  [the longest x1 21.8 us: on_device(): lax.psum_scatter(down_terms.astype(jnp.bfloat16), 'mp', scatter_dimension...]
    all_to_all x0 -> x4, waiting for transfers between devices: none -> 39.9 us  [the longest x1 13 us: on_device(): lax.all_to_all(jnp.broadcast_to(gathered[None], (32, 2, HEAD)), ('z', 'c'...]
    all_gather x1 -> x2, blocking collectives: 9.37 us -> 35.9 us  [the longest x1 27.3 us: on_device(): mine = jnp.sum(lax.all_gather(mine, 'z', axis=0), axis=0)]
  transfers between devices with their start and end apart: 8 -> 5, of which waited for: 8 -> 5; matrix products, arithmetic and copies ran while one was open for 1% -> 6% of each run, Pallas kernels for 0% -> 0%
where the time goes in v1:
time: 228 us; the launch traced here: 226 us
  blocking collectives  90.4 us (40%)
  waiting for transfers between devices  62.1 us (27%)
  local copies, waits for them, and re-layouts  25.8 us (11%)
  starting transfers between devices  20.2 us (9%)
  between operations  15.3 us (7%)
  matrix products  7.97 us (3%)
  other arithmetic  4.31 us (2%)
    all_to_all x2, blocking collectives, scatter(): return jnp.sum(lax.all_to_all(terms, ('y', 'x'), 0, 0).astype(F32), axis=0)  44.7 us
    all_gather x1, blocking collectives, on_device(): mine = jnp.sum(lax.all_gather(mine, 'z', axis=0), axis=0)  27.3 us
    all_gather x1, waiting for transfers between devices, on_device(): weights = lax.all_gather(got[:, 192:], ('z', 'c'), axis=0)  22.2 us
    all_to_all x1, waiting for transfers between devices, on_device(): lax.all_to_all(jnp.broadcast_to(gathered[None], (32, 2, HEAD)), ('z', 'c'...  13 us
    all_to_all x1, waiting for transfers between devices, on_device(): parts = lax.all_to_all(send, ('z', 'c'), 0, 0)  11 us
    all_to_all x1, waiting for transfers between devices, on_device(): lax.all_to_all(jnp.broadcast_to(resid[None], (16, 64, 512)), ('y', 'x'),...  10.7 us
    all_to_all x1, blocking collectives, on_device(): mine = jnp.sum(lax.all_to_all(sums, 'c', 0, 0), axis=0)  9.88 us
    all_gather x1, blocking collectives, on_device(): marks = lax.all_gather(mine / seg_lengths.astype(F32)[:, None], 'c', axis=0)  8.61 us
  transfers between devices with their start and end apart: 5, of which 5 were waited for; matrix products, arithmetic and copies ran while one was open for 6% of the time, Pallas kernels for 0%

profile of v1, /device:TPU:1, one launch (start us, length us, event | category | flops | bytes accessed | tf_op | source)
XLA Modules:
  0.0 226.1 jit_solution(7001369280153762893)
XLA Ops:
  6.5 0.7 slice.109
  7.2 0.7 slice.108
  8.0 0.7 slice.84
  8.7 0.7 slice.82
  9.4 0.7 slice.85
  10.1 0.7 slice.83
  11.1 0.7 reshape.214
  11.8 0.9 reshape.205
  12.7 0.9 reshape.206
  13.6 0.9 reshape.207
  14.8 0.7 copy.103
  15.5 5.0 %all-to-all-start = ((bf16[4,288,128]{2,1,0:T(8,128)(2,1)}), bf16[4,288,128]{2,1,0:T(8,128)(2,1)S(1)}, u32[]{:S(2)}, u32[]{:S(2)}) async-start(bf16[4,288,128]{2,1,0:T(8,128)(2,1)} %copy.103), calls=%async_computation | async-start | bytes 589824 | tf_op jit(solution)/shard_map/all_to_all | solution.py:63
  21.0 5.2 %all-to-all-done = bf16[4,288,128]{2,1,0:T(8,128)(2,1)S(1)} async-done(((bf16[4,288,128]{2,1,0:T(8,128)(2,1)}), bf16[4,288,128]{2,1,0:T(8,128)(2,1)S(1)}, u32[]{:S(2)}, u32[]{:S(2)}) %all-to-all-start) | async-done | bytes 294944 | tf_op jit(solution)/shard_map/all_to_all | solution.py:63
  26.2 0.3 convolution_bitcast_fusion.1
  26.5 0.3 convolution_bitcast_fusion.2
  26.8 9.9 %all_to_all.35 = f32[2,64,128]{2,1,0:T(8,128)S(1)} all-to-all(f32[2,64,128]{2,1,0:T(8,128)S(1)} %pad_maximum_fusion.1), channel_id=1, replica_groups=mesh['z'=16,'y'=4,'c'=2,'x'=4] {'c'}, dimensions={0} | all-to-all | bytes 131072 | tf_op jit(solution)/shard_map/all_to_all | solution.py:83
  36.7 27.3 %all-gather = f32[1024,128]{1,0:T(8,128)S(1)} all-gather(f32[64,128]{1,0:T(8,128)S(1)} %reduce_sum.110), channel_id=2, replica_groups=mesh['z'=16,'y'=4,'c'=2,'x'=4] {'z'}, dimensions={0}, use_global_device_ids=true | all-gather | bytes 557056 | tf_op jit(solution)/shard_map/all_gather | solution.py:84
  64.1 8.6 %all_gather.18 = f32[2,64,128]{2,1,0:T(8,128)S(1)} all-gather(f32[1,64,128]{2,1,0:T(8,128)S(1)} %bitcast_divide_fusion), channel_id=1, replica_groups=mesh['z'=16,'y'=4,'c'=2,'x'=4] {'c'}, dimensions={0}, use_global_device_ids=true | all-gather | bytes 98304 | tf_op jit(solution)/shard_map/all_gather | solution.py:85
  72.7 0.3 fusion.78
  73.0 0.2 fusion.79
  73.2 0.6 slice.118
  74.0 0.2 fusion.72
  74.3 0.6 reduce_max.56
  74.9 0.7 reduce_max.57
  77.0 0.2 fusion.39
  78.1 0.7 copy.106
  78.8 7.6 %all-to-all-start.2 = ((f32[32,3,128]{2,1,0:T(4,128)}), f32[32,3,128]{2,1,0:T(4,128)S(1)}, u32[]{:S(2)}, u32[]{:S(2)}) async-start(f32[32,3,128]{2,1,0:T(4,128)} %copy.106), calls=%async_computation.2 | async-start | bytes 131072 | tf_op jit(solution)/shard_map/all_to_all | solution.py:98
  86.4 0.2 fusion.66
  87.1 0.2 fusion.64
  87.9 0.2 fusion.62
  88.7 0.2 fusion.60
  89.4 0.2 fusion.58
  89.9 0.2 fusion.80
  90.3 11.0 %all-to-all-done.2 = f32[32,3,128]{2,1,0:T(4,128)S(1)} async-done(((f32[32,3,128]{2,1,0:T(4,128)}), f32[32,3,128]{2,1,0:T(4,128)S(1)}, u32[]{:S(2)}, u32[]{:S(2)}) %all-to-all-start.2) | async-done | bytes 49184 | tf_op jit(solution)/shard_map/all_to_all | solution.py:98
  101.5 0.2 fusion.41
  102.0 0.6 broadcast_in_dim.4
  102.6 3.9 %all-to-all-start.3 = ((f32[32,2,128]{2,1,0:T(2,128)}), f32[32,2,128]{2,1,0:T(2,128)S(1)}, u32[]{:S(2)}, u32[]{:S(2)}) async-start(f32[32,2,128]{2,1,0:T(2,128)} %broadcast_in_dim.4), calls=%async_computation.3 | async-start | bytes 65536 | tf_op jit(solution)/shard_map/all_to_all | solution.py:103
  106.7 13.0 %all-to-all-done.3 = f32[32,2,128]{2,1,0:T(2,128)S(1)} async-done(((f32[32,2,128]{2,1,0:T(2,128)}), f32[32,2,128]{2,1,0:T(2,128)S(1)}, u32[]{:S(2)}, u32[]{:S(2)}) %all-to-all-start.3) | async-done | bytes 32800 | tf_op jit(solution)/shard_map/all_to_all | solution.py:103
  119.9 0.4 convolution_convert_fusion.2
  120.3 22.2 %all-gather.4.cloned.1.call-done = bf16[128,96,128]{2,1,0:T(8,128)(2,1)} async-done(((bf16[4,96,128]{2,1,0:T(8,128)(2,1)}), bf16[128,96,128]{2,1,0:T(8,128)(2,1)}) %all-gather.4.cloned.1.call-update) | async-done | bytes 3145744 | tf_op jit(solution)/shard_map/all_gather | solution.py:67
  142.5 2.6 %fusion.73 = (bf16[1,16,4,2,16,128]{5,4,0,2,3,1:T(8,128)(2,1)S(1)}, bf16[1,16,4,2,16,128]{5,4,0,2,3,1:T(8,128)(2,1)}, bf16[1,16,4,2,16,128]{5,4,0,2,3,1:T(8,128)(2,1)S(1)}) fusion(bf16[6,16,4,2,16,128]{5,4,0,2,3,1:T(8,128)(2,1)} %bitcast.135), kind=kLoop, calls=%fused_computation.137 | loop fusion | bytes 3145728 | tf_op jit(solution)/shard_map/slice | solution.py:116
  145.1 0.4 convolution_convert_fusion
  145.6 0.8 reshape.222
  146.4 0.2 copy.111
  146.6 23.9 %all_to_all.36 = bf16[16,64,512]{2,1,0:T(8,128)(2,1)S(1)} all-to-all(bf16[16,64,512]{2,1,0:T(8,128)(2,1)S(1)} %bitcast.133), channel_id=1, replica_groups=mesh['z'=16,'y'=4,'c'=2,'x'=4] {'y','x'}, dimensions={0} | all-to-all | bytes 2097152 | tf_op jit(solution)/shard_map/all_to_all | solution.py:114
  170.7 1.1 broadcast_in_dim.5
  171.8 3.7 %all-to-all-start.5 = ((bf16[16,64,512]{2,1,0:T(8,128)(2,1)}), bf16[16,64,512]{2,1,0:T(8,128)(2,1)S(1)}, u32[]{:S(2)}, u32[]{:S(2)}) async-start(bf16[16,64,512]{2,1,0:T(8,128)(2,1)} %broadcast_in_dim.5), calls=%async_computation.5 | async-start | bytes 2097152 | tf_op jit(solution)/shard_map/all_to_all | solution.py:118
  175.4 1.7 slice.120
  177.2 0.4 copy.112
  177.7 0.6 copy-done
  178.2 0.9 copy.116
  179.1 0.9 copy.115
  180.0 10.7 %all-to-all-done.5 = bf16[16,64,512]{2,1,0:T(8,128)(2,1)S(1)} async-done(((bf16[16,64,512]{2,1,0:T(8,128)(2,1)}), bf16[16,64,512]{2,1,0:T(8,128)(2,1)S(1)}, u32[]{:S(2)}, u32[]{:S(2)}) %all-to-all-start.5) | async-done | bytes 1048608 | tf_op jit(solution)/shard_map/all_to_all | solution.py:118
  190.7 0.3 fusion
  191.0 0.3 fusion.3
  191.3 1.8 copy.113
  193.1 1.8 reshape.231
  194.9 0.6 convolution_bitcast_fusion
  195.6 0.3 copy-done.1
  196.1 0.5 convolution_convert_fusion.1
  196.6 0.8 reshape.224
  197.4 0.2 copy.117
  197.6 20.8 %all_to_all.37 = bf16[16,64,512]{2,1,0:T(8,128)(2,1)S(1)} all-to-all(bf16[16,64,512]{2,1,0:T(8,128)(2,1)S(1)} %bitcast.134), channel_id=1, replica_groups=mesh['z'=16,'y'=4,'c'=2,'x'=4] {'y','x'}, dimensions={0} | all-to-all | bytes 2097152 | tf_op jit(solution)/shard_map/all_to_all | solution.py:114
  218.6 0.6 add_convert_fusion
  (82 shorter events, 6.1 us)
Async XLA Ops:
  6.5 14.1 %copy-start.5 = (s32[64]{0:T(128)S(1)}, s32[64]{0:T(128)}, u32[]{:S(2)}) copy-start(s32[64]{0:T(128)} %param.14) | copy-start | bytes 772
  15.5 10.7 %all-to-all-start = ((bf16[4,288,128]{2,1,0:T(8,128)(2,1)}), bf16[4,288,128]{2,1,0:T(8,128)(2,1)S(1)}, u32[]{:S(2)}, u32[]{:S(2)}) async-start(bf16[4,288,128]{2,1,0:T(8,128)(2,1)} %copy.103), calls=%async_computation | async-start | bytes 589824 | tf_op jit(solution)/shard_map/all_to_all | solution.py:63
  20.5 122.0 %all-gather.4.cloned.1.call-start = ((), (), s32[]{:S(2)}) async-start(), calls=%async_computation.7 | async-start | bytes 3244032 | tf_op jit(solution)/shard_map/all_gather | solution.py:67
  78.8 22.4 %all-to-all-start.2 = ((f32[32,3,128]{2,1,0:T(4,128)}), f32[32,3,128]{2,1,0:T(4,128)S(1)}, u32[]{:S(2)}, u32[]{:S(2)}) async-start(f32[32,3,128]{2,1,0:T(4,128)} %copy.106), calls=%async_computation.2 | async-start | bytes 131072 | tf_op jit(solution)/shard_map/all_to_all | solution.py:98
  102.6 17.1 %all-to-all-start.3 = ((f32[32,2,128]{2,1,0:T(2,128)}), f32[32,2,128]{2,1,0:T(2,128)S(1)}, u32[]{:S(2)}, u32[]{:S(2)}) async-start(f32[32,2,128]{2,1,0:T(2,128)} %broadcast_in_dim.4), calls=%async_computation.3 | async-start | bytes 65536 | tf_op jit(solution)/shard_map/all_to_all | solution.py:103
  146.6 24.0 %copy-start.3 = (bf16[64,512]{1,0:T(8,128)(2,1)S(1)}, bf16[64,512]{1,0:T(8,128)(2,1)}, u32[]{:S(2)}) copy-start(bf16[64,512]{1,0:T(8,128)(2,1)} %param.13) | copy-start | bytes 196612
  170.5 4.9 %copy-start.4 = (f32[2048]{0:T(1024)S(1)}, f32[2048]{0:T(1024)}, u32[]{:S(2)}) copy-start(f32[2048]{0:T(1024)} %param.15) | copy-start | bytes 24580
  171.8 18.9 %all-to-all-start.5 = ((bf16[16,64,512]{2,1,0:T(8,128)(2,1)}), bf16[16,64,512]{2,1,0:T(8,128)(2,1)S(1)}, u32[]{:S(2)}, u32[]{:S(2)}) async-start(bf16[16,64,512]{2,1,0:T(8,128)(2,1)} %broadcast_in_dim.5), calls=%async_computation.5 | async-start | bytes 2097152 | tf_op jit(solution)/shard_map/all_to_all | solution.py:118
  177.2 1.0 copy-start
  194.9 1.0 copy-start.1
  194.9 1.2 copy-start.2
Sparse Core Ops, SparseCore 0:
  74.0 68.4 all-gather.3

commit v2 on v1

v2 whole, which is shorter than its diff:
```python
import math

import jax
import jax.numpy as jnp
from jax import lax
from jax.experimental import pallas as pl
from jax.experimental.pallas import tpu as pltpu
from jax.sharding import Mesh
from jax.sharding import PartitionSpec as P

PINV_ITERS = 6
HEAD = 128
EPS = 1e-05
SCALE = 1.0 / math.sqrt(HEAD)
HI = lax.Precision.HIGHEST
F32 = jnp.float32
BF16 = jnp.bfloat16


def mm(spec, a, b):
    return jnp.einsum(spec, a, b, precision=HI, preferred_element_type=F32)


def dot(a, b, dims, precision=None):
    return lax.dot_general(
        a, b, (dims, ((), ())), precision=precision, preferred_element_type=F32
    )


def kernel_call(body, out_shape, n_in, scratch=(), cost=None):
    whole = pl.BlockSpec(memory_space=pltpu.VMEM)
    many = isinstance(out_shape, (list, tuple))
    return pl.pallas_call(
        body,
        out_shape=out_shape,
        in_specs=[whole] * n_in,
        out_specs=[whole] * len(out_shape) if many else whole,
        scratch_shapes=list(scratch),
        cost_estimate=cost,
    )


def shape(dims, dtype):
    return jax.ShapeDtypeStruct(dims, dtype)


def pack_body(q, k, v, wg, wu, wd, wo, out):
    for y in range(4):
        tile = slice(y * 128, y * 128 + 128)
        out[y, 0:64] = q[:, tile]
        out[y, 64:128] = k[:, tile]
        out[y, 128:192] = v[:, tile]
        out[y, 192:208] = wg[:, tile]
        out[y, 208:224] = wu[:, tile]
        last = slice(512 + (y // 2) * 128, 640 + (y // 2) * 128)
        lane = lax.broadcasted_iota(jnp.int32, (16, 128), 1)
        g, u, d = (w[:, last].astype(F32) for w in (wg, wu, wd))
        if y % 2 == 0:
            mixed = jnp.where(lane < 64, g, pltpu.roll(u, 64, 1))
        else:
            mixed = jnp.where(lane < 64, pltpu.roll(g, 64, 1), u)
            d = pltpu.roll(d, 64, 1)
        out[y, 224:240] = mixed.astype(BF16)
        out[y, 240:256] = wd[:, tile]
        out[y, 256:272] = jnp.where(lane < 64, d, 0.0).astype(BF16)
        out[y, 272:288] = wo[:, tile]


def marks_body(got, starts, ends, sums, weights):
    weights[...] = got[:, 192:288]
    at = lax.broadcasted_iota(jnp.int32, (64, 256), 1)
    at = at + (at // 64) * 64
    member = ((at >= starts[...]) & (at < ends[...])).astype(BF16)
    for i in range(2):
        part = got[:, 64 * i : 64 * i + 64].reshape(256, HEAD)
        sums[i] = dot(member, part, ((1,), (0,)))


def far_body(got, marks, out):
    k = got[:, 64:128].reshape(256, HEAD).astype(F32)
    v = got[:, 128:192].reshape(256, HEAD).astype(F32)
    far = dot(marks[0], k, ((1,), (1,)), HI) * SCALE
    peak = jnp.max(far, axis=-1, keepdims=True)
    far = jnp.exp(far - peak)
    mass = jnp.sum(far, axis=-1, keepdims=True)
    part = dot(far, v, ((1,), (0,)), HI)
    lane = lax.broadcasted_iota(jnp.int32, (64, HEAD), 1)
    stats = jnp.where(lane < 64, peak, mass)
    for i in range(2):
        out[:, i, :] = part[32 * i : 32 * i + 32]
        out[:, 2 + i, :] = stats[32 * i : 32 * i + 32]


def merge_body(parts, out):
    rows = []
    for i in range(2):
        stats = parts[:, 2 + i, :]
        low = lax.broadcasted_iota(jnp.int32, (32, HEAD), 1) < 64
        other = pltpu.roll(stats, 64, 1)
        peak = jnp.where(low, stats, other)
        mass = jnp.where(low, other, stats)
        factor = jnp.exp(peak - jnp.max(peak, axis=0, keepdims=True))
        total = jnp.sum(factor * mass, axis=0, keepdims=True)
        rows.append(jnp.sum(factor * parts[:, i, :], axis=0, keepdims=True) / total)
    for i in range(2):
        out[:, i, :] = jnp.broadcast_to(rows[i], (32, HEAD))


def spread(terms, out, y):
    for x in range(4):
        out[y * 4 + x] = terms[:, x * 512 : x * 512 + 512].astype(BF16)


def unmix(weights, tile, dest, lanes):
    for z in range(16):
        for c in range(2):
            for y in range(4):
                low = (z * 8 + y * 2 + c) * 16
                dest[low : low + 16, lanes] = weights[
                    z * 2 + c, y, tile * 16 : tile * 16 + 16, :
                ]


def proj_body(near, inverse, gathered, weights, out, wo):
    unmix(weights, 5, wo, slice(0, 128))
    gath = jnp.concatenate([gathered[:, 0, :], gathered[:, 1, :]], axis=0)
    mixer = dot(inverse[...], gath, ((1,), (0,)), HI)
    attn = dot(near[...], mixer, ((1,), (0,)), HI).astype(BF16)
    for y in range(4):
        spread(dot(attn[y * 64 : y * 64 + 64], wo[...], ((1,), (1,))), out, y)


def resid_body(parts, stream, out):
    total = parts[0].astype(F32)
    for i in range(1, 16):
        total = total + parts[i].astype(F32)
    resid = (stream[...].astype(F32) + total).astype(BF16)
    for i in range(16):
        out[i] = resid


def last_body(parts, resid, out):
    total = parts[0].astype(F32)
    for i in range(1, 16):
        total = total + parts[i].astype(F32)
    out[...] = (resid[0].astype(F32) + total).astype(BF16)


def ffn_body(whole, gain, weights, out, normed, w1, w2):
    for t in range(3):
        unmix(weights, t, w1, slice(t * 128, t * 128 + 128))
    for t in range(2):
        unmix(weights, 3 + t, w2, slice(t * 128, t * 128 + 128))
    for y in range(4):
        blocks = [whole[y * 4 + x].astype(F32) for x in range(4)]
        square = sum(jnp.sum(b * b, axis=-1, keepdims=True) for b in blocks)
        factor = lax.rsqrt(square * (1.0 / 2048.0) + EPS)
        for x in range(4):
            lanes = slice(x * 512, x * 512 + 512)
            normed[y * 64 : y * 64 + 64, lanes] = (
                blocks[x] * factor * gain[:, lanes]
            ).astype(BF16)
    first = dot(normed[...], w1[...], ((1,), (0,)))
    lane = lax.broadcasted_iota(jnp.int32, (256, 128), 1)
    gate, up, mixed = (first[:, t * 128 : t * 128 + 128] for t in range(3))
    hid0 = gate / (1.0 + jnp.exp(-gate)) * up
    hid1 = mixed / (1.0 + jnp.exp(-mixed)) * pltpu.roll(mixed, 64, 1)
    hid1 = jnp.where(lane < 64, hid1, 0.0)
    hidden = jnp.concatenate([hid0, hid1], axis=-1).astype(BF16)
    for y in range(4):
        spread(dot(hidden[y * 64 : y * 64 + 64], w2[...], ((1,), (1,))), out, y)


def inverse_rounds(land):
    eye = jnp.eye(land.shape[-1], dtype=F32)
    col_most = jnp.max(jnp.sum(land, axis=0))
    row_most = jnp.max(jnp.sum(land, axis=1))
    approx = land.T / (col_most * row_most)
    for _ in range(PINV_ITERS):
        prod = mm("ij,jk->ik", land, approx)
        inner = 7.0 * eye - prod
        inner = 15.0 * eye - mm("ij,jk->ik", prod, inner)
        inner = 13.0 * eye - mm("ij,jk->ik", prod, inner)
        approx = 0.25 * mm("ij,jk->ik", approx, inner)
    return approx


def on_device(queries, keys, values, stream, seg_lengths, gain, w_out, w_gate, w_up, w_down):
    z, c = lax.axis_index("z"), lax.axis_index("c")
    pack = kernel_call(pack_body, shape((4, 288, 128), BF16), 7)(
        queries, keys, values, w_gate, w_up, w_down.T, w_out.T
    )
    got = lax.all_to_all(pack, "y", 0, 0)
    ends = jnp.cumsum(seg_lengths) - (z * 512 + c * 64)
    sums, mine_w = kernel_call(
        marks_body, [shape((2, 64, HEAD), F32), shape((4, 96, 128), BF16)], 3
    )(got, (ends - seg_lengths)[:, None], ends[:, None])
    weights = lax.all_gather(mine_w, ("z", "c"), axis=0)

    mine = jnp.sum(lax.all_to_all(sums, "c", 0, 0), axis=0)
    mine = jnp.sum(lax.all_gather(mine, "z", axis=0), axis=0)
    marks = lax.all_gather(mine / seg_lengths.astype(F32)[:, None], "c", axis=0)
    qm, km = marks[0], marks[1]

    send = kernel_call(far_body, shape((32, 4, HEAD), F32), 2)(got, marks)
    parts = lax.all_to_all(send, ("z", "c"), 0, 0)
    gathered = kernel_call(merge_body, shape((32, 2, HEAD), F32), 1)(parts)
    gathered = lax.all_to_all(gathered, ("z", "c"), 0, 0)

    q32 = got[:, 0:64].reshape(256, HEAD).astype(F32)
    near = jax.nn.softmax(mm("td,jd->tj", q32, km) * SCALE, axis=-1)
    land = jax.nn.softmax(mm("id,jd->ij", qm, km) * SCALE, axis=-1)
    inverse = inverse_rounds(land)

    terms = kernel_call(
        proj_body, shape((16, 64, 512), BF16), 4, [pltpu.VMEM((2048, 128), BF16)]
    )(near, inverse, gathered, weights)
    resid = kernel_call(resid_body, shape((16, 64, 512), BF16), 2)(
        lax.all_to_all(terms, ("y", "x"), 0, 0), stream
    )
    whole = lax.all_to_all(resid, ("y", "x"), 0, 0)
    terms = kernel_call(
        ffn_body,
        shape((16, 64, 512), BF16),
        3,
        [
            pltpu.VMEM((256, 2048), BF16),
            pltpu.VMEM((2048, 384), BF16),
            pltpu.VMEM((2048, 256), BF16),
        ],
    )(whole, gain[None, :], weights)
    return kernel_call(last_body, shape((64, 512), BF16), 2)(
        lax.all_to_all(terms, ("y", "x"), 0, 0), resid[0:1]
    )


def solution(mesh):
    fine = Mesh(mesh.devices.reshape(16, 4, 2, 4), ("z", "y", "c", "x"))
    seq = ("z", "y", "c")
    return jax.shard_map(
        on_device,
        mesh=fine,
        in_specs=(
            P(seq, "x"),
            P(seq, "x"),
            P(seq, "x"),
            P(seq, "x"),
            P(),
            P(),
            P("x", seq),
            P(seq, "x"),
            P(seq, "x"),
            P("x", seq),
        ),
        out_specs=P(seq, "x"),
        check_vma=False,
    )
```

time: 228 us -> 200 us (0.88)
  waiting for transfers between devices: 62.1 us -> 32.4 us
  Pallas kernels: 0 us -> 21.6 us
  local copies, waits for them, and re-layouts: 25.8 us -> 6.28 us
  starting transfers between devices: 20.2 us -> 23.8 us
  blocking collectives: 90.4 us -> 87.4 us
    all_gather x1, waiting for transfers between devices: 22.2 us -> 0.01 us  [on_device(): weights = lax.all_gather(mine_w, ('z', 'c'), axis=0)]
    pallas_call x0 -> x8, Pallas kernels: none -> 21.6 us  [the longest x1 5.56 us: on_device(): kernel_call(ffn_body, shape((16, 64, 512), BF16), 3, [pltpu.VMEM((256, 20...]
    slice x17 -> x3, local copies, waits for them, and re-layouts: 11.6 us -> 1.47 us  [the longest x1 1.46 us: on_device(): resid[0:1]]
    all_to_all x1, waiting for transfers between devices: 11 us -> 5.53 us  [on_device(): parts = lax.all_to_all(send, ('z', 'c'), 0, 0)]
    reshape x14 -> x1, local copies, waits for them, and re-layouts: 5.64 us -> 0.74 us  [the longest x7 3.35 us: tiles(): return a[:, :512].reshape(a.shape[0], 4, 128).transpose(1, 0, 2)]
    all_to_all x2, blocking collectives: 44.7 us -> 40.1 us  [the longest x1 20.2 us: on_device(): lax.all_to_all(terms, ('y', 'x'), 0, 0)]
    convert_element_type x2 -> x0, local copies, waits for them, and re-layouts: 3.61 us -> none  [on_device(): normed = (whole * lax.rsqrt(meansq + EPS) * gain[None, :]).astype(BF16)]
    all_to_all x2, starting transfers between devices: 7.56 us -> 10.3 us  [the longest x1 6.65 us: on_device(): gathered = lax.all_to_all(gathered, ('z', 'c'), 0, 0)]
  transfers between devices with their start and end apart: 5 -> 5, of which waited for: 5 -> 4; matrix products, arithmetic and copies ran while one was open for 6% -> 7% of each run, Pallas kernels for 0% -> 2%
where the time goes in v2:
time: 200 us; the launch traced here: 197 us
  blocking collectives  87.4 us (44%)
  waiting for transfers between devices  32.4 us (16%)
  starting transfers between devices  23.8 us (12%)
  Pallas kernels  21.6 us (11%)
  between operations  14.9 us (7%)
  matrix products  6.3 us (3%)
  local copies, waits for them, and re-layouts  6.28 us (3%)
  other arithmetic  4.1 us (2%)
    all_gather x1, blocking collectives, on_device(): mine = jnp.sum(lax.all_gather(mine, 'z', axis=0), axis=0)  28.8 us
    all_to_all x1, blocking collectives, on_device(): lax.all_to_all(terms, ('y', 'x'), 0, 0)  20.2 us
    all_to_all x1, blocking collectives, on_device(): whole = lax.all_to_all(resid, ('y', 'x'), 0, 0)  19.9 us
    all_to_all x1, waiting for transfers between devices, on_device(): lax.all_to_all(terms, ('y', 'x'), 0, 0)  12.9 us
    all_to_all x1, waiting for transfers between devices, on_device(): gathered = lax.all_to_all(gathered, ('z', 'c'), 0, 0)  11.3 us
    all_to_all x1, blocking collectives, on_device(): mine = jnp.sum(lax.all_to_all(sums, 'c', 0, 0), axis=0)  10.8 us
    all_to_all x1, starting transfers between devices, on_device(): parts = lax.all_to_all(send, ('z', 'c'), 0, 0)  8.5 us
    all_gather x1, blocking collectives, on_device(): marks = lax.all_gather(mine / seg_lengths.astype(F32)[:, None], 'c', axis=0)  7.63 us
  transfers between devices with their start and end apart: 5, of which 4 were waited for; matrix products, arithmetic and copies ran while one was open for 7% of the time, Pallas kernels for 2%

profile of v2, /device:TPU:1, one launch (start us, length us, event | category | flops | bytes accessed | tf_op | source)
XLA Modules:
  0.0 196.8 jit_solution(4318652630298687067)
XLA Ops:
  6.5 1.7 shard_map.100
  8.3 5.0 %all-to-all-start = ((bf16[4,288,128]{2,1,0:T(8,128)(2,1)}), bf16[4,288,128]{2,1,0:T(8,128)(2,1)S(1)}, u32[]{:S(2)}, u32[]{:S(2)}) async-start(bf16[4,288,128]{2,1,0:T(8,128)(2,1)} %shard_map.100), calls=%async_computation | async-start | bytes 589824 | tf_op jit(solution)/shard_map/all_to_all | solution.py:193
  13.3 0.7 copy.20
  14.0 0.1 reduce-window.4
  14.1 0.7 fusion.45
  14.8 0.7 fusion.46
  15.6 0.7 copy.21.starts
  16.3 2.7 %all-to-all-done.got = bf16[4,288,128]{2,1,0:T(8,128)(2,1)S(1)} async-done(((bf16[4,288,128]{2,1,0:T(8,128)(2,1)}), bf16[4,288,128]{2,1,0:T(8,128)(2,1)S(1)}, u32[]{:S(2)}, u32[]{:S(2)}) %all-to-all-start) | async-done | bytes 294944 | tf_op jit(solution)/shard_map/all_to_all | solution.py:193
  19.0 0.7 copy-done.1
  19.7 1.8 shard_map.101
  21.6 10.8 %all_to_all.35 = f32[2,64,128]{2,1,0:T(8,128)S(1)} all-to-all(f32[2,64,128]{2,1,0:T(8,128)} %get-tuple-element.7), channel_id=1, replica_groups=mesh['z'=16,'y'=4,'c'=2,'x'=4] {'c'}, dimensions={0} | all-to-all | bytes 131072 | tf_op jit(solution)/shard_map/all_to_all | solution.py:200
  32.4 28.8 %all-gather = f32[1024,128]{1,0:T(8,128)S(1)} all-gather(f32[64,128]{1,0:T(8,128)S(1)} %reduce_sum.56), channel_id=2, replica_groups=mesh['z'=16,'y'=4,'c'=2,'x'=4] {'z'}, dimensions={0}, use_global_device_ids=true | all-gather | bytes 557056 | tf_op jit(solution)/shard_map/all_gather | solution.py:201
  61.2 0.1 bitcast_divide_fusion
  61.3 7.6 %all_gather.18.marks = f32[2,64,128]{2,1,0:T(8,128)S(1)} all-gather(f32[1,64,128]{2,1,0:T(8,128)S(1)} %bitcast_divide_fusion), channel_id=1, replica_groups=mesh['z'=16,'y'=4,'c'=2,'x'=4] {'c'}, dimensions={0}, use_global_device_ids=true | all-gather | bytes 98304 | tf_op jit(solution)/shard_map/all_gather | solution.py:202
  68.9 0.2 fusion.48
  69.1 0.4 copy-done.2
  69.5 2.2 %shard_map.102 = f32[32,4,128]{2,1,0:T(4,128)} custom-call(bf16[4,288,128]{2,1,0:T(8,128)(2,1)} %copy-done.1, f32[2,64,128]{2,1,0:T(8,128)} %copy-done.2), custom_call_target="tpu_custom_call" | custom-call | tf_op jit(solution)/shard_map/pallas_call | solution.py:205
  71.7 8.5 %all-to-all-start.2 = ((f32[32,4,128]{2,1,0:T(4,128)}), f32[32,4,128]{2,1,0:T(4,128)S(1)}, u32[]{:S(2)}, u32[]{:S(2)}) async-start(f32[32,4,128]{2,1,0:T(4,128)} %shard_map.102), calls=%async_computation.2 | async-start | bytes 131072 | tf_op jit(solution)/shard_map/all_to_all | solution.py:206
  80.3 0.1 fusion.43
  80.4 0.6 reduce_max.38
  81.0 0.7 reduce_max.39
  82.9 0.2 fusion.18
  83.2 0.2 convolution_subtract_fusion.11
  83.4 0.2 convolution_subtract_fusion.10
  83.5 0.2 convolution_multiply_fusion.6
  83.7 0.2 fusion.40
  84.0 0.2 convolution_subtract_fusion.9
  84.1 0.2 convolution_subtract_fusion.8
  84.3 0.2 convolution_multiply_fusion.5
  84.5 0.2 fusion.38
  84.7 0.2 convolution_subtract_fusion.7
  84.9 0.2 convolution_subtract_fusion.6
  85.1 0.2 convolution_multiply_fusion.4
  85.2 0.2 fusion.36
  85.5 0.2 convolution_subtract_fusion.5
  85.7 0.2 convolution_subtract_fusion.4
  85.8 0.2 convolution_multiply_fusion.3
  86.0 0.2 fusion.34
  86.3 0.2 convolution_subtract_fusion.3
  86.4 0.2 convolution_subtract_fusion.2
  86.6 0.2 convolution_multiply_fusion.2
  86.8 0.2 fusion.32
  87.0 0.2 convolution_subtract_fusion.1
  87.2 0.2 convolution_subtract_fusion
  87.4 1.1 fusion.47
  88.4 0.2 fusion.1
  88.6 0.8 fusion.near
  89.4 5.5 %all-to-all-done.2.parts = f32[32,4,128]{2,1,0:T(4,128)S(1)} async-done(((f32[32,4,128]{2,1,0:T(4,128)}), f32[32,4,128]{2,1,0:T(4,128)S(1)}, u32[]{:S(2)}, u32[]{:S(2)}) %all-to-all-start.2) | async-done | bytes 65568 | tf_op jit(solution)/shard_map/all_to_all | solution.py:206
  95.0 0.6 copy-done.3
  95.6 1.6 shard_map.103
  97.2 6.7 %all-to-all-start.3 = ((f32[32,2,128]{2,1,0:T(2,128)}), f32[32,2,128]{2,1,0:T(2,128)S(1)}, u32[]{:S(2)}, u32[]{:S(2)}) async-start(f32[32,2,128]{2,1,0:T(2,128)} %shard_map.103), calls=%async_computation.3 | async-start | bytes 65536 | tf_op jit(solution)/shard_map/all_to_all | solution.py:208
  103.8 0.8 convolution_multiply_fusion.1.inverse
  104.6 11.3 %all-to-all-done.3.gathered = f32[32,2,128]{2,1,0:T(2,128)S(1)} async-done(((f32[32,2,128]{2,1,0:T(2,128)}), f32[32,2,128]{2,1,0:T(2,128)S(1)}, u32[]{:S(2)}, u32[]{:S(2)}) %all-to-all-start.3) | async-done | bytes 32800 | tf_op jit(solution)/shard_map/all_to_all | solution.py:208
  116.0 0.6 copy-done.4
  116.6 4.4 %shard_map.104 = bf16[16,64,512]{2,1,0:T(8,128)(2,1)} custom-call(f32[256,64]{1,0:T(8,128)} %fusion.near, f32[64,64]{1,0:T(8,128)} %convolution_multiply_fusion.1.inverse, f32[32,2,128]{2,1,0:T(2,128)} %copy-done.4, bf16[32,4,96,128]{3,2,1,0:T(8,128)(2,1)} %bitcast.59), custom_call_target="tpu_custom_call" | custom-call | tf_op jit(solution)/shard_map/pallas_call | solution.py:215
  120.9 20.2 %all_to_all.36.parts = bf16[16,64,512]{2,1,0:T(8,128)(2,1)} all-to-all(bf16[16,64,512]{2,1,0:T(8,128)(2,1)} %shard_map.104), channel_id=1, replica_groups=mesh['z'=16,'y'=4,'c'=2,'x'=4] {'y','x'}, dimensions={0} | all-to-all | bytes 2097152 | tf_op jit(solution)/shard_map/all_to_all | solution.py:219
  141.1 2.4 %shard_map.105 = bf16[16,64,512]{2,1,0:T(8,128)(2,1)} custom-call(bf16[16,64,512]{2,1,0:T(8,128)(2,1)} %all_to_all.36.parts, bf16[64,512]{1,0:T(8,128)(2,1)} %stream.1), custom_call_target="tpu_custom_call" | custom-call | tf_op jit(solution)/shard_map/pallas_call | solution.py:218
  143.5 19.9 %all_to_all.37.whole = bf16[16,64,512]{2,1,0:T(8,128)(2,1)} all-to-all(bf16[16,64,512]{2,1,0:T(8,128)(2,1)} %shard_map.105), channel_id=1, replica_groups=mesh['z'=16,'y'=4,'c'=2,'x'=4] {'y','x'}, dimensions={0} | all-to-all | bytes 2097152 | tf_op jit(solution)/shard_map/all_to_all | solution.py:221
  163.4 5.6 %shard_map.106 = bf16[16,64,512]{2,1,0:T(8,128)(2,1)} custom-call(bf16[16,64,512]{2,1,0:T(8,128)(2,1)} %all_to_all.37.whole, f32[1,2048]{1,0:T(1,128)} %bitcast.65, bf16[32,4,96,128]{3,2,1,0:T(8,128)(2,1)} %bitcast.60), custom_call_target="tpu_custom_call" | custom-call | tf_op jit(solution)/shard_map/pallas_call | solution.py:222
  169.0 3.7 %all-to-all-start.6 = ((bf16[16,64,512]{2,1,0:T(8,128)(2,1)}), bf16[16,64,512]{2,1,0:T(8,128)(2,1)S(1)}, u32[]{:S(2)}, u32[]{:S(2)}) async-start(bf16[16,64,512]{2,1,0:T(8,128)(2,1)} %shard_map.106), calls=%async_computation.6 | async-start | bytes 2097152 | tf_op jit(solution)/shard_map/all_to_all | solution.py:233
  172.7 1.5 slice.19.resid
  174.1 12.9 %all-to-all-done.6.parts = bf16[16,64,512]{2,1,0:T(8,128)(2,1)S(1)} async-done(((bf16[16,64,512]{2,1,0:T(8,128)(2,1)}), bf16[16,64,512]{2,1,0:T(8,128)(2,1)S(1)}, u32[]{:S(2)}, u32[]{:S(2)}) %all-to-all-start.6) | async-done | bytes 1048608 | tf_op jit(solution)/shard_map/all_to_all | solution.py:233
  187.0 1.0 copy-done
  188.0 2.0 %shard_map.107 = bf16[64,512]{1,0:T(8,128)(2,1)} custom-call(bf16[16,64,512]{2,1,0:T(8,128)(2,1)} %copy-done, bf16[1,64,512]{2,1,0:T(8,128)(2,1)} %slice.19.resid), custom_call_target="tpu_custom_call" | custom-call | tf_op jit(solution)/shard_map/pallas_call | solution.py:232
  (14 shorter events, 0.1 us)
Async XLA Ops:
  8.3 10.7 %all-to-all-start = ((bf16[4,288,128]{2,1,0:T(8,128)(2,1)}), bf16[4,288,128]{2,1,0:T(8,128)(2,1)S(1)}, u32[]{:S(2)}, u32[]{:S(2)}) async-start(bf16[4,288,128]{2,1,0:T(8,128)(2,1)} %shard_map.100), calls=%async_computation | async-start | bytes 589824 | tf_op jit(solution)/shard_map/all_to_all | solution.py:193
  13.3 102.7 %all-gather.4.cloned.1.call-start = ((), (), s32[]{:S(2)}) async-start(), calls=%async_computation.7 | async-start | bytes 3244032 | tf_op jit(solution)/shard_map/all_gather | solution.py:198
  19.0 0.7 copy-start.1
  21.5 65.8 %slice-start = ((bf16[4,288,128]{2,1,0:T(8,128)(2,1)}), bf16[4,64,128]{2,1,0:T(8,128)(2,1)S(1)}, s32[]{:S(2)}) async-start(bf16[4,288,128]{2,1,0:T(8,128)(2,1)} %copy-done.1), calls=%async_computation.8 | async-start | bytes 131072 | tf_op jit(solution)/shard_map/slice | solution.py:210
  68.9 0.6 copy-start.2
  71.7 23.2 %all-to-all-start.2 = ((f32[32,4,128]{2,1,0:T(4,128)}), f32[32,4,128]{2,1,0:T(4,128)S(1)}, u32[]{:S(2)}, u32[]{:S(2)}) async-start(f32[32,4,128]{2,1,0:T(4,128)} %shard_map.102), calls=%async_computation.2 | async-start | bytes 131072 | tf_op jit(solution)/shard_map/all_to_all | solution.py:206
  95.0 0.6 copy-start.3
  97.2 18.8 %all-to-all-start.3 = ((f32[32,2,128]{2,1,0:T(2,128)}), f32[32,2,128]{2,1,0:T(2,128)S(1)}, u32[]{:S(2)}, u32[]{:S(2)}) async-start(f32[32,2,128]{2,1,0:T(2,128)} %shard_map.103), calls=%async_computation.3 | async-start | bytes 65536 | tf_op jit(solution)/shard_map/all_to_all | solution.py:208
  116.0 0.6 copy-start.4
  169.0 18.0 %all-to-all-start.6 = ((bf16[16,64,512]{2,1,0:T(8,128)(2,1)}), bf16[16,64,512]{2,1,0:T(8,128)(2,1)S(1)}, u32[]{:S(2)}, u32[]{:S(2)}) async-start(bf16[16,64,512]{2,1,0:T(8,128)(2,1)} %shard_map.106), calls=%async_computation.6 | async-start | bytes 2097152 | tf_op jit(solution)/shard_map/all_to_all | solution.py:233
  187.0 1.0 copy-start
Sparse Core Ops, SparseCore 0:
  21.7 78.7 all-gather.3

commit v3 on v2

--- a/solution.py
+++ b/solution.py
@@ -72,14 +72,25 @@
     at = at + (at // 64) * 64
     member = ((at >= starts[...]) & (at < ends[...])).astype(BF16)
     for i in range(2):
-        part = got[:, 64 * i : 64 * i + 64].reshape(256, HEAD)
-        sums[i] = dot(member, part, ((1,), (0,)))
+        part = dot(member, got[:, 64 * i : 64 * i + 64].reshape(256, HEAD), ((1,), (0,)))
+        sums[:, 2 * i, :] = part[0:32]
+        sums[:, 2 * i + 1, :] = part[32:64]
+
+
+def total_body(parts, counts, out):
+    for i in range(4):
+        row = jnp.sum(parts[:, i, :], axis=0, keepdims=True) / counts[i % 2]
+        out[:, i, :] = jnp.broadcast_to(row, (32, HEAD))
+
+
+def both(ref, i):
+    return jnp.concatenate([ref[:, i, :], ref[:, i + 1, :]], axis=0)
 
 
 def far_body(got, marks, out):
     k = got[:, 64:128].reshape(256, HEAD).astype(F32)
     v = got[:, 128:192].reshape(256, HEAD).astype(F32)
-    far = dot(marks[0], k, ((1,), (1,)), HI) * SCALE
+    far = dot(both(marks, 0), k, ((1,), (1,)), HI) * SCALE
     peak = jnp.max(far, axis=-1, keepdims=True)
     far = jnp.exp(far - peak)
     mass = jnp.sum(far, axis=-1, keepdims=True)
@@ -121,10 +132,16 @@
                 ]
 
 
-def proj_body(near, inverse, gathered, weights, out, wo):
+def unmix_body(weights, w1, w2, wo):
+    for t in range(3):
+        unmix(weights, t, w1, slice(t * 128, t * 128 + 128))
+    for t in range(2):
+        unmix(weights, 3 + t, w2, slice(t * 128, t * 128 + 128))
     unmix(weights, 5, wo, slice(0, 128))
-    gath = jnp.concatenate([gathered[:, 0, :], gathered[:, 1, :]], axis=0)
-    mixer = dot(inverse[...], gath, ((1,), (0,)), HI)
+
+
+def proj_body(near, inverse, gathered, wo, out):
+    mixer = dot(inverse[...], both(gathered, 0), ((1,), (0,)), HI)
     attn = dot(near[...], mixer, ((1,), (0,)), HI).astype(BF16)
     for y in range(4):
         spread(dot(attn[y * 64 : y * 64 + 64], wo[...], ((1,), (1,))), out, y)
@@ -146,11 +163,7 @@
     out[...] = (resid[0].astype(F32) + total).astype(BF16)
 
 
-def ffn_body(whole, gain, weights, out, normed, w1, w2):
-    for t in range(3):
-        unmix(weights, t, w1, slice(t * 128, t * 128 + 128))
-    for t in range(2):
-        unmix(weights, 3 + t, w2, slice(t * 128, t * 128 + 128))
+def ffn_body(whole, gain, w1, w2, out, normed):
     for y in range(4):
         blocks = [whole[y * 4 + x].astype(F32) for x in range(4)]
         square = sum(jnp.sum(b * b, axis=-1, keepdims=True) for b in blocks)
@@ -193,14 +206,22 @@
     got = lax.all_to_all(pack, "y", 0, 0)
     ends = jnp.cumsum(seg_lengths) - (z * 512 + c * 64)
     sums, mine_w = kernel_call(
-        marks_body, [shape((2, 64, HEAD), F32), shape((4, 96, 128), BF16)], 3
+        marks_body, [shape((32, 4, HEAD), F32), shape((4, 96, 128), BF16)], 3
     )(got, (ends - seg_lengths)[:, None], ends[:, None])
     weights = lax.all_gather(mine_w, ("z", "c"), axis=0)
-
-    mine = jnp.sum(lax.all_to_all(sums, "c", 0, 0), axis=0)
-    mine = jnp.sum(lax.all_gather(mine, "z", axis=0), axis=0)
-    marks = lax.all_gather(mine / seg_lengths.astype(F32)[:, None], "c", axis=0)
-    qm, km = marks[0], marks[1]
+    w1, w2, wo = kernel_call(
+        unmix_body,
+        [shape((2048, 384), BF16), shape((2048, 256), BF16), shape((2048, 128), BF16)],
+        1,
+    )(weights)
+
+    counts = lax.dynamic_index_in_dim(seg_lengths.reshape(2, 32), z * 2 + c, 1, keepdims=False)
+    counts = jnp.broadcast_to(counts.astype(F32)[:, None, None], (2, 1, HEAD))
+    marks = lax.all_to_all(sums, ("z", "c"), 0, 0)
+    marks = kernel_call(total_body, shape((32, 4, HEAD), F32), 2)(marks, counts)
+    marks = lax.all_to_all(marks, ("z", "c"), 0, 0)
+    qm = jnp.concatenate([marks[:, 0], marks[:, 1]], axis=0)
+    km = jnp.concatenate([marks[:, 2], marks[:, 3]], axis=0)
 
     send = kernel_call(far_body, shape((32, 4, HEAD), F32), 2)(got, marks)
     parts = lax.all_to_all(send, ("z", "c"), 0, 0)
@@ -212,23 +233,14 @@
     land = jax.nn.softmax(mm("id,jd->ij", qm, km) * SCALE, axis=-1)
     inverse = inverse_rounds(land)
 
-    terms = kernel_call(
-        proj_body, shape((16, 64, 512), BF16), 4, [pltpu.VMEM((2048, 128), BF16)]
-    )(near, inverse, gathered, weights)
+    terms = kernel_call(proj_body, shape((16, 64, 512), BF16), 4)(near, inverse, gathered, wo)
     resid = kernel_call(resid_body, shape((16, 64, 512), BF16), 2)(
         lax.all_to_all(terms, ("y", "x"), 0, 0), stream
     )
     whole = lax.all_to_all(resid, ("y", "x"), 0, 0)
     terms = kernel_call(
-        ffn_body,
-        shape((16, 64, 512), BF16),
-        3,
-        [
-            pltpu.VMEM((256, 2048), BF16),
-            pltpu.VMEM((2048, 384), BF16),
-            pltpu.VMEM((2048, 256), BF16),
-        ],
-    )(whole, gain[None, :], weights)
+        ffn_body, shape((16, 64, 512), BF16), 4, [pltpu.VMEM((256, 2048), BF16)]
+    )(whole, gain[None, :], w1, w2)
     return kernel_call(last_body, shape((64, 512), BF16), 2)(
         lax.all_to_all(terms, ("y", "x"), 0, 0), resid[0:1]
     )

time: 200 us -> 227 us (1.14)
  waiting for transfers between devices: 32.4 us -> 82.2 us
  blocking collectives: 87.4 us -> 42.9 us
  starting transfers between devices: 23.8 us -> 41.6 us
  Pallas kernels: 21.6 us -> 26.2 us
    all_gather x2 -> x0, blocking collectives: 36.4 us -> none  [the longest x1 28.8 us: on_device(): mine = jnp.sum(lax.all_gather(mine, 'z', axis=0), axis=0)]
    all_gather x1, waiting for transfers between devices: 0.01 us -> 32.9 us  [on_device(): weights = lax.all_gather(mine_w, ('z', 'c'), axis=0)]
    all_to_all x0 -> x2, waiting for transfers between devices: none -> 24.5 us  [the longest x1 12.3 us: on_device(): marks = lax.all_to_all(marks, ('z', 'c'), 0, 0)]
    all_to_all x0 -> x2, starting transfers between devices: none -> 22.7 us  [the longest x1 17.6 us: on_device(): marks = lax.all_to_all(sums, ('z', 'c'), 0, 0)]
    all_to_all x1, waiting for transfers between devices: 11.3 us -> 0.01 us  [on_device(): gathered = lax.all_to_all(gathered, ('z', 'c'), 0, 0)]
    all_to_all x1 -> x0, blocking collectives: 10.8 us -> none  [on_device(): mine = jnp.sum(lax.all_to_all(sums, 'c', 0, 0), axis=0)]
    pallas_call x3 -> x5, Pallas kernels: 11.7 us -> 16.3 us  [the longest x1 5.34 us: on_device(): kernel_call(ffn_body, shape((16, 64, 512), BF16), 4, [pltpu.VMEM((256, 20...]
    all_to_all x1, starting transfers between devices: 8.5 us -> 5.13 us  [on_device(): parts = lax.all_to_all(send, ('z', 'c'), 0, 0)]
  transfers between devices with their start and end apart: 5 -> 7, of which waited for: 4 -> 6; matrix products, arithmetic and copies ran while one was open for 7% -> 6% of each run, Pallas kernels for 2% -> 3%
where the time goes in v3:
time: 227 us; the launch traced here: 224 us
  waiting for transfers between devices  82.2 us (36%)
  blocking collectives  42.9 us (19%)
  starting transfers between devices  41.6 us (18%)
  Pallas kernels  26.2 us (12%)
  between operations  14.8 us (7%)
  local copies, waits for them, and re-layouts  7.3 us (3%)
  matrix products  5.54 us (2%)
  other arithmetic  3.98 us (2%)
    all_gather x1, waiting for transfers between devices, on_device(): weights = lax.all_gather(mine_w, ('z', 'c'), axis=0)  32.9 us
    all_to_all x1, blocking collectives, on_device(): lax.all_to_all(terms, ('y', 'x'), 0, 0)  22.8 us
    all_to_all x1, blocking collectives, on_device(): whole = lax.all_to_all(resid, ('y', 'x'), 0, 0)  20.1 us
    all_to_all x1, starting transfers between devices, on_device(): marks = lax.all_to_all(sums, ('z', 'c'), 0, 0)  17.6 us
    all_to_all x1, waiting for transfers between devices, on_device(): lax.all_to_all(terms, ('y', 'x'), 0, 0)  13.5 us
    all_to_all x1, waiting for transfers between devices, on_device(): marks = lax.all_to_all(marks, ('z', 'c'), 0, 0)  12.3 us
    all_to_all x1, waiting for transfers between devices, on_device(): marks = lax.all_to_all(sums, ('z', 'c'), 0, 0)  12.1 us
    all_to_all x1, waiting for transfers between devices, on_device(): parts = lax.all_to_all(send, ('z', 'c'), 0, 0)  7.83 us
  transfers between devices with their start and end apart: 7, of which 6 were waited for; matrix products, arithmetic and copies ran while one was open for 6% of the time, Pallas kernels for 3%

profile of v3, /device:TPU:1, one launch (start us, length us, event | category | flops | bytes accessed | tf_op | source)
XLA Modules:
  0.0 224.5 jit_solution(4759416498368394327)
XLA Ops:
  6.5 1.7 shard_map.100
  8.3 5.0 %all-to-all-start = ((bf16[4,288,128]{2,1,0:T(8,128)(2,1)}), bf16[4,288,128]{2,1,0:T(8,128)(2,1)S(1)}, u32[]{:S(2)}, u32[]{:S(2)}) async-start(bf16[4,288,128]{2,1,0:T(8,128)(2,1)} %shard_map.100), calls=%async_computation | async-start | bytes 589824 | tf_op jit(solution)/shard_map/all_to_all | solution.py:206
  13.3 0.7 copy.21
  14.1 0.7 fusion.50
  14.8 0.7 subtract_bitcast_fusion
  15.5 0.7 copy.22.starts
  16.2 2.8 %all-to-all-done.got = bf16[4,288,128]{2,1,0:T(8,128)(2,1)S(1)} async-done(((bf16[4,288,128]{2,1,0:T(8,128)(2,1)}), bf16[4,288,128]{2,1,0:T(8,128)(2,1)S(1)}, u32[]{:S(2)}, u32[]{:S(2)}) %all-to-all-start) | async-done | bytes 294944 | tf_op jit(solution)/shard_map/all_to_all | solution.py:206
  19.0 0.7 copy-done.1
  19.7 1.8 shard_map.101
  21.6 17.6 %all-to-all-start.1 = ((f32[32,4,128]{2,1,0:T(4,128)}), f32[32,4,128]{2,1,0:T(4,128)S(1)}, u32[]{:S(2)}, u32[]{:S(2)}) async-start(f32[32,4,128]{2,1,0:T(4,128)} %get-tuple-element.10), calls=%async_computation.1 | async-start | bytes 131072 | tf_op jit(solution)/shard_map/all_to_all | solution.py:220
  39.2 0.7 reshape.32
  39.9 0.2 convert_reduce_fusion
  40.1 12.1 %all-to-all-done.1.parts = f32[32,4,128]{2,1,0:T(4,128)S(1)} async-done(((f32[32,4,128]{2,1,0:T(4,128)}), f32[32,4,128]{2,1,0:T(4,128)S(1)}, u32[]{:S(2)}, u32[]{:S(2)}) %all-to-all-start.1) | async-done | bytes 65568 | tf_op jit(solution)/shard_map/all_to_all | solution.py:220
  52.3 0.7 broadcast_in_dim.7.counts
  52.9 1.5 shard_map.102
  54.5 5.1 %all-to-all-start.2 = ((f32[32,4,128]{2,1,0:T(4,128)}), f32[32,4,128]{2,1,0:T(4,128)S(1)}, u32[]{:S(2)}, u32[]{:S(2)}) async-start(f32[32,4,128]{2,1,0:T(4,128)} %shard_map.102), calls=%async_computation.2 | async-start | bytes 131072 | tf_op jit(solution)/shard_map/all_to_all | solution.py:222
  59.6 0.7 all-gather.3.cloned.1.call-update
  60.3 12.3 %all-to-all-done.2.marks = f32[32,4,128]{2,1,0:T(4,128)S(1)} async-done(((f32[32,4,128]{2,1,0:T(4,128)}), f32[32,4,128]{2,1,0:T(4,128)S(1)}, u32[]{:S(2)}, u32[]{:S(2)}) %all-to-all-start.2) | async-done | bytes 65568 | tf_op jit(solution)/shard_map/all_to_all | solution.py:222
  72.7 0.2 fusion.53
  73.1 0.6 reduce_max.38
  73.7 0.6 reduce_max.39
  75.4 2.2 shard_map.103
  77.6 5.1 %all-to-all-start.3 = ((f32[32,4,128]{2,1,0:T(4,128)}), f32[32,4,128]{2,1,0:T(4,128)S(1)}, u32[]{:S(2)}, u32[]{:S(2)}) async-start(f32[32,4,128]{2,1,0:T(4,128)} %shard_map.103), calls=%async_computation.3 | async-start | bytes 131072 | tf_op jit(solution)/shard_map/all_to_all | solution.py:227
  82.7 0.2 fusion.21
  83.0 0.2 convolution_subtract_fusion.11
  83.2 0.2 convolution_subtract_fusion.10
  83.3 0.2 convolution_multiply_fusion.6
  83.5 0.2 fusion.45
  83.8 0.2 convolution_subtract_fusion.9
  83.9 0.2 convolution_subtract_fusion.8
  84.1 0.2 convolution_multiply_fusion.5
  84.3 0.2 fusion.43
  84.5 0.2 convolution_subtract_fusion.7
  84.7 0.2 convolution_subtract_fusion.6
  84.9 0.2 convolution_multiply_fusion.4
  85.0 0.2 fusion.41
  85.3 0.2 convolution_subtract_fusion.5
  85.8 0.2 fusion.39
  86.1 0.2 convolution_subtract_fusion.3
  86.2 0.2 convolution_subtract_fusion.2
  86.4 0.2 convolution_multiply_fusion.2
  86.6 0.2 fusion.37
  86.8 0.2 convolution_subtract_fusion.1
  87.2 0.3 fusion.52
  87.5 0.2 fusion.1
  87.7 0.8 fusion.near
  88.5 7.8 %all-to-all-done.3.parts = f32[32,4,128]{2,1,0:T(4,128)S(1)} async-done(((f32[32,4,128]{2,1,0:T(4,128)}), f32[32,4,128]{2,1,0:T(4,128)S(1)}, u32[]{:S(2)}, u32[]{:S(2)}) %all-to-all-start.3) | async-done | bytes 65568 | tf_op jit(solution)/shard_map/all_to_all | solution.py:227
  96.3 0.6 copy-done.3
  96.9 1.6 shard_map.104
  98.5 5.0 %all-to-all-start.4 = ((f32[32,2,128]{2,1,0:T(2,128)}), f32[32,2,128]{2,1,0:T(2,128)S(1)}, u32[]{:S(2)}, u32[]{:S(2)}) async-start(f32[32,2,128]{2,1,0:T(2,128)} %shard_map.104), calls=%async_computation.4 | async-start | bytes 65536 | tf_op jit(solution)/shard_map/all_to_all | solution.py:229
  103.5 0.8 convolution_multiply_fusion.1.inverse
  104.3 32.9 %all-gather.3.cloned.1.call-done = bf16[128,96,128]{2,1,0:T(8,128)(2,1)} async-done(((bf16[4,96,128]{2,1,0:T(8,128)(2,1)}), bf16[128,96,128]{2,1,0:T(8,128)(2,1)}) %all-gather.3.cloned.1.call-update) | async-done | bytes 3145744 | tf_op jit(solution)/shard_map/all_gather | solution.py:211
  137.2 4.0 %shard_map.105 = (bf16[2048,384]{1,0:T(8,128)(2,1)}, bf16[2048,256]{1,0:T(8,128)(2,1)}, bf16[2048,128]{1,0:T(8,128)(2,1)}) custom-call(bf16[32,4,96,128]{3,2,1,0:T(8,128)(2,1)} %bitcast.51), custom_call_target="tpu_custom_call" | custom-call | tf_op jit(solution)/shard_map/pallas_call | solution.py:212
  141.3 0.6 copy-done.5
  141.9 3.5 %shard_map.106 = bf16[16,64,512]{2,1,0:T(8,128)(2,1)} custom-call(f32[256,64]{1,0:T(8,128)} %fusion.near, f32[64,64]{1,0:T(8,128)} %convolution_multiply_fusion.1.inverse, f32[32,2,128]{2,1,0:T(2,128)} %copy-done.5, bf16[2048,128]{1,0:T(8,128)(2,1)} %get-tuple-element.12.wo), custom_call_target="tpu_custom_call" | custom-call | tf_op jit(solution)/shard_map/pallas_call | solution.py:236
  145.4 22.8 %all_to_all.40.parts = bf16[16,64,512]{2,1,0:T(8,128)(2,1)} all-to-all(bf16[16,64,512]{2,1,0:T(8,128)(2,1)} %shard_map.106), channel_id=1, replica_groups=mesh['z'=16,'y'=4,'c'=2,'x'=4] {'y','x'}, dimensions={0} | all-to-all | bytes 2097152 | tf_op jit(solution)/shard_map/all_to_all | solution.py:238
  168.2 2.4 %shard_map.107 = bf16[16,64,512]{2,1,0:T(8,128)(2,1)} custom-call(bf16[16,64,512]{2,1,0:T(8,128)(2,1)} %all_to_all.40.parts, bf16[64,512]{1,0:T(8,128)(2,1)} %stream.1), custom_call_target="tpu_custom_call" | custom-call | tf_op jit(solution)/shard_map/pallas_call | solution.py:237
  170.6 20.1 %all_to_all.41.whole = bf16[16,64,512]{2,1,0:T(8,128)(2,1)} all-to-all(bf16[16,64,512]{2,1,0:T(8,128)(2,1)} %shard_map.107), channel_id=1, replica_groups=mesh['z'=16,'y'=4,'c'=2,'x'=4] {'y','x'}, dimensions={0} | all-to-all | bytes 2097152 | tf_op jit(solution)/shard_map/all_to_all | solution.py:240
  190.7 5.3 %shard_map.108 = bf16[16,64,512]{2,1,0:T(8,128)(2,1)} custom-call(bf16[16,64,512]{2,1,0:T(8,128)(2,1)} %all_to_all.41.whole, f32[1,2048]{1,0:T(1,128)} %bitcast.61, bf16[2048,384]{1,0:T(8,128)(2,1)} %get-tuple-element.13.w1, bf16[2048,256]{1,0:T(8,128)(2,1)} %get-tuple-element.14.w2), custom_call_target="tpu_custom_call" | custom-call | tf_op jit(solution)/shard_map/pallas_call | solution.py:241
  196.0 3.7 %all-to-all-start.7 = ((bf16[16,64,512]{2,1,0:T(8,128)(2,1)}), bf16[16,64,512]{2,1,0:T(8,128)(2,1)S(1)}, u32[]{:S(2)}, u32[]{:S(2)}) async-start(bf16[16,64,512]{2,1,0:T(8,128)(2,1)} %shard_map.108), calls=%async_computation.7 | async-start | bytes 2097152 | tf_op jit(solution)/shard_map/all_to_all | solution.py:245
  199.7 1.5 slice.29.resid
  201.1 13.5 %all-to-all-done.7.parts = bf16[16,64,512]{2,1,0:T(8,128)(2,1)S(1)} async-done(((bf16[16,64,512]{2,1,0:T(8,128)(2,1)}), bf16[16,64,512]{2,1,0:T(8,128)(2,1)S(1)}, u32[]{:S(2)}, u32[]{:S(2)}) %all-to-all-start.7) | async-done | bytes 1048608 | tf_op jit(solution)/shard_map/all_to_all | solution.py:245
  214.6 1.0 copy-done
  215.6 2.0 shard_map.109
  (20 shorter events, 0.9 us)
Async XLA Ops:
  8.3 10.7 %all-to-all-start = ((bf16[4,288,128]{2,1,0:T(8,128)(2,1)}), bf16[4,288,128]{2,1,0:T(8,128)(2,1)S(1)}, u32[]{:S(2)}, u32[]{:S(2)}) async-start(bf16[4,288,128]{2,1,0:T(8,128)(2,1)} %shard_map.100), calls=%async_computation | async-start | bytes 589824 | tf_op jit(solution)/shard_map/all_to_all | solution.py:206
  19.0 0.7 copy-start.1
  21.6 65.6 %slice-start = ((bf16[4,288,128]{2,1,0:T(8,128)(2,1)}), bf16[4,64,128]{2,1,0:T(8,128)(2,1)S(1)}, s32[]{:S(2)}) async-start(bf16[4,288,128]{2,1,0:T(8,128)(2,1)} %copy-done.1), calls=%async_computation.9 | async-start | bytes 131072 | tf_op jit(solution)/shard_map/slice | solution.py:231
  21.6 30.7 %all-to-all-start.1 = ((f32[32,4,128]{2,1,0:T(4,128)}), f32[32,4,128]{2,1,0:T(4,128)S(1)}, u32[]{:S(2)}, u32[]{:S(2)}) async-start(f32[32,4,128]{2,1,0:T(4,128)} %get-tuple-element.10), calls=%async_computation.1 | async-start | bytes 131072 | tf_op jit(solution)/shard_map/all_to_all | solution.py:220
  52.3 0.7 copy-start.4
  54.5 18.2 %all-to-all-start.2 = ((f32[32,4,128]{2,1,0:T(4,128)}), f32[32,4,128]{2,1,0:T(4,128)S(1)}, u32[]{:S(2)}, u32[]{:S(2)}) async-start(f32[32,4,128]{2,1,0:T(4,128)} %shard_map.102), calls=%async_computation.2 | async-start | bytes 131072 | tf_op jit(solution)/shard_map/all_to_all | solution.py:222
  59.6 77.7 %all-gather.3.cloned.1.call-start = ((), (), s32[]{:S(2)}) async-start(), calls=%async_computation.8 | async-start | bytes 3244032 | tf_op jit(solution)/shard_map/all_gather | solution.py:211
  72.6 2.7 %copy-start.2 = (f32[32,4,128]{2,1,0:T(4,128)}, f32[32,4,128]{2,1,0:T(4,128)S(1)}, u32[]{:S(2)}) copy-start(f32[32,4,128]{2,1,0:T(4,128)S(1)} %all-to-all-done.2.marks) | copy-start | bytes 196612
  77.6 18.7 %all-to-all-start.3 = ((f32[32,4,128]{2,1,0:T(4,128)}), f32[32,4,128]{2,1,0:T(4,128)S(1)}, u32[]{:S(2)}, u32[]{:S(2)}) async-start(f32[32,4,128]{2,1,0:T(4,128)} %shard_map.103), calls=%async_computation.3 | async-start | bytes 131072 | tf_op jit(solution)/shard_map/all_to_all | solution.py:227
  96.3 0.6 copy-start.3
  98.5 42.8 %all-to-all-start.4 = ((f32[32,2,128]{2,1,0:T(2,128)}), f32[32,2,128]{2,1,0:T(2,128)S(1)}, u32[]{:S(2)}, u32[]{:S(2)}) async-start(f32[32,2,128]{2,1,0:T(2,128)} %shard_map.104), calls=%async_computation.4 | async-start | bytes 65536 | tf_op jit(solution)/shard_map/all_to_all | solution.py:229
  141.3 0.6 copy-start.5
  196.0 18.6 %all-to-all-start.7 = ((bf16[16,64,512]{2,1,0:T(8,128)(2,1)}), bf16[16,64,512]{2,1,0:T(8,128)(2,1)S(1)}, u32[]{:S(2)}, u32[]{:S(2)}) async-start(bf16[16,64,512]{2,1,0:T(8,128)(2,1)} %shard_map.108), calls=%async_computation.7 | async-start | bytes 2097152 | tf_op jit(solution)/shard_map/all_to_all | solution.py:245
  214.6 1.0 copy-start
Sparse Core Ops, SparseCore 0:
  62.5 74.6 all-gather.2

commit v4 on v2

--- a/solution.py
+++ b/solution.py
@@ -50,24 +50,16 @@
         out[y, 0:64] = q[:, tile]
         out[y, 64:128] = k[:, tile]
         out[y, 128:192] = v[:, tile]
-        out[y, 192:208] = wg[:, tile]
-        out[y, 208:224] = wu[:, tile]
-        last = slice(512 + (y // 2) * 128, 640 + (y // 2) * 128)
-        lane = lax.broadcasted_iota(jnp.int32, (16, 128), 1)
-        g, u, d = (w[:, last].astype(F32) for w in (wg, wu, wd))
-        if y % 2 == 0:
-            mixed = jnp.where(lane < 64, g, pltpu.roll(u, 64, 1))
-        else:
-            mixed = jnp.where(lane < 64, pltpu.roll(g, 64, 1), u)
-            d = pltpu.roll(d, 64, 1)
-        out[y, 224:240] = mixed.astype(BF16)
-        out[y, 240:256] = wd[:, tile]
-        out[y, 256:272] = jnp.where(lane < 64, d, 0.0).astype(BF16)
-        out[y, 272:288] = wo[:, tile]
+        out[y, 192:208] = wo[:, tile]
+        for t in range(3):
+            low = ((y % 2) * 3 + t) * 128
+            for i, w in enumerate((wg, wu, wd)):
+                at = 208 + (3 * i + t) * 16
+                out[y, at : at + 16] = w[:, low : low + 128]
 
 
 def marks_body(got, starts, ends, sums, weights):
-    weights[...] = got[:, 192:288]
+    weights[...] = got[:, 192:352]
     at = lax.broadcasted_iota(jnp.int32, (64, 256), 1)
     at = at + (at // 64) * 64
     member = ((at >= starts[...]) & (at < ends[...])).astype(BF16)
@@ -106,9 +98,10 @@
         out[:, i, :] = jnp.broadcast_to(rows[i], (32, HEAD))
 
 
-def spread(terms, out, y):
-    for x in range(4):
-        out[y * 4 + x] = terms[:, x * 512 : x * 512 + 512].astype(BF16)
+def spread(terms, out):
+    for y in range(terms.shape[0] // 64):
+        for x in range(4):
+            out[y * 4 + x] = terms[y * 64 : y * 64 + 64, x * 512 : x * 512 + 512].astype(BF16)
 
 
 def unmix(weights, tile, dest, lanes):
@@ -121,37 +114,26 @@
                 ]
 
 
+def unmix_body(weights, w1, w2):
+    for t in range(6):
+        unmix(weights, 1 + t, w1, slice(t * 128, t * 128 + 128))
+    for t in range(3):
+        unmix(weights, 7 + t, w2, slice(t * 128, t * 128 + 128))
+
+
+def both(ref, i):
+    return jnp.concatenate([ref[:, i, :], ref[:, i + 1, :]], axis=0)
+
+
 def proj_body(near, inverse, gathered, weights, out, wo):
-    unmix(weights, 5, wo, slice(0, 128))
-    gath = jnp.concatenate([gathered[:, 0, :], gathered[:, 1, :]], axis=0)
-    mixer = dot(inverse[...], gath, ((1,), (0,)), HI)
+    unmix(weights, 0, wo, slice(0, 128))
+    mixer = dot(inverse[...], both(gathered, 0), ((1,), (0,)), HI)
     attn = dot(near[...], mixer, ((1,), (0,)), HI).astype(BF16)
-    for y in range(4):
-        spread(dot(attn[y * 64 : y * 64 + 64], wo[...], ((1,), (1,))), out, y)
-
-
-def resid_body(parts, stream, out):
-    total = parts[0].astype(F32)
-    for i in range(1, 16):
-        total = total + parts[i].astype(F32)
-    resid = (stream[...].astype(F32) + total).astype(BF16)
-    for i in range(16):
-        out[i] = resid
-
-
-def last_body(parts, resid, out):
-    total = parts[0].astype(F32)
-    for i in range(1, 16):
-        total = total + parts[i].astype(F32)
-    out[...] = (resid[0].astype(F32) + total).astype(BF16)
-
-
-def ffn_body(whole, gain, weights, out, normed, w1, w2):
-    for t in range(3):
-        unmix(weights, t, w1, slice(t * 128, t * 128 + 128))
-    for t in range(2):
-        unmix(weights, 3 + t, w2, slice(t * 128, t * 128 + 128))
-    for y in range(4):
+    spread(dot(attn, wo[...], ((1,), (1,))), out)
+
+
+def ffn_body(whole, gain, w1, w2, out, normed):
+    for y in range(2):
         blocks = [whole[y * 4 + x].astype(F32) for x in range(4)]
         square = sum(jnp.sum(b * b, axis=-1, keepdims=True) for b in blocks)
         factor = lax.rsqrt(square * (1.0 / 2048.0) + EPS)
@@ -161,14 +143,9 @@
                 blocks[x] * factor * gain[:, lanes]
             ).astype(BF16)
     first = dot(normed[...], w1[...], ((1,), (0,)))
-    lane = lax.broadcasted_iota(jnp.int32, (256, 128), 1)
-    gate, up, mixed = (first[:, t * 128 : t * 128 + 128] for t in range(3))
-    hid0 = gate / (1.0 + jnp.exp(-gate)) * up
-    hid1 = mixed / (1.0 + jnp.exp(-mixed)) * pltpu.roll(mixed, 64, 1)
-    hid1 = jnp.where(lane < 64, hid1, 0.0)
-    hidden = jnp.concatenate([hid0, hid1], axis=-1).astype(BF16)
-    for y in range(4):
-        spread(dot(hidden[y * 64 : y * 64 + 64], w2[...], ((1,), (1,))), out, y)
+    gate, up = first[:, :384], first[:, 384:]
+    hidden = (gate / (1.0 + jnp.exp(-gate)) * up).astype(BF16)
+    spread(dot(hidden, w2[...], ((1,), (1,))), out)
 
 
 def inverse_rounds(land):
@@ -187,13 +164,14 @@
 
 def on_device(queries, keys, values, stream, seg_lengths, gain, w_out, w_gate, w_up, w_down):
     z, c = lax.axis_index("z"), lax.axis_index("c")
-    pack = kernel_call(pack_body, shape((4, 288, 128), BF16), 7)(
+    y_axes = ("yh", "yl")
+    pack = kernel_call(pack_body, shape((4, 352, 128), BF16), 7)(
         queries, keys, values, w_gate, w_up, w_down.T, w_out.T
     )
-    got = lax.all_to_all(pack, "y", 0, 0)
+    got = lax.all_to_all(pack, y_axes, 0, 0)
     ends = jnp.cumsum(seg_lengths) - (z * 512 + c * 64)
     sums, mine_w = kernel_call(
-        marks_body, [shape((2, 64, HEAD), F32), shape((4, 96, 128), BF16)], 3
+        marks_body, [shape((2, 64, HEAD), F32), shape((4, 160, 128), BF16)], 3
     )(got, (ends - seg_lengths)[:, None], ends[:, None])
     weights = lax.all_gather(mine_w, ("z", "c"), axis=0)
 
@@ -212,31 +190,31 @@
     land = jax.nn.softmax(mm("id,jd->ij", qm, km) * SCALE, axis=-1)
     inverse = inverse_rounds(land)
 
+    block = pl.BlockSpec(memory_space=pltpu.VMEM)
+    terms = pl.pallas_call(
+        proj_body,
+        grid=(1,),
+        out_shape=shape((16, 64, 512), BF16),
+        in_specs=[block] * 3 + [pl.BlockSpec((32, 4, 16, 128), lambda i: (0, 0, 0, 0))],
+        out_specs=block,
+        scratch_shapes=[pltpu.VMEM((2048, 128), BF16)],
+    )(near, inverse, gathered, weights)
+    parts = lax.all_to_all(terms, (*y_axes, "x"), 0, 0)
+    w1, w2 = kernel_call(unmix_body, [shape((2048, 768), BF16), shape((2048, 384), BF16)], 1)(
+        weights
+    )
+    resid = (stream.astype(F32) + jnp.sum(parts.astype(F32), axis=0)).astype(BF16)
+    whole = lax.all_to_all(jnp.broadcast_to(resid[None], (8, 64, 512)), ("yl", "x"), 0, 0)
     terms = kernel_call(
-        proj_body, shape((16, 64, 512), BF16), 4, [pltpu.VMEM((2048, 128), BF16)]
-    )(near, inverse, gathered, weights)
-    resid = kernel_call(resid_body, shape((16, 64, 512), BF16), 2)(
-        lax.all_to_all(terms, ("y", "x"), 0, 0), stream
-    )
-    whole = lax.all_to_all(resid, ("y", "x"), 0, 0)
-    terms = kernel_call(
-        ffn_body,
-        shape((16, 64, 512), BF16),
-        3,
-        [
-            pltpu.VMEM((256, 2048), BF16),
-            pltpu.VMEM((2048, 384), BF16),
-            pltpu.VMEM((2048, 256), BF16),
-        ],
-    )(whole, gain[None, :], weights)
-    return kernel_call(last_body, shape((64, 512), BF16), 2)(
-        lax.all_to_all(terms, ("y", "x"), 0, 0), resid[0:1]
-    )
+        ffn_body, shape((8, 64, 512), BF16), 4, [pltpu.VMEM((128, 2048), BF16)]
+    )(whole, gain[None, :], w1, w2)
+    parts = lax.all_to_all(terms, ("yl", "x"), 0, 0)
+    return (resid.astype(F32) + jnp.sum(parts.astype(F32), axis=0)).astype(BF16)
 
 
 def solution(mesh):
-    fine = Mesh(mesh.devices.reshape(16, 4, 2, 4), ("z", "y", "c", "x"))
-    seq = ("z", "y", "c")
+    fine = Mesh(mesh.devices.reshape(16, 2, 2, 2, 4), ("z", "yh", "yl", "c", "x"))
+    seq = ("z", "yh", "yl", "c")
     return jax.shard_map(
         on_device,
         mesh=fine,

time: 200 us -> 181 us (0.905)
  waiting for transfers between devices: 32.4 us -> 23.4 us
  blocking collectives: 87.4 us -> 80.5 us
    all_to_all x2, waiting for transfers between devices: 15.6 us -> 5.59 us  [the longest x1 3.06 us: on_device(): got = lax.all_to_all(pack, y_axes, 0, 0)]
    all_to_all x2, blocking collectives: 40.1 us -> 31.1 us  [the longest x1 19.8 us: on_device(): parts = lax.all_to_all(terms, (*y_axes, 'x'), 0, 0)]
    pallas_call x6 -> x5, Pallas kernels: 17.9 us -> 17 us  [the longest x1 5.47 us: on_device(): kernel_call(unmix_body, [shape((2048, 768), BF16), shape((2048, 384), BF1...]
  transfers between devices with their start and end apart: 5 -> 5, of which waited for: 4 -> 4; matrix products, arithmetic and copies ran while one was open for 7% -> 7% of each run, Pallas kernels for 2% -> 5%
where the time goes in v4:
time: 181 us; the launch traced here: 178 us
  blocking collectives  80.5 us (44%)
  waiting for transfers between devices  23.4 us (13%)
  starting transfers between devices  22.1 us (12%)
  Pallas kernels  20.8 us (11%)
  between operations  14.9 us (8%)
  matrix products  6.3 us (3%)
  local copies, waits for them, and re-layouts  5.03 us (3%)
  other arithmetic  5 us (3%)
    all_gather x1, blocking collectives, on_device(): mine = jnp.sum(lax.all_gather(mine, 'z', axis=0), axis=0)  30.2 us
    all_to_all x1, blocking collectives, on_device(): parts = lax.all_to_all(terms, (*y_axes, 'x'), 0, 0)  19.8 us
    all_to_all x1, waiting for transfers between devices, on_device(): gathered = lax.all_to_all(gathered, ('z', 'c'), 0, 0)  11.3 us
    all_to_all x1, blocking collectives, on_device(): parts = lax.all_to_all(terms, ('yl', 'x'), 0, 0)  11.3 us
    all_to_all x1, blocking collectives, on_device(): mine = jnp.sum(lax.all_to_all(sums, 'c', 0, 0), axis=0)  10.8 us
    all_gather x1, blocking collectives, on_device(): marks = lax.all_gather(mine / seg_lengths.astype(F32)[:, None], 'c', axis=0)  8.42 us
    all_to_all x1, starting transfers between devices, on_device(): parts = lax.all_to_all(send, ('z', 'c'), 0, 0)  7.88 us
    all_to_all x1, waiting for transfers between devices, on_device(): parts = lax.all_to_all(send, ('z', 'c'), 0, 0)  6.45 us
  transfers between devices with their start and end apart: 5, of which 4 were waited for; matrix products, arithmetic and copies ran while one was open for 7% of the time, Pallas kernels for 5%

profile of v4, /device:TPU:1, one launch (start us, length us, event | category | flops | bytes accessed | tf_op | source)
XLA Modules:
  0.0 178.0 jit_solution(8648932180996469369)
XLA Ops:
  6.5 1.7 shard_map.100
  8.3 5.0 %all-to-all-start = ((bf16[4,352,128]{2,1,0:T(8,128)(2,1)}), bf16[4,352,128]{2,1,0:T(8,128)(2,1)S(1)}, u32[]{:S(2)}, u32[]{:S(2)}) async-start(bf16[4,352,128]{2,1,0:T(8,128)(2,1)} %shard_map.100), calls=%async_computation | async-start | bytes 720896 | tf_op jit(solution)/shard_map/all_to_all | solution.py:171
  13.3 0.7 copy.20
  14.0 0.1 reduce-window.4
  14.1 0.7 fusion.45
  14.8 0.7 fusion.46
  15.6 0.7 copy.21.starts
  16.3 3.1 %all-to-all-done.got = bf16[4,352,128]{2,1,0:T(8,128)(2,1)S(1)} async-done(((bf16[4,352,128]{2,1,0:T(8,128)(2,1)}), bf16[4,352,128]{2,1,0:T(8,128)(2,1)S(1)}, u32[]{:S(2)}, u32[]{:S(2)}) %all-to-all-start) | async-done | bytes 360480 | tf_op jit(solution)/shard_map/all_to_all | solution.py:171
  19.3 0.7 copy-done
  20.1 1.9 %shard_map.101 = (f32[2,64,128]{2,1,0:T(8,128)}, bf16[4,160,128]{2,1,0:T(8,128)(2,1)}) custom-call(bf16[4,352,128]{2,1,0:T(8,128)(2,1)} %copy-done, s32[64,1]{1,0:T(8,128)} %copy.21.starts, s32[64,1]{1,0:T(8,128)} %get-tuple-element.16.ends), custom_call_target="tpu_custom_call" | custom-call | tf_op jit(solution)/shard_map/pallas_call | solution.py:173
  21.9 10.8 %all_to_all.35 = f32[2,64,128]{2,1,0:T(8,128)S(1)} all-to-all(f32[2,64,128]{2,1,0:T(8,128)} %get-tuple-element.9), channel_id=1, replica_groups=mesh['z'=16,'yh'=2,'yl'=2,'c'=2,'x'=4] {'c'}, dimensions={0} | all-to-all | bytes 131072 | tf_op jit(solution)/shard_map/all_to_all | solution.py:178
  32.7 30.2 %all-gather = f32[1024,128]{1,0:T(8,128)S(1)} all-gather(f32[64,128]{1,0:T(8,128)S(1)} %reduce_sum.74), channel_id=2, replica_groups=mesh['z'=16,'yh'=2,'yl'=2,'c'=2,'x'=4] {'z'}, dimensions={0}, use_global_device_ids=true | all-gather | bytes 557056 | tf_op jit(solution)/shard_map/all_gather | solution.py:179
  63.0 0.1 bitcast_divide_fusion
  63.1 8.4 %all_gather.18.marks = f32[2,64,128]{2,1,0:T(8,128)S(1)} all-gather(f32[1,64,128]{2,1,0:T(8,128)S(1)} %bitcast_divide_fusion), channel_id=1, replica_groups=mesh['z'=16,'yh'=2,'yl'=2,'c'=2,'x'=4] {'c'}, dimensions={0}, use_global_device_ids=true | all-gather | bytes 98304 | tf_op jit(solution)/shard_map/all_gather | solution.py:180
  71.5 0.2 fusion.48
  71.7 0.1 fusion.43
  71.9 0.7 reduce_max.38
  72.5 0.6 reduce_max.39
  73.2 2.2 %shard_map.102 = f32[32,4,128]{2,1,0:T(4,128)} custom-call(bf16[4,352,128]{2,1,0:T(8,128)(2,1)} %copy-done, f32[2,64,128]{2,1,0:T(8,128)} %copy-done.2), custom_call_target="tpu_custom_call" | custom-call | tf_op jit(solution)/shard_map/pallas_call | solution.py:183
  75.4 7.9 %all-to-all-start.2 = ((f32[32,4,128]{2,1,0:T(4,128)}), f32[32,4,128]{2,1,0:T(4,128)S(1)}, u32[]{:S(2)}, u32[]{:S(2)}) async-start(f32[32,4,128]{2,1,0:T(4,128)} %shard_map.102), calls=%async_computation.2 | async-start | bytes 131072 | tf_op jit(solution)/shard_map/all_to_all | solution.py:184
  84.6 0.2 fusion.18
  84.8 0.2 convolution_subtract_fusion.11
  85.0 0.2 convolution_subtract_fusion.10
  85.2 0.2 convolution_multiply_fusion.6
  85.3 0.2 fusion.40
  85.6 0.2 convolution_subtract_fusion.9
  85.8 0.2 convolution_subtract_fusion.8
  85.9 0.2 convolution_multiply_fusion.5
  86.1 0.2 fusion.38
  86.4 0.2 convolution_subtract_fusion.7
  86.5 0.2 convolution_subtract_fusion.6
  86.7 0.2 convolution_multiply_fusion.4
  86.9 0.2 fusion.36
  87.1 0.2 convolution_subtract_fusion.5
  87.3 0.2 convolution_subtract_fusion.4
  87.5 0.2 convolution_multiply_fusion.3
  87.6 0.2 fusion.34
  87.9 0.2 convolution_subtract_fusion.3
  88.1 0.2 convolution_subtract_fusion.2
  88.2 0.2 convolution_multiply_fusion.2
  88.4 0.2 fusion.32
  88.7 0.2 convolution_subtract_fusion.1
  88.8 0.2 convolution_subtract_fusion
  89.0 1.1 fusion.47
  90.1 0.2 fusion.1
  90.3 0.8 fusion.near
  91.1 6.4 %all-to-all-done.2.parts = f32[32,4,128]{2,1,0:T(4,128)S(1)} async-done(((f32[32,4,128]{2,1,0:T(4,128)}), f32[32,4,128]{2,1,0:T(4,128)S(1)}, u32[]{:S(2)}, u32[]{:S(2)}) %all-to-all-start.2) | async-done | bytes 65568 | tf_op jit(solution)/shard_map/all_to_all | solution.py:184
  97.5 0.6 copy-done.3
  98.1 1.6 shard_map.103
  99.7 5.7 %all-to-all-start.3 = ((f32[32,2,128]{2,1,0:T(2,128)}), f32[32,2,128]{2,1,0:T(2,128)S(1)}, u32[]{:S(2)}, u32[]{:S(2)}) async-start(f32[32,2,128]{2,1,0:T(2,128)} %shard_map.103), calls=%async_computation.3 | async-start | bytes 65536 | tf_op jit(solution)/shard_map/all_to_all | solution.py:186
  105.5 0.8 convolution_multiply_fusion.1.inverse
  106.2 11.3 %all-to-all-done.3.gathered = f32[32,2,128]{2,1,0:T(2,128)S(1)} async-done(((f32[32,2,128]{2,1,0:T(2,128)}), f32[32,2,128]{2,1,0:T(2,128)S(1)}, u32[]{:S(2)}, u32[]{:S(2)}) %all-to-all-start.3) | async-done | bytes 32800 | tf_op jit(solution)/shard_map/all_to_all | solution.py:186
  117.6 0.6 copy-done.4
  118.2 3.1 %shard_map.104 = bf16[16,64,512]{2,1,0:T(8,128)(2,1)} custom-call(f32[256,64]{1,0:T(8,128)} %fusion.near, f32[64,64]{1,0:T(8,128)} %convolution_multiply_fusion.1.inverse, f32[32,2,128]{2,1,0:T(2,128)} %copy-done.4, bf16[32,4,160,128]{3,2,1,0:T(8,128)(2,1)} %bitcast.59), custom_call_target="tpu_custom_call" | custom-call | tf_op jit(solution)/shard_map/pallas_call | solution.py:194
  121.3 19.8 %all_to_all.36 = bf16[16,64,512]{2,1,0:T(8,128)(2,1)S(1)} all-to-all(bf16[16,64,512]{2,1,0:T(8,128)(2,1)} %shard_map.104), channel_id=1, replica_groups=mesh['z'=16,'yh'=2,'yl'=2,'c'=2,'x'=4] {'yh','yl','x'}, dimensions={0} | all-to-all | bytes 2097152 | tf_op jit(solution)/shard_map/all_to_all | solution.py:202
  141.1 0.1 convert_reduce_fusion
  141.3 0.8 broadcast_in_dim.7
  142.1 3.5 %all-to-all-start.5 = ((bf16[8,64,512]{2,1,0:T(8,128)(2,1)}), bf16[8,64,512]{2,1,0:T(8,128)(2,1)S(1)}, u32[]{:S(2)}, u32[]{:S(2)}) async-start(bf16[8,64,512]{2,1,0:T(8,128)(2,1)} %broadcast_in_dim.7), calls=%async_computation.5 | async-start | bytes 1048576 | tf_op jit(solution)/shard_map/all_to_all | solution.py:207
  145.6 5.5 %shard_map.105 = (bf16[2048,768]{1,0:T(8,128)(2,1)}, bf16[2048,384]{1,0:T(8,128)(2,1)}) custom-call(bf16[32,4,160,128]{3,2,1,0:T(8,128)(2,1)} %bitcast.60), custom_call_target="tpu_custom_call" | custom-call | tf_op jit(solution)/shard_map/pallas_call | solution.py:203
  151.1 2.5 %all-to-all-done.5.whole = bf16[8,64,512]{2,1,0:T(8,128)(2,1)S(1)} async-done(((bf16[8,64,512]{2,1,0:T(8,128)(2,1)}), bf16[8,64,512]{2,1,0:T(8,128)(2,1)S(1)}, u32[]{:S(2)}, u32[]{:S(2)}) %all-to-all-start.5) | async-done | bytes 524320 | tf_op jit(solution)/shard_map/all_to_all | solution.py:207
  153.6 0.8 copy-done.1
  154.4 4.8 %shard_map.106 = bf16[8,64,512]{2,1,0:T(8,128)(2,1)} custom-call(bf16[8,64,512]{2,1,0:T(8,128)(2,1)} %copy-done.1, f32[1,2048]{1,0:T(1,128)} %bitcast.65, bf16[2048,768]{1,0:T(8,128)(2,1)} %get-tuple-element.11.w1, bf16[2048,384]{1,0:T(8,128)(2,1)} %get-tuple-element.12.w2), custom_call_target="tpu_custom_call" | custom-call | tf_op jit(solution)/shard_map/pallas_call | solution.py:208
  159.2 11.3 %all_to_all.37 = bf16[8,64,512]{2,1,0:T(8,128)(2,1)S(1)} all-to-all(bf16[8,64,512]{2,1,0:T(8,128)(2,1)} %shard_map.106), channel_id=1, replica_groups=mesh['z'=16,'yh'=2,'yl'=2,'c'=2,'x'=4] {'yl','x'}, dimensions={0} | all-to-all | bytes 1048576 | tf_op jit(solution)/shard_map/all_to_all | solution.py:211
  170.5 0.6 add_convert_fusion
  (19 shorter events, 0.2 us)
Async XLA Ops:
  8.3 11.1 %all-to-all-start = ((bf16[4,352,128]{2,1,0:T(8,128)(2,1)}), bf16[4,352,128]{2,1,0:T(8,128)(2,1)S(1)}, u32[]{:S(2)}, u32[]{:S(2)}) async-start(bf16[4,352,128]{2,1,0:T(8,128)(2,1)} %shard_map.100), calls=%async_computation | async-start | bytes 720896 | tf_op jit(solution)/shard_map/all_to_all | solution.py:171
  13.3 104.3 %all-gather.4.cloned.1.call-start = ((), (), s32[]{:S(2)}) async-start(), calls=%async_computation.7 | async-start | bytes 5406720 | tf_op jit(solution)/shard_map/all_gather | solution.py:176
  19.3 0.7 copy-start
  21.9 67.1 %slice-start = ((bf16[4,352,128]{2,1,0:T(8,128)(2,1)}), bf16[4,64,128]{2,1,0:T(8,128)(2,1)S(1)}, s32[]{:S(2)}) async-start(bf16[4,352,128]{2,1,0:T(8,128)(2,1)} %copy-done), calls=%async_computation.8 | async-start | bytes 131072 | tf_op jit(solution)/shard_map/slice | solution.py:188
  71.5 1.7 copy-start.2
  75.4 22.1 %all-to-all-start.2 = ((f32[32,4,128]{2,1,0:T(4,128)}), f32[32,4,128]{2,1,0:T(4,128)S(1)}, u32[]{:S(2)}, u32[]{:S(2)}) async-start(f32[32,4,128]{2,1,0:T(4,128)} %shard_map.102), calls=%async_computation.2 | async-start | bytes 131072 | tf_op jit(solution)/shard_map/all_to_all | solution.py:184
  97.5 0.6 copy-start.3
  99.7 17.9 %all-to-all-start.3 = ((f32[32,2,128]{2,1,0:T(2,128)}), f32[32,2,128]{2,1,0:T(2,128)S(1)}, u32[]{:S(2)}, u32[]{:S(2)}) async-start(f32[32,2,128]{2,1,0:T(2,128)} %shard_map.103), calls=%async_computation.3 | async-start | bytes 65536 | tf_op jit(solution)/shard_map/all_to_all | solution.py:186
  117.6 0.6 copy-start.4
  121.3 20.0 %copy-start.5 = (bf16[64,512]{1,0:T(8,128)(2,1)S(1)}, bf16[64,512]{1,0:T(8,128)(2,1)}, u32[]{:S(2)}) copy-start(bf16[64,512]{1,0:T(8,128)(2,1)} %param.13) | copy-start | bytes 196612
  142.1 11.5 %all-to-all-start.5 = ((bf16[8,64,512]{2,1,0:T(8,128)(2,1)}), bf16[8,64,512]{2,1,0:T(8,128)(2,1)S(1)}, u32[]{:S(2)}, u32[]{:S(2)}) async-start(bf16[8,64,512]{2,1,0:T(8,128)(2,1)} %broadcast_in_dim.7), calls=%async_computation.5 | async-start | bytes 1048576 | tf_op jit(solution)/shard_map/all_to_all | solution.py:207
  153.6 0.8 copy-start.1
Sparse Core Ops, SparseCore 0:
  22.1 83.1 all-gather.3

commit v5 on v4

--- a/solution.py
+++ b/solution.py
@@ -15,10 +15,6 @@
 HI = lax.Precision.HIGHEST
 F32 = jnp.float32
 BF16 = jnp.bfloat16
-
-
-def mm(spec, a, b):
-    return jnp.einsum(spec, a, b, precision=HI, preferred_element_type=F32)
 
 
 def dot(a, b, dims, precision=None):
@@ -58,8 +54,9 @@
                 out[y, at : at + 16] = w[:, low : low + 128]
 
 
-def marks_body(got, starts, ends, sums, weights):
+def marks_body(got, starts, ends, sums, weights, kv):
     weights[...] = got[:, 192:352]
+    kv[...] = got[:, 64:192]
     at = lax.broadcasted_iota(jnp.int32, (64, 256), 1)
     at = at + (at // 64) * 64
     member = ((at >= starts[...]) & (at < ends[...])).astype(BF16)
@@ -68,34 +65,64 @@
         sums[i] = dot(member, part, ((1,), (0,)))
 
 
-def far_body(got, marks, out):
-    k = got[:, 64:128].reshape(256, HEAD).astype(F32)
-    v = got[:, 128:192].reshape(256, HEAD).astype(F32)
-    far = dot(marks[0], k, ((1,), (1,)), HI) * SCALE
-    peak = jnp.max(far, axis=-1, keepdims=True)
-    far = jnp.exp(far - peak)
-    mass = jnp.sum(far, axis=-1, keepdims=True)
-    part = dot(far, v, ((1,), (0,)), HI)
-    lane = lax.broadcasted_iota(jnp.int32, (64, HEAD), 1)
-    stats = jnp.where(lane < 64, peak, mass)
-    for i in range(2):
-        out[:, i, :] = part[32 * i : 32 * i + 32]
-        out[:, 2 + i, :] = stats[32 * i : 32 * i + 32]
+def far_body(core, mine, other, marks, out):
+    query = marks[0, pl.ds(core[0] * 32, 32), :]
+    far = [
+        dot(query, kv[:, 0:64].reshape(256, HEAD).astype(F32), ((1,), (1,)), HI) * SCALE
+        for kv in (mine, other)
+    ]
+    peak = jnp.maximum(*(jnp.max(f, axis=-1, keepdims=True) for f in far))
+    far = [jnp.exp(f - peak) for f in far]
+    mass = sum(jnp.sum(f, axis=-1, keepdims=True) for f in far)
+    part = sum(
+        dot(f, kv[:, 64:128].reshape(256, HEAD).astype(F32), ((1,), (0,)), HI)
+        for f, kv in zip(far, (mine, other))
+    )
+    row = lax.broadcasted_iota(jnp.int32, (32, HEAD), 0)
+    lane = lax.broadcasted_iota(jnp.int32, (32, HEAD), 1)
+    stats = jnp.where(lane == row, peak, 0.0) + jnp.where(lane == row + 32, mass, 0.0)
+    stats = jnp.broadcast_to(jnp.sum(stats, axis=0, keepdims=True), (8, HEAD))
+    for z in range(16):
+        out[z, 0:32] = part
+        out[z, 32:40] = stats
 
 
 def merge_body(parts, out):
-    rows = []
-    for i in range(2):
-        stats = parts[:, 2 + i, :]
-        low = lax.broadcasted_iota(jnp.int32, (32, HEAD), 1) < 64
-        other = pltpu.roll(stats, 64, 1)
-        peak = jnp.where(low, stats, other)
-        mass = jnp.where(low, other, stats)
-        factor = jnp.exp(peak - jnp.max(peak, axis=0, keepdims=True))
-        total = jnp.sum(factor * mass, axis=0, keepdims=True)
-        rows.append(jnp.sum(factor * parts[:, i, :], axis=0, keepdims=True) / total)
-    for i in range(2):
-        out[:, i, :] = jnp.broadcast_to(rows[i], (32, HEAD))
+    row = lax.broadcasted_iota(jnp.int32, (16, 32, HEAD), 1)
+    lane = lax.broadcasted_iota(jnp.int32, (16, 32, HEAD), 2)
+    stats = jnp.broadcast_to(parts[:, 32:33, :], (16, 32, HEAD))
+    peak = jnp.sum(jnp.where(lane == row, stats, 0.0), axis=-1, keepdims=True)
+    mass = jnp.sum(jnp.where(lane == row + 32, stats, 0.0), axis=-1, keepdims=True)
+    factor = jnp.exp(peak - jnp.max(peak, axis=0, keepdims=True))
+    total = jnp.sum(factor * mass, axis=0)
+    out[...] = jnp.sum(factor * parts[:, 0:32, :], axis=0) / total
+
+
+def softmax(scores, axis):
+    scores = jnp.exp(scores - jnp.max(scores, axis=axis, keepdims=True))
+    return scores / jnp.sum(scores, axis=axis, keepdims=True)
+
+
+def near_body(got, marks, near, inverse):
+    qm, km = marks[0], marks[1]
+    query = got[:, 0:64].reshape(256, HEAD).astype(F32)
+    near[...] = softmax(dot(query, km, ((1,), (1,)), HI) * SCALE, -1)
+    land = softmax(dot(qm, km, ((1,), (1,)), HI) * SCALE, 1)
+    across = softmax(dot(km, qm, ((1,), (1,)), HI) * SCALE, 0)
+    most = jnp.max(jnp.sum(land, axis=0, keepdims=True), axis=1, keepdims=True) * jnp.max(
+        jnp.sum(land, axis=1, keepdims=True), axis=0, keepdims=True
+    )
+    row = lax.broadcasted_iota(jnp.int32, (64, 64), 0)
+    eye = (row == lax.broadcasted_iota(jnp.int32, (64, 64), 1)).astype(F32)
+    mul = lambda a, b: dot(a, b, ((1,), (0,)), HI)
+    approx = across / most
+    for _ in range(PINV_ITERS):
+        prod = mul(land, approx)
+        inner = 7.0 * eye - prod
+        inner = 15.0 * eye - mul(prod, inner)
+        inner = 13.0 * eye - mul(prod, inner)
+        approx = 0.25 * mul(approx, inner)
+    inverse[...] = approx
 
 
 def spread(terms, out):
@@ -121,13 +148,9 @@
         unmix(weights, 7 + t, w2, slice(t * 128, t * 128 + 128))
 
 
-def both(ref, i):
-    return jnp.concatenate([ref[:, i, :], ref[:, i + 1, :]], axis=0)
-
-
 def proj_body(near, inverse, gathered, weights, out, wo):
     unmix(weights, 0, wo, slice(0, 128))
-    mixer = dot(inverse[...], both(gathered, 0), ((1,), (0,)), HI)
+    mixer = dot(inverse[...], gathered[...], ((1,), (0,)), HI)
     attn = dot(near[...], mixer, ((1,), (0,)), HI).astype(BF16)
     spread(dot(attn, wo[...], ((1,), (1,))), out)
 
@@ -148,20 +171,6 @@
     spread(dot(hidden, w2[...], ((1,), (1,))), out)
 
 
-def inverse_rounds(land):
-    eye = jnp.eye(land.shape[-1], dtype=F32)
-    col_most = jnp.max(jnp.sum(land, axis=0))
-    row_most = jnp.max(jnp.sum(land, axis=1))
-    approx = land.T / (col_most * row_most)
-    for _ in range(PINV_ITERS):
-        prod = mm("ij,jk->ik", land, approx)
-        inner = 7.0 * eye - prod
-        inner = 15.0 * eye - mm("ij,jk->ik", prod, inner)
-        inner = 13.0 * eye - mm("ij,jk->ik", prod, inner)
-        approx = 0.25 * mm("ij,jk->ik", approx, inner)
-    return approx
-
-
 def on_device(queries, keys, values, stream, seg_lengths, gain, w_out, w_gate, w_up, w_down):
     z, c = lax.axis_index("z"), lax.axis_index("c")
     y_axes = ("yh", "yl")
@@ -170,27 +179,36 @@
     )
     got = lax.all_to_all(pack, y_axes, 0, 0)
     ends = jnp.cumsum(seg_lengths) - (z * 512 + c * 64)
-    sums, mine_w = kernel_call(
-        marks_body, [shape((2, 64, HEAD), F32), shape((4, 160, 128), BF16)], 3
+    sums, mine_w, kv = kernel_call(
+        marks_body,
+        [shape((2, 64, HEAD), F32), shape((4, 160, 128), BF16), shape((4, 128, 128), BF16)],
+        3,
     )(got, (ends - seg_lengths)[:, None], ends[:, None])
     weights = lax.all_gather(mine_w, ("z", "c"), axis=0)
 
-    mine = jnp.sum(lax.all_to_all(sums, "c", 0, 0), axis=0)
+    other = lax.ppermute(kv, "c", [(0, 1), (1, 0)])
+    mine = lax.all_to_all(sums, "c", 0, 0)
+    mine, other = lax.optimization_barrier((mine, other))
+    mine = jnp.sum(mine, axis=0)
     mine = jnp.sum(lax.all_gather(mine, "z", axis=0), axis=0)
     marks = lax.all_gather(mine / seg_lengths.astype(F32)[:, None], "c", axis=0)
-    qm, km = marks[0], marks[1]
-
-    send = kernel_call(far_body, shape((32, 4, HEAD), F32), 2)(got, marks)
-    parts = lax.all_to_all(send, ("z", "c"), 0, 0)
-    gathered = kernel_call(merge_body, shape((32, 2, HEAD), F32), 1)(parts)
-    gathered = lax.all_to_all(gathered, ("z", "c"), 0, 0)
-
-    q32 = got[:, 0:64].reshape(256, HEAD).astype(F32)
-    near = jax.nn.softmax(mm("td,jd->tj", q32, km) * SCALE, axis=-1)
-    land = jax.nn.softmax(mm("id,jd->ij", qm, km) * SCALE, axis=-1)
-    inverse = inverse_rounds(land)
-
     block = pl.BlockSpec(memory_space=pltpu.VMEM)
+    send = pl.pallas_call(
+        far_body,
+        out_shape=shape((16, 40, HEAD), F32),
+        in_specs=[pl.BlockSpec(memory_space=pltpu.SMEM)] + [block] * 3,
+        out_specs=block,
+    )(c[None], kv, other, marks)
+    parts = lax.all_to_all(send, "z", 0, 0)
+    near, inverse = kernel_call(
+        near_body,
+        [shape((256, 64), F32), shape((64, 64), F32)],
+        2,
+        cost=pl.CostEstimate(flops=10**9, bytes_accessed=2 * 10**7, transcendentals=0),
+    )(got, marks)
+    gathered = kernel_call(merge_body, shape((32, HEAD), F32), 1)(parts)
+    gathered = lax.all_gather(gathered, "c", axis=0, tiled=True)
+
     terms = pl.pallas_call(
         proj_body,
         grid=(1,),

time: 181 us -> 181 us (level); the launches traced: 178 us -> 180 us
  blocking collectives: 80.5 us -> 87.5 us
  Pallas kernels: 20.8 us -> 27.3 us
  matrix products: 6.3 us -> 0 us
  other arithmetic: 5 us -> 2.56 us
    ppermute x0 -> x1, starting transfers between devices: none -> 8.35 us  [on_device(): other = lax.ppermute(kv, 'c', [(0, 1), (1, 0)])]
    all_to_all x2 -> x1, starting transfers between devices: 13.6 us -> 6.39 us  [on_device(): parts = lax.all_to_all(send, 'z', 0, 0)]
    all_gather x0 -> x1, blocking collectives: none -> 6.81 us  [on_device(): gathered = lax.all_gather(gathered, 'c', axis=0, tiled=True)]
    pallas_call x2 -> x3, Pallas kernels: 3.8 us -> 10.3 us  [the longest x1 6.14 us: on_device(): kernel_call(near_body, [shape((256, 64), F32), shape((64, 64), F32)], 2,...]
    all_to_all x1, blocking collectives: 10.8 us -> 4.37 us  [on_device(): mine = lax.all_to_all(sums, 'c', 0, 0)]
    dot_general x26 -> x0, matrix products: 6.3 us -> none  [mm(): return jnp.einsum(spec, a, b, precision=HI, preferred_element_type=F32)]
    all_to_all x1, blocking collectives: 19.8 us -> 23 us  [on_device(): parts = lax.all_to_all(terms, (*y_axes, 'x'), 0, 0)]
    all_to_all x2 -> x1, waiting for transfers between devices: 17.8 us -> 14.7 us  [on_device(): parts = lax.all_to_all(send, 'z', 0, 0)]
  transfers between devices with their start and end apart: 5 -> 5, of which waited for: 4 -> 3; matrix products, arithmetic and copies ran while one was open for 7% -> 2% of each run, Pallas kernels for 5% -> 9%
where the time goes in v5:
time: 181 us; the launch traced here: 180 us
  blocking collectives  87.5 us (48%)
  Pallas kernels  27.3 us (15%)
  starting transfers between devices  23.2 us (13%)
  waiting for transfers between devices  21.7 us (12%)
  between operations  13.5 us (7%)
  local copies, waits for them, and re-layouts  4.56 us (3%)
  other arithmetic  2.56 us (1%)
    all_gather x1, blocking collectives, on_device(): mine = jnp.sum(lax.all_gather(mine, 'z', axis=0), axis=0)  31.6 us
    all_to_all x1, blocking collectives, on_device(): parts = lax.all_to_all(terms, (*y_axes, 'x'), 0, 0)  23 us
    all_to_all x1, waiting for transfers between devices, on_device(): parts = lax.all_to_all(send, 'z', 0, 0)  14.7 us
    all_to_all x1, blocking collectives, on_device(): parts = lax.all_to_all(terms, ('yl', 'x'), 0, 0)  12.3 us
    all_gather x1, blocking collectives, on_device(): marks = lax.all_gather(mine / seg_lengths.astype(F32)[:, None], 'c', axis=0)  9.39 us
    ppermute x1, starting transfers between devices, on_device(): other = lax.ppermute(kv, 'c', [(0, 1), (1, 0)])  8.35 us
    all_gather x1, blocking collectives, on_device(): gathered = lax.all_gather(gathered, 'c', axis=0, tiled=True)  6.81 us
    all_to_all x1, starting transfers between devices, on_device(): parts = lax.all_to_all(send, 'z', 0, 0)  6.39 us
  transfers between devices with their start and end apart: 5, of which 3 were waited for; matrix products, arithmetic and copies ran while one was open for 2% of the time, Pallas kernels for 9%

profile of v5, /device:TPU:1, one launch (start us, length us, event | category | flops | bytes accessed | tf_op | source)
XLA Modules:
  0.0 180.3 jit_solution(4289692292699018574)
XLA Ops:
  6.5 1.7 shard_map.100
  8.3 5.0 %all-to-all-start = ((bf16[4,352,128]{2,1,0:T(8,128)(2,1)}), bf16[4,352,128]{2,1,0:T(8,128)(2,1)S(1)}, u32[]{:S(2)}, u32[]{:S(2)}) async-start(bf16[4,352,128]{2,1,0:T(8,128)(2,1)} %shard_map.100), calls=%async_computation | async-start | bytes 720896 | tf_op jit(solution)/shard_map/all_to_all | solution.py:180
  13.3 0.0 all-gather.4.cloned.1.call-start
  13.3 0.7 copy.17
  14.0 0.1 reduce-window.4
  14.1 0.7 fusion
  14.8 0.7 fusion.1
  15.6 0.7 copy.18.starts
  16.3 3.0 %all-to-all-done.got = bf16[4,352,128]{2,1,0:T(8,128)(2,1)S(1)} async-done(((bf16[4,352,128]{2,1,0:T(8,128)(2,1)}), bf16[4,352,128]{2,1,0:T(8,128)(2,1)S(1)}, u32[]{:S(2)}, u32[]{:S(2)}) %all-to-all-start) | async-done | bytes 360480 | tf_op jit(solution)/shard_map/all_to_all | solution.py:180
  19.3 0.0 copy-start.1
  19.3 0.8 copy-done.1
  20.1 1.9 %shard_map.101 = (f32[2,64,128]{2,1,0:T(8,128)}, bf16[4,160,128]{2,1,0:T(8,128)(2,1)}, bf16[4,128,128]{2,1,0:T(8,128)(2,1)}) custom-call(bf16[4,352,128]{2,1,0:T(8,128)(2,1)} %copy-done.1, s32[64,1]{1,0:T(8,128)} %copy.18.starts, s32[64,1]{1,0:T(8,128)} %get-tuple-element.24.ends), custom_call_target="tpu_custom_call" | custom-call | tf_op jit(solution)/shard_map/pallas_call | solution.py:182
  21.9 0.0 all-gather.4.cloned.1.call-update
  22.0 8.4 %collective-permute-start = (bf16[4,128,128]{2,1,0:T(8,128)(2,1)}, bf16[4,128,128]{2,1,0:T(8,128)(2,1)S(1)}, u32[]{:S(2)}, u32[]{:S(2)}) collective-permute-start(bf16[4,128,128]{2,1,0:T(8,128)(2,1)} %get-tuple-element.15.mine), channel_id=1, source_target_pairs={{0,4},{4,0},{1,5},{5,1},{2,6},{6,2},{3,7},{7,3},{8,12},{12,8},{9,1... | collective-permute-start | bytes 393224 | tf_op jit(solution)/shard_map/ppermute | solution.py:189
  30.3 4.4 %all_to_all.30 = f32[2,64,128]{2,1,0:T(8,128)S(1)} all-to-all(f32[2,64,128]{2,1,0:T(8,128)} %get-tuple-element.14), channel_id=1, replica_groups=mesh['z'=16,'yh'=2,'yl'=2,'c'=2,'x'=4] {'c'}, dimensions={0} | all-to-all | bytes 131072 | tf_op jit(solution)/shard_map/all_to_all | solution.py:190
  34.7 0.0 collective-permute-done.other
  34.7 0.0 copy-start.3
  34.7 31.6 %all-gather = f32[1024,128]{1,0:T(8,128)S(1)} all-gather(f32[64,128]{1,0:T(8,128)S(1)} %reduce_sum.38), channel_id=2, replica_groups=mesh['z'=16,'yh'=2,'yl'=2,'c'=2,'x'=4] {'z'}, dimensions={0}, use_global_device_ids=true | all-gather | bytes 557056 | tf_op jit(solution)/shard_map/all_gather | solution.py:193
  66.4 0.1 bitcast_divide_fusion
  66.5 9.4 %all_gather.21.marks = f32[2,64,128]{2,1,0:T(8,128)} all-gather(f32[1,64,128]{2,1,0:T(8,128)S(1)} %bitcast_divide_fusion), channel_id=1, replica_groups=mesh['z'=16,'yh'=2,'yl'=2,'c'=2,'x'=4] {'c'}, dimensions={0}, use_global_device_ids=true | all-gather | bytes 98304 | tf_op jit(solution)/shard_map/all_gather | solution.py:194
  75.9 0.0 copy-done.3
  75.9 2.4 %shard_map.103 = f32[16,40,128]{2,1,0:T(8,128)} custom-call(s32[1]{0:T(128)} %bitcast.6.core, bf16[4,128,128]{2,1,0:T(8,128)(2,1)} %get-tuple-element.15.mine, bf16[4,128,128]{2,1,0:T(8,128)(2,1)} %copy-done.3, f32[2,64,128]{2,1,0:T(8,128)} %all_gather.21.marks), custom_call_target="tpu_custom_call" | custom-call | tf_op jit(solution)/shard_map/pallas_call | solution.py:196
  78.2 6.4 %all-to-all-start.2 = ((f32[16,40,128]{2,1,0:T(8,128)}), f32[16,40,128]{2,1,0:T(8,128)S(1)}, u32[]{:S(2)}, u32[]{:S(2)}) async-start(f32[16,40,128]{2,1,0:T(8,128)} %shard_map.103), calls=%async_computation.2 | async-start | bytes 655360 | tf_op jit(solution)/shard_map/all_to_all | solution.py:202
  84.6 6.1 %shard_map.102 = (f32[256,64]{1,0:T(8,128)}, f32[64,64]{1,0:T(8,128)}) custom-call(bf16[4,352,128]{2,1,0:T(8,128)(2,1)} %copy-done.1, f32[2,64,128]{2,1,0:T(8,128)} %all_gather.21.marks), custom_call_target="tpu_custom_call" | custom-call | flops 1000000000 | bytes 20000000 | tf_op jit(solution)/shard_map/pallas_call | solution.py:203
  90.8 14.7 %all-to-all-done.2.parts = f32[16,40,128]{2,1,0:T(8,128)S(1)} async-done(((f32[16,40,128]{2,1,0:T(8,128)}), f32[16,40,128]{2,1,0:T(8,128)S(1)}, u32[]{:S(2)}, u32[]{:S(2)}) %all-to-all-start.2) | async-done | bytes 327712 | tf_op jit(solution)/shard_map/all_to_all | solution.py:202
  105.4 0.0 copy-start.2
  105.5 0.7 copy-done.2
  106.2 1.8 shard_map.104
  108.0 6.8 %all_gather.22.gathered = f32[64,128]{1,0:T(8,128)} all-gather(f32[32,128]{1,0:T(8,128)} %shard_map.104), channel_id=1, replica_groups=mesh['z'=16,'yh'=2,'yl'=2,'c'=2,'x'=4] {'c'}, dimensions={0}, use_global_device_ids=true | all-gather | bytes 49152 | tf_op jit(solution)/shard_map/all_gather | solution.py:210
  114.8 0.0 all-gather.4.cloned.1.call-done
  114.8 3.1 %shard_map.105 = bf16[16,64,512]{2,1,0:T(8,128)(2,1)} custom-call(f32[256,64]{1,0:T(8,128)} %get-tuple-element.17.near, f32[64,64]{1,0:T(8,128)} %get-tuple-element.18.inverse, f32[64,128]{1,0:T(8,128)} %all_gather.22.gathered, bf16[32,4,160,128]{3,2,1,0:T(8,128)(2,1)} %bitcast.11), custom_call_target="tpu_custom_call" | custom-call | tf_op jit(solution)/shard_map/pallas_call | solution.py:212
  117.9 0.0 copy-start.4
  117.9 23.0 %all_to_all.31 = bf16[16,64,512]{2,1,0:T(8,128)(2,1)S(1)} all-to-all(bf16[16,64,512]{2,1,0:T(8,128)(2,1)} %shard_map.105), channel_id=1, replica_groups=mesh['z'=16,'yh'=2,'yl'=2,'c'=2,'x'=4] {'yh','yl','x'}, dimensions={0} | all-to-all | bytes 2097152 | tf_op jit(solution)/shard_map/all_to_all | solution.py:220
  140.9 0.1 convert_reduce_fusion
  141.0 0.0 copy-done.4
  141.1 0.8 broadcast_in_dim.19
  141.9 3.5 %all-to-all-start.4 = ((bf16[8,64,512]{2,1,0:T(8,128)(2,1)}), bf16[8,64,512]{2,1,0:T(8,128)(2,1)S(1)}, u32[]{:S(2)}, u32[]{:S(2)}) async-start(bf16[8,64,512]{2,1,0:T(8,128)(2,1)} %broadcast_in_dim.19), calls=%async_computation.4 | async-start | bytes 1048576 | tf_op jit(solution)/shard_map/all_to_all | solution.py:225
  145.4 5.5 %shard_map.106 = (bf16[2048,768]{1,0:T(8,128)(2,1)}, bf16[2048,384]{1,0:T(8,128)(2,1)}) custom-call(bf16[32,4,160,128]{3,2,1,0:T(8,128)(2,1)} %bitcast.12), custom_call_target="tpu_custom_call" | custom-call | tf_op jit(solution)/shard_map/pallas_call | solution.py:221
  150.9 4.0 %all-to-all-done.4.whole = bf16[8,64,512]{2,1,0:T(8,128)(2,1)S(1)} async-done(((bf16[8,64,512]{2,1,0:T(8,128)(2,1)}), bf16[8,64,512]{2,1,0:T(8,128)(2,1)S(1)}, u32[]{:S(2)}, u32[]{:S(2)}) %all-to-all-start.4) | async-done | bytes 524320 | tf_op jit(solution)/shard_map/all_to_all | solution.py:225
  154.9 0.0 copy-start
  154.9 0.8 copy-done
  155.7 4.8 %shard_map.107 = bf16[8,64,512]{2,1,0:T(8,128)(2,1)} custom-call(bf16[8,64,512]{2,1,0:T(8,128)(2,1)} %copy-done, f32[1,2048]{1,0:T(1,128)} %bitcast.16, bf16[2048,768]{1,0:T(8,128)(2,1)} %get-tuple-element.21.w1, bf16[2048,384]{1,0:T(8,128)(2,1)} %get-tuple-element.22.w2), custom_call_target="tpu_custom_call" | custom-call | tf_op jit(solution)/shard_map/pallas_call | solution.py:226
  160.5 12.3 %all_to_all.32 = bf16[8,64,512]{2,1,0:T(8,128)(2,1)S(1)} all-to-all(bf16[8,64,512]{2,1,0:T(8,128)(2,1)} %shard_map.107), channel_id=1, replica_groups=mesh['z'=16,'yh'=2,'yl'=2,'c'=2,'x'=4] {'yl','x'}, dimensions={0} | all-to-all | bytes 1048576 | tf_op jit(solution)/shard_map/all_to_all | solution.py:229
  172.7 0.1 convert_reduce_fusion.1
  172.8 0.6 add_convert_fusion
  (3 shorter events, 0.1 us)
Async XLA Ops:
  8.3 11.1 %all-to-all-start = ((bf16[4,352,128]{2,1,0:T(8,128)(2,1)}), bf16[4,352,128]{2,1,0:T(8,128)(2,1)S(1)}, u32[]{:S(2)}, u32[]{:S(2)}) async-start(bf16[4,352,128]{2,1,0:T(8,128)(2,1)} %shard_map.100), calls=%async_computation | async-start | bytes 720896 | tf_op jit(solution)/shard_map/all_to_all | solution.py:180
  13.3 101.5 %all-gather.4.cloned.1.call-start = ((), (), s32[]{:S(2)}) async-start(), calls=%async_computation.6 | async-start | bytes 5406720 | tf_op jit(solution)/shard_map/all_gather | solution.py:187
  19.3 0.8 copy-start.1
  22.0 12.7 %collective-permute-start = (bf16[4,128,128]{2,1,0:T(8,128)(2,1)}, bf16[4,128,128]{2,1,0:T(8,128)(2,1)S(1)}, u32[]{:S(2)}, u32[]{:S(2)}) collective-permute-start(bf16[4,128,128]{2,1,0:T(8,128)(2,1)} %get-tuple-element.15.mine), channel_id=1, source_target_pairs={{0,4},{4,0},{1,5},{5,1},{2,6},{6,2},{3,7},{7,3},{8,12},{12,8},{9,1... | collective-permute-start | bytes 393224 | tf_op jit(solution)/shard_map/ppermute | solution.py:189
  34.7 41.2 %copy-start.3 = (bf16[4,128,128]{2,1,0:T(8,128)(2,1)}, bf16[4,128,128]{2,1,0:T(8,128)(2,1)S(1)}, u32[]{:S(2)}) copy-start(bf16[4,128,128]{2,1,0:T(8,128)(2,1)S(1)} %collective-permute-done.other) | copy-start | bytes 393220
  78.2 27.2 %all-to-all-start.2 = ((f32[16,40,128]{2,1,0:T(8,128)}), f32[16,40,128]{2,1,0:T(8,128)S(1)}, u32[]{:S(2)}, u32[]{:S(2)}) async-start(f32[16,40,128]{2,1,0:T(8,128)} %shard_map.103), calls=%async_computation.2 | async-start | bytes 655360 | tf_op jit(solution)/shard_map/all_to_all | solution.py:202
  105.4 0.7 copy-start.2
  117.9 23.1 %copy-start.4 = (bf16[64,512]{1,0:T(8,128)(2,1)S(1)}, bf16[64,512]{1,0:T(8,128)(2,1)}, u32[]{:S(2)}) copy-start(bf16[64,512]{1,0:T(8,128)(2,1)} %param.13) | copy-start | bytes 196612
  141.9 13.0 %all-to-all-start.4 = ((bf16[8,64,512]{2,1,0:T(8,128)(2,1)}), bf16[8,64,512]{2,1,0:T(8,128)(2,1)S(1)}, u32[]{:S(2)}, u32[]{:S(2)}) async-start(bf16[8,64,512]{2,1,0:T(8,128)(2,1)} %broadcast_in_dim.19), calls=%async_computation.4 | async-start | bytes 1048576 | tf_op jit(solution)/shard_map/all_to_all | solution.py:225
  154.9 0.8 copy-start
Sparse Core Ops, SparseCore 0:
  22.1 92.3 all-gather.3

commit v6 on v5

--- a/solution.py
+++ b/solution.py
@@ -15,6 +15,8 @@
 HI = lax.Precision.HIGHEST
 F32 = jnp.float32
 BF16 = jnp.bfloat16
+SMALL = 24 << 20
+LARGE = 60 << 20
 
 
 def dot(a, b, dims, precision=None):
@@ -23,17 +25,21 @@
     )
 
 
-def kernel_call(body, out_shape, n_in, scratch=(), cost=None):
+def kernel_call(body, out_shape, n_in, scratch=(), cost=None, core=None, grant=SMALL, n_far=0):
     whole = pl.BlockSpec(memory_space=pltpu.VMEM)
     many = isinstance(out_shape, (list, tuple))
-    return pl.pallas_call(
+    call = pl.pallas_call(
         body,
         out_shape=out_shape,
-        in_specs=[whole] * n_in,
+        in_specs=([] if core is None else [pl.BlockSpec(memory_space=pltpu.SMEM)])
+        + [whole] * n_in
+        + [pl.BlockSpec(memory_space=pltpu.HBM)] * n_far,
         out_specs=[whole] * len(out_shape) if many else whole,
         scratch_shapes=list(scratch),
         cost_estimate=cost,
-    )
+        compiler_params=pltpu.CompilerParams(vmem_limit_bytes=grant),
+    )
+    return call if core is None else lambda *args: call(core, *args)
 
 
 def shape(dims, dtype):
@@ -54,29 +60,31 @@
                 out[y, at : at + 16] = w[:, low : low + 128]
 
 
-def marks_body(got, starts, ends, sums, weights, kv):
-    weights[...] = got[:, 192:352]
-    kv[...] = got[:, 64:192]
-    at = lax.broadcasted_iota(jnp.int32, (64, 256), 1)
-    at = at + (at // 64) * 64
-    member = ((at >= starts[...]) & (at < ends[...])).astype(BF16)
-    for i in range(2):
-        part = got[:, 64 * i : 64 * i + 64].reshape(256, HEAD)
-        sums[i] = dot(member, part, ((1,), (0,)))
+def marks_body(core, mine, other, starts, ends, out):
+    c = core[0]
+    low = pl.multiple_of(c * 64, 64)
+    total = None
+    for got, place in ((mine, c), (other, 1 - c)):
+        at = lax.broadcasted_iota(jnp.int32, (64, 256), 1)
+        at = at + (at // 64) * 64 + place * 64
+        member = ((at >= starts[...]) & (at < ends[...])).astype(BF16)
+        part = dot(member, got[:, pl.ds(low, 64), :].reshape(256, HEAD), ((1,), (0,)))
+        total = part if total is None else total + part
+    out[...] = total
 
 
 def far_body(core, mine, other, marks, out):
     query = marks[0, pl.ds(core[0] * 32, 32), :]
     far = [
-        dot(query, kv[:, 0:64].reshape(256, HEAD).astype(F32), ((1,), (1,)), HI) * SCALE
-        for kv in (mine, other)
+        dot(query, got[:, 64:128].reshape(256, HEAD).astype(F32), ((1,), (1,)), HI) * SCALE
+        for got in (mine, other)
     ]
     peak = jnp.maximum(*(jnp.max(f, axis=-1, keepdims=True) for f in far))
     far = [jnp.exp(f - peak) for f in far]
     mass = sum(jnp.sum(f, axis=-1, keepdims=True) for f in far)
     part = sum(
-        dot(f, kv[:, 64:128].reshape(256, HEAD).astype(F32), ((1,), (0,)), HI)
-        for f, kv in zip(far, (mine, other))
+        dot(f, got[:, 128:192].reshape(256, HEAD).astype(F32), ((1,), (0,)), HI)
+        for f, got in zip(far, (mine, other))
     )
     row = lax.broadcasted_iota(jnp.int32, (32, HEAD), 0)
     lane = lax.broadcasted_iota(jnp.int32, (32, HEAD), 1)
@@ -141,21 +149,31 @@
                 ]
 
 
-def unmix_body(weights, w1, w2):
+def unmix_body(weights, w1, w2, raw, sem):
+    copy = pltpu.make_async_copy(weights.at[:, :, 16:160], raw, sem)
+    copy.start()
+    copy.wait()
     for t in range(6):
-        unmix(weights, 1 + t, w1, slice(t * 128, t * 128 + 128))
+        unmix(raw, t, w1, slice(t * 128, t * 128 + 128))
     for t in range(3):
-        unmix(weights, 7 + t, w2, slice(t * 128, t * 128 + 128))
-
-
-def proj_body(near, inverse, gathered, weights, out, wo):
-    unmix(weights, 0, wo, slice(0, 128))
+        unmix(raw, 6 + t, w2, slice(t * 128, t * 128 + 128))
+
+
+def proj_body(near, inverse, gathered, weights, out, raw, wo, sem):
+    copy = pltpu.make_async_copy(weights.at[:, :, 0:16], raw, sem)
+    copy.start()
     mixer = dot(inverse[...], gathered[...], ((1,), (0,)), HI)
     attn = dot(near[...], mixer, ((1,), (0,)), HI).astype(BF16)
+    copy.wait()
+    unmix(raw, 0, wo, slice(0, 128))
     spread(dot(attn, wo[...], ((1,), (1,))), out)
 
 
-def ffn_body(whole, gain, w1, w2, out, normed):
+def ffn_body(whole, gain, far1, far2, out, normed, w1, w2, sems):
+    first_copy = pltpu.make_async_copy(far1, w1, sems.at[0])
+    second_copy = pltpu.make_async_copy(far2, w2, sems.at[1])
+    first_copy.start()
+    second_copy.start()
     for y in range(2):
         blocks = [whole[y * 4 + x].astype(F32) for x in range(4)]
         square = sum(jnp.sum(b * b, axis=-1, keepdims=True) for b in blocks)
@@ -165,40 +183,30 @@
             normed[y * 64 : y * 64 + 64, lanes] = (
                 blocks[x] * factor * gain[:, lanes]
             ).astype(BF16)
+    first_copy.wait()
     first = dot(normed[...], w1[...], ((1,), (0,)))
     gate, up = first[:, :384], first[:, 384:]
     hidden = (gate / (1.0 + jnp.exp(-gate)) * up).astype(BF16)
+    second_copy.wait()
     spread(dot(hidden, w2[...], ((1,), (1,))), out)
 
 
 def on_device(queries, keys, values, stream, seg_lengths, gain, w_out, w_gate, w_up, w_down):
     z, c = lax.axis_index("z"), lax.axis_index("c")
     y_axes = ("yh", "yl")
-    pack = kernel_call(pack_body, shape((4, 352, 128), BF16), 7)(
+    pack = kernel_call(pack_body, shape((4, 352, 128), BF16), 7, grant=None)(
         queries, keys, values, w_gate, w_up, w_down.T, w_out.T
     )
     got = lax.all_to_all(pack, y_axes, 0, 0)
-    ends = jnp.cumsum(seg_lengths) - (z * 512 + c * 64)
-    sums, mine_w, kv = kernel_call(
-        marks_body,
-        [shape((2, 64, HEAD), F32), shape((4, 160, 128), BF16), shape((4, 128, 128), BF16)],
-        3,
-    )(got, (ends - seg_lengths)[:, None], ends[:, None])
-    weights = lax.all_gather(mine_w, ("z", "c"), axis=0)
-
-    other = lax.ppermute(kv, "c", [(0, 1), (1, 0)])
-    mine = lax.all_to_all(sums, "c", 0, 0)
-    mine, other = lax.optimization_barrier((mine, other))
-    mine = jnp.sum(mine, axis=0)
+    weights = lax.all_gather(got[:, 192:352], ("z", "c"), axis=0)
+    other = lax.ppermute(got, "c", [(0, 1), (1, 0)])
+    ends = jnp.cumsum(seg_lengths) - z * 512
+    mine = kernel_call(marks_body, shape((64, HEAD), F32), 4, core=c[None])(
+        got, other, (ends - seg_lengths)[:, None], ends[:, None]
+    )
     mine = jnp.sum(lax.all_gather(mine, "z", axis=0), axis=0)
     marks = lax.all_gather(mine / seg_lengths.astype(F32)[:, None], "c", axis=0)
-    block = pl.BlockSpec(memory_space=pltpu.VMEM)
-    send = pl.pallas_call(
-        far_body,
-        out_shape=shape((16, 40, HEAD), F32),
-        in_specs=[pl.BlockSpec(memory_space=pltpu.SMEM)] + [block] * 3,
-        out_specs=block,
-    )(c[None], kv, other, marks)
+    send = kernel_call(far_body, shape((16, 40, HEAD), F32), 3, core=c[None])(got, other, marks)
     parts = lax.all_to_all(send, "z", 0, 0)
     near, inverse = kernel_call(
         near_body,
@@ -209,22 +217,41 @@
     gathered = kernel_call(merge_body, shape((32, HEAD), F32), 1)(parts)
     gathered = lax.all_gather(gathered, "c", axis=0, tiled=True)
 
-    terms = pl.pallas_call(
+    terms = kernel_call(
         proj_body,
-        grid=(1,),
-        out_shape=shape((16, 64, 512), BF16),
-        in_specs=[block] * 3 + [pl.BlockSpec((32, 4, 16, 128), lambda i: (0, 0, 0, 0))],
-        out_specs=block,
-        scratch_shapes=[pltpu.VMEM((2048, 128), BF16)],
+        shape((16, 64, 512), BF16),
+        3,
+        [
+            pltpu.VMEM((32, 4, 16, 128), BF16),
+            pltpu.VMEM((2048, 128), BF16),
+            pltpu.SemaphoreType.DMA(()),
+        ],
+        n_far=1,
+        grant=LARGE,
     )(near, inverse, gathered, weights)
     parts = lax.all_to_all(terms, (*y_axes, "x"), 0, 0)
-    w1, w2 = kernel_call(unmix_body, [shape((2048, 768), BF16), shape((2048, 384), BF16)], 1)(
-        weights
-    )
+    w1, w2 = kernel_call(
+        unmix_body,
+        [shape((2048, 768), BF16), shape((2048, 384), BF16)],
+        0,
+        [pltpu.VMEM((32, 4, 144, 128), BF16), pltpu.SemaphoreType.DMA(())],
+        n_far=1,
+        grant=LARGE,
+    )(weights)
     resid = (stream.astype(F32) + jnp.sum(parts.astype(F32), axis=0)).astype(BF16)
     whole = lax.all_to_all(jnp.broadcast_to(resid[None], (8, 64, 512)), ("yl", "x"), 0, 0)
     terms = kernel_call(
-        ffn_body, shape((8, 64, 512), BF16), 4, [pltpu.VMEM((128, 2048), BF16)]
+        ffn_body,
+        shape((8, 64, 512), BF16),
+        2,
+        [
+            pltpu.VMEM((128, 2048), BF16),
+            pltpu.VMEM((2048, 768), BF16),
+            pltpu.VMEM((2048, 384), BF16),
+            pltpu.SemaphoreType.DMA((2,)),
+        ],
+        n_far=2,
+        grant=LARGE,
     )(whole, gain[None, :], w1, w2)
     parts = lax.all_to_all(terms, ("yl", "x"), 0, 0)
     return (resid.astype(F32) + jnp.sum(parts.astype(F32), axis=0)).astype(BF16)

time: 181 us -> 179 us (0.989)
  waiting for transfers between devices: 21.7 us -> 27.3 us
  Pallas kernels: 27.3 us -> 22 us
  starting transfers between devices: 23.2 us -> 18 us
  blocking collectives: 87.5 us -> 91.8 us
    all_gather x1, waiting for transfers between devices: 0.01 us -> 7.05 us  [on_device(): weights = lax.all_gather(got[:, 192:352], ('z', 'c'), axis=0)]
    all_to_all x1, blocking collectives: 4.37 us -> 11.1 us  [on_device(): got = lax.all_to_all(pack, y_axes, 0, 0)]
    all_to_all x1 -> x0, starting transfers between devices: 5.01 us -> none  [on_device(): got = lax.all_to_all(pack, y_axes, 0, 0)]
    all_to_all x1 -> x0, waiting for transfers between devices: 3.04 us -> none  [on_device(): got = lax.all_to_all(pack, y_axes, 0, 0)]
    all_gather x1, blocking collectives: 9.39 us -> 7.43 us  [on_device(): marks = lax.all_gather(mine / seg_lengths.astype(F32)[:, None], 'c', axis=0)]
    pallas_call x5, Pallas kernels: 13.8 us -> 11.9 us  [the longest x1 5.1 us: on_device(): kernel_call(ffn_body, shape((8, 64, 512), BF16), 2, [pltpu.VMEM((128, 204...]
  transfers between devices with their start and end apart: 5 -> 4, of which waited for: 3 -> 4; matrix products, arithmetic and copies ran while one was open for 2% -> 1% of each run, Pallas kernels for 9% -> 7%
where the time goes in v6:
time: 179 us; the launch traced here: 178 us
  blocking collectives  91.8 us (51%)
  waiting for transfers between devices  27.3 us (15%)
  Pallas kernels  22 us (12%)
  starting transfers between devices  18 us (10%)
  between operations  13.5 us (8%)
  local copies, waits for them, and re-layouts  3.82 us (2%)
  other arithmetic  1.94 us (1%)
    all_gather x1, blocking collectives, on_device(): mine = jnp.sum(lax.all_gather(mine, 'z', axis=0), axis=0)  31.3 us
    all_to_all x1, blocking collectives, on_device(): parts = lax.all_to_all(terms, (*y_axes, 'x'), 0, 0)  23.6 us
    all_to_all x1, waiting for transfers between devices, on_device(): parts = lax.all_to_all(send, 'z', 0, 0)  15.8 us
    all_to_all x1, blocking collectives, on_device(): parts = lax.all_to_all(terms, ('yl', 'x'), 0, 0)  12.3 us
    all_to_all x1, blocking collectives, on_device(): got = lax.all_to_all(pack, y_axes, 0, 0)  11.1 us
    ppermute x1, starting transfers between devices, on_device(): other = lax.ppermute(got, 'c', [(0, 1), (1, 0)])  8.34 us
    all_gather x1, blocking collectives, on_device(): marks = lax.all_gather(mine / seg_lengths.astype(F32)[:, None], 'c', axis=0)  7.43 us
    all_gather x1, waiting for transfers between devices, on_device(): weights = lax.all_gather(got[:, 192:352], ('z', 'c'), axis=0)  7.05 us
  transfers between devices with their start and end apart: 4, of which 4 were waited for; matrix products, arithmetic and copies ran while one was open for 1% of the time, Pallas kernels for 7%

profile of v6, /device:TPU:1, one launch (start us, length us, event | category | flops | bytes accessed | tf_op | source)
XLA Modules:
  0.0 178.3 jit_solution(7482270291614287795)
XLA Ops:
  6.5 0.0 all-gather.4.cloned.1.call-start
  6.5 1.7 shard_map.100
  8.3 11.1 %all_to_all.25.mine.got = bf16[4,352,128]{2,1,0:T(8,128)(2,1)S(1)} all-to-all(bf16[4,352,128]{2,1,0:T(8,128)(2,1)} %shard_map.100), channel_id=1, replica_groups=mesh['z'=16,'yh'=2,'yl'=2,'c'=2,'x'=4] {'yh','yl'}, dimensions={0} | all-to-all | bytes 720896 | tf_op jit(solution)/shard_map/all_to_all | solution.py:200
  19.3 0.7 slice.4
  20.0 0.0 all-gather.4.cloned.1.call-update
  20.0 0.7 copy.15
  20.8 0.1 reduce-window.4
  20.9 8.3 %collective-permute-start = (bf16[4,352,128]{2,1,0:T(8,128)(2,1)S(1)}, bf16[4,352,128]{2,1,0:T(8,128)(2,1)S(1)}, u32[]{:S(2)}, u32[]{:S(2)}) collective-permute-start(bf16[4,352,128]{2,1,0:T(8,128)(2,1)S(1)} %all_to_all.25.mine.got), channel_id=1, source_target_pairs={{0,4},{4,0},{1,5},{5,1},{2,6},{6,2},{3,7},{7,3},{8,12},{12,8},{9,1... | collective-permute-start | bytes 1081352 | tf_op jit(solution)/shard_map/ppermute | solution.py:202
  29.2 0.1 fusion
  29.3 0.7 fusion.1
  30.1 0.1 copy.16.starts
  30.2 0.3 collective-permute-done.other
  30.5 0.2 shard_map.101
  30.7 31.3 %all-gather = f32[1024,128]{1,0:T(8,128)S(1)} all-gather(f32[64,128]{1,0:T(8,128)S(1)} %shard_map.101), channel_id=2, replica_groups=mesh['z'=16,'yh'=2,'yl'=2,'c'=2,'x'=4] {'z'}, dimensions={0}, use_global_device_ids=true | all-gather | bytes 557056 | tf_op jit(solution)/shard_map/all_gather | solution.py:207
  62.0 0.1 bitcast_divide_fusion
  62.1 7.4 %all_gather.21.marks = f32[2,64,128]{2,1,0:T(8,128)S(1)} all-gather(f32[1,64,128]{2,1,0:T(8,128)S(1)} %bitcast_divide_fusion), channel_id=1, replica_groups=mesh['z'=16,'yh'=2,'yl'=2,'c'=2,'x'=4] {'c'}, dimensions={0}, use_global_device_ids=true | all-gather | bytes 98304 | tf_op jit(solution)/shard_map/all_gather | solution.py:208
  69.6 1.4 shard_map.103
  70.9 6.2 %all-to-all-start.1 = ((f32[16,40,128]{2,1,0:T(8,128)}), f32[16,40,128]{2,1,0:T(8,128)S(1)}, u32[]{:S(2)}, u32[]{:S(2)}) async-start(f32[16,40,128]{2,1,0:T(8,128)} %shard_map.103), calls=%async_computation.1 | async-start | bytes 655360 | tf_op jit(solution)/shard_map/all_to_all | solution.py:210
  77.1 4.5 %shard_map.102 = (f32[256,64]{1,0:T(8,128)S(1)}, f32[64,64]{1,0:T(8,128)S(1)}) custom-call(bf16[4,352,128]{2,1,0:T(8,128)(2,1)S(1)} %all_to_all.25.mine.got, f32[2,64,128]{2,1,0:T(8,128)S(1)} %all_gather.21.marks), custom_call_target="tpu_custom_call" | custom-call | flops 1000000000 | bytes 20000000 | tf_op jit(solution)/shard_map/pallas_call | solution.py:211
  81.6 0.0 copy-start
  81.6 0.6 copy-done
  82.3 0.0 copy-start.1
  82.3 15.8 %all-to-all-done.1.parts = f32[16,40,128]{2,1,0:T(8,128)S(1)} async-done(((f32[16,40,128]{2,1,0:T(8,128)}), f32[16,40,128]{2,1,0:T(8,128)S(1)}, u32[]{:S(2)}, u32[]{:S(2)}) %all-to-all-start.1) | async-done | bytes 327712 | tf_op jit(solution)/shard_map/all_to_all | solution.py:210
  98.0 0.2 shard_map.104
  98.3 6.1 %all_gather.22.gathered = f32[64,128]{1,0:T(8,128)} all-gather(f32[32,128]{1,0:T(8,128)S(1)} %shard_map.104), channel_id=1, replica_groups=mesh['z'=16,'yh'=2,'yl'=2,'c'=2,'x'=4] {'c'}, dimensions={0}, use_global_device_ids=true | all-gather | bytes 49152 | tf_op jit(solution)/shard_map/all_gather | solution.py:218
  104.3 7.0 %all-gather.4.cloned.1.call-done = bf16[128,160,128]{2,1,0:T(8,128)(2,1)} async-done(((bf16[4,160,128]{2,1,0:T(8,128)(2,1)}), bf16[128,160,128]{2,1,0:T(8,128)(2,1)}) %all-gather.4.cloned.1.call-update) | async-done | bytes 5242896 | tf_op jit(solution)/shard_map/all_gather | solution.py:201
  111.4 0.0 copy-done.1
  111.4 3.5 %shard_map.105 = bf16[16,64,512]{2,1,0:T(8,128)(2,1)} custom-call(f32[256,64]{1,0:T(8,128)} %copy-done, f32[64,64]{1,0:T(8,128)} %copy-done.1, f32[64,128]{1,0:T(8,128)} %all_gather.22.gathered, bf16[32,4,160,128]{3,2,1,0:T(8,128)(2,1)} %bitcast.11), custom_call_target="tpu_custom_call" | custom-call | tf_op jit(solution)/shard_map/pallas_call | solution.py:220
  114.9 0.0 copy-start.3
  114.9 23.6 %all_to_all.26 = bf16[16,64,512]{2,1,0:T(8,128)(2,1)S(1)} all-to-all(bf16[16,64,512]{2,1,0:T(8,128)(2,1)} %shard_map.105), channel_id=1, replica_groups=mesh['z'=16,'yh'=2,'yl'=2,'c'=2,'x'=4] {'yh','yl','x'}, dimensions={0} | all-to-all | bytes 2097152 | tf_op jit(solution)/shard_map/all_to_all | solution.py:232
  138.6 0.1 convert_reduce_fusion
  138.7 0.0 copy-done.3
  138.8 0.8 broadcast_in_dim.20
  139.6 3.5 %all-to-all-start.3 = ((bf16[8,64,512]{2,1,0:T(8,128)(2,1)}), bf16[8,64,512]{2,1,0:T(8,128)(2,1)S(1)}, u32[]{:S(2)}, u32[]{:S(2)}) async-start(bf16[8,64,512]{2,1,0:T(8,128)(2,1)} %broadcast_in_dim.20), calls=%async_computation.3 | async-start | bytes 1048576 | tf_op jit(solution)/shard_map/all_to_all | solution.py:242
  143.1 5.3 %shard_map.106 = (bf16[2048,768]{1,0:T(8,128)(2,1)}, bf16[2048,384]{1,0:T(8,128)(2,1)}) custom-call(bf16[32,4,160,128]{3,2,1,0:T(8,128)(2,1)} %bitcast.12), custom_call_target="tpu_custom_call" | custom-call | tf_op jit(solution)/shard_map/pallas_call | solution.py:233
  148.4 4.2 %all-to-all-done.3.whole = bf16[8,64,512]{2,1,0:T(8,128)(2,1)S(1)} async-done(((bf16[8,64,512]{2,1,0:T(8,128)(2,1)}), bf16[8,64,512]{2,1,0:T(8,128)(2,1)S(1)}, u32[]{:S(2)}, u32[]{:S(2)}) %all-to-all-start.3) | async-done | bytes 524320 | tf_op jit(solution)/shard_map/all_to_all | solution.py:242
  152.6 0.0 copy-start.2
  152.6 0.8 copy-done.2
  153.4 5.1 %shard_map.107 = bf16[8,64,512]{2,1,0:T(8,128)(2,1)} custom-call(bf16[8,64,512]{2,1,0:T(8,128)(2,1)} %copy-done.2, f32[1,2048]{1,0:T(1,128)} %bitcast.16, bf16[2048,768]{1,0:T(8,128)(2,1)} %get-tuple-element.11.far1, bf16[2048,384]{1,0:T(8,128)(2,1)} %get-tuple-element.12.far2), custom_call_target="tpu_custom_call" | custom-call | tf_op jit(solution)/shard_map/pallas_call | solution.py:243
  158.5 12.3 %all_to_all.27 = bf16[8,64,512]{2,1,0:T(8,128)(2,1)S(1)} all-to-all(bf16[8,64,512]{2,1,0:T(8,128)(2,1)} %shard_map.107), channel_id=1, replica_groups=mesh['z'=16,'yh'=2,'yl'=2,'c'=2,'x'=4] {'yl','x'}, dimensions={0} | all-to-all | bytes 1048576 | tf_op jit(solution)/shard_map/all_to_all | solution.py:256
  170.8 0.1 convert_reduce_fusion.1
  170.8 0.6 add_convert_fusion
  (2 shorter events, 0.0 us)
Async XLA Ops:
  6.5 104.9 %all-gather.4.cloned.1.call-start = ((), (), s32[]{:S(2)}) async-start(), calls=%async_computation.5 | async-start | bytes 5406720 | tf_op jit(solution)/shard_map/all_gather | solution.py:201
  20.9 9.6 %collective-permute-start = (bf16[4,352,128]{2,1,0:T(8,128)(2,1)S(1)}, bf16[4,352,128]{2,1,0:T(8,128)(2,1)S(1)}, u32[]{:S(2)}, u32[]{:S(2)}) collective-permute-start(bf16[4,352,128]{2,1,0:T(8,128)(2,1)S(1)} %all_to_all.25.mine.got), channel_id=1, source_target_pairs={{0,4},{4,0},{1,5},{5,1},{2,6},{6,2},{3,7},{7,3},{8,12},{12,8},{9,1... | collective-permute-start | bytes 1081352 | tf_op jit(solution)/shard_map/ppermute | solution.py:202
  70.9 27.1 %all-to-all-start.1 = ((f32[16,40,128]{2,1,0:T(8,128)}), f32[16,40,128]{2,1,0:T(8,128)S(1)}, u32[]{:S(2)}, u32[]{:S(2)}) async-start(f32[16,40,128]{2,1,0:T(8,128)} %shard_map.103), calls=%async_computation.1 | async-start | bytes 655360 | tf_op jit(solution)/shard_map/all_to_all | solution.py:210
  81.6 0.7 copy-start
  82.3 29.1 %copy-start.1 = (f32[64,64]{1,0:T(8,128)}, f32[64,64]{1,0:T(8,128)S(1)}, u32[]{:S(2)}) copy-start(f32[64,64]{1,0:T(8,128)S(1)} %get-tuple-element.10.inverse) | copy-start | bytes 49156
  114.9 23.8 %copy-start.3 = (bf16[64,512]{1,0:T(8,128)(2,1)S(1)}, bf16[64,512]{1,0:T(8,128)(2,1)}, u32[]{:S(2)}) copy-start(bf16[64,512]{1,0:T(8,128)(2,1)} %param.13) | copy-start | bytes 196612
  139.6 13.0 %all-to-all-start.3 = ((bf16[8,64,512]{2,1,0:T(8,128)(2,1)}), bf16[8,64,512]{2,1,0:T(8,128)(2,1)S(1)}, u32[]{:S(2)}, u32[]{:S(2)}) async-start(bf16[8,64,512]{2,1,0:T(8,128)(2,1)} %broadcast_in_dim.20), calls=%async_computation.3 | async-start | bytes 1048576 | tf_op jit(solution)/shard_map/all_to_all | solution.py:242
  152.6 0.8 copy-start.2
Sparse Core Ops, SparseCore 0:
  20.2 91.1 all-gather.3

commit v7 on v6

--- a/solution.py
+++ b/solution.py
@@ -52,11 +52,12 @@
         out[y, 0:64] = q[:, tile]
         out[y, 64:128] = k[:, tile]
         out[y, 128:192] = v[:, tile]
-        out[y, 192:208] = wo[:, tile]
+        for t in range(4):
+            out[y, 192 + t * 16 : 208 + t * 16] = wo[:, t * 128 : t * 128 + 128]
         for t in range(3):
             low = ((y % 2) * 3 + t) * 128
             for i, w in enumerate((wg, wu, wd)):
-                at = 208 + (3 * i + t) * 16
+                at = 256 + (3 * i + t) * 16
                 out[y, at : at + 16] = w[:, low : low + 128]
 
 
@@ -111,10 +112,9 @@
     return scores / jnp.sum(scores, axis=axis, keepdims=True)
 
 
-def near_body(got, marks, near, inverse):
+def inverse_body(marks, out):
     qm, km = marks[0], marks[1]
-    query = got[:, 0:64].reshape(256, HEAD).astype(F32)
-    near[...] = softmax(dot(query, km, ((1,), (1,)), HI) * SCALE, -1)
+    out[0] = km
     land = softmax(dot(qm, km, ((1,), (1,)), HI) * SCALE, 1)
     across = softmax(dot(km, qm, ((1,), (1,)), HI) * SCALE, 0)
     most = jnp.max(jnp.sum(land, axis=0, keepdims=True), axis=1, keepdims=True) * jnp.max(
@@ -130,7 +130,14 @@
         inner = 15.0 * eye - mul(prod, inner)
         inner = 13.0 * eye - mul(prod, inner)
         approx = 0.25 * mul(approx, inner)
-    inverse[...] = approx
+    out[1] = jnp.concatenate([approx, jnp.zeros_like(approx)], axis=-1)
+
+
+def near_body(queries, heads, out):
+    for h in range(4):
+        query = queries[:, h * HEAD : h * HEAD + HEAD].astype(F32)
+        near = softmax(dot(query, heads[h, 0], ((1,), (1,)), HI) * SCALE, -1)
+        out[h] = jnp.concatenate([near, jnp.zeros_like(near)], axis=-1)
 
 
 def spread(terms, out):
@@ -139,33 +146,44 @@
             out[y * 4 + x] = terms[y * 64 : y * 64 + 64, x * 512 : x * 512 + 512].astype(BF16)
 
 
-def unmix(weights, tile, dest, lanes):
+def unmix(blocks, tile, dest, lanes, c):
     for z in range(16):
-        for c in range(2):
-            for y in range(4):
-                low = (z * 8 + y * 2 + c) * 16
-                dest[low : low + 16, lanes] = weights[
-                    z * 2 + c, y, tile * 16 : tile * 16 + 16, :
-                ]
-
-
-def unmix_body(weights, w1, w2, raw, sem):
-    copy = pltpu.make_async_copy(weights.at[:, :, 16:160], raw, sem)
-    copy.start()
-    copy.wait()
-    for t in range(6):
-        unmix(raw, t, w1, slice(t * 128, t * 128 + 128))
-    for t in range(3):
-        unmix(raw, 6 + t, w2, slice(t * 128, t * 128 + 128))
-
-
-def proj_body(near, inverse, gathered, weights, out, raw, wo, sem):
-    copy = pltpu.make_async_copy(weights.at[:, :, 0:16], raw, sem)
-    copy.start()
-    mixer = dot(inverse[...], gathered[...], ((1,), (0,)), HI)
-    attn = dot(near[...], mixer, ((1,), (0,)), HI).astype(BF16)
-    copy.wait()
-    unmix(raw, 0, wo, slice(0, 128))
+        for y in range(4):
+            low = pl.multiple_of((z * 8 + y * 2 + c) * 16, 16)
+            dest[pl.ds(low, 16), lanes] = blocks[z, y, tile * 16 : tile * 16 + 16, :]
+
+
+def unmix_body(core, mine, other, w1, w2, raw, sems):
+    copies = [
+        pltpu.make_async_copy(far.at[:, :, 64:208], raw.at[i], sems.at[i])
+        for i, far in enumerate((mine, other))
+    ]
+    for copy in copies:
+        copy.start()
+    for i, c in enumerate((core[0], 1 - core[0])):
+        copies[i].wait()
+        for t in range(6):
+            unmix(raw.at[i], t, w1, slice(t * 128, t * 128 + 128), c)
+        for t in range(3):
+            unmix(raw.at[i], 6 + t, w2, slice(t * 128, t * 128 + 128), c)
+
+
+def proj_body(core, near, heads, gathered, mine, other, out, raw, wo, sems):
+    copies = [
+        pltpu.make_async_copy(far.at[:, :, 0:64], raw.at[i], sems.at[i])
+        for i, far in enumerate((mine, other))
+    ]
+    for copy in copies:
+        copy.start()
+    attn = []
+    for h in range(4):
+        mixer = dot(heads[h, 1][:, :64], gathered[h], ((1,), (0,)), HI)
+        attn.append(dot(near[h][:, :64], mixer, ((1,), (0,)), HI).astype(BF16))
+    attn = jnp.concatenate(attn, axis=-1)
+    for i, c in enumerate((core[0], 1 - core[0])):
+        copies[i].wait()
+        for t in range(4):
+            unmix(raw.at[i], t, wo, slice(t * 128, t * 128 + 128), c)
     spread(dot(attn, wo[...], ((1,), (1,))), out)
 
 
@@ -194,11 +212,11 @@
 def on_device(queries, keys, values, stream, seg_lengths, gain, w_out, w_gate, w_up, w_down):
     z, c = lax.axis_index("z"), lax.axis_index("c")
     y_axes = ("yh", "yl")
-    pack = kernel_call(pack_body, shape((4, 352, 128), BF16), 7, grant=None)(
+    pack = kernel_call(pack_body, shape((4, 400, 128), BF16), 7, grant=None)(
         queries, keys, values, w_gate, w_up, w_down.T, w_out.T
     )
     got = lax.all_to_all(pack, y_axes, 0, 0)
-    weights = lax.all_gather(got[:, 192:352], ("z", "c"), axis=0)
+    weights = lax.all_gather(got[:, 192:400], "z", axis=0)
     other = lax.ppermute(got, "c", [(0, 1), (1, 0)])
     ends = jnp.cumsum(seg_lengths) - z * 512
     mine = kernel_call(marks_body, shape((64, HEAD), F32), 4, core=c[None])(
@@ -208,36 +226,43 @@
     marks = lax.all_gather(mine / seg_lengths.astype(F32)[:, None], "c", axis=0)
     send = kernel_call(far_body, shape((16, 40, HEAD), F32), 3, core=c[None])(got, other, marks)
     parts = lax.all_to_all(send, "z", 0, 0)
-    near, inverse = kernel_call(
-        near_body,
-        [shape((256, 64), F32), shape((64, 64), F32)],
-        2,
+    heads = kernel_call(
+        inverse_body,
+        shape((2, 64, HEAD), F32),
+        1,
         cost=pl.CostEstimate(flops=10**9, bytes_accessed=2 * 10**7, transcendentals=0),
-    )(got, marks)
+    )(marks)
+    heads = lax.all_gather(heads, y_axes, axis=0)
+    near = kernel_call(near_body, shape((4, 64, HEAD), F32), 2)(queries, heads)
+    parts, near, heads = lax.optimization_barrier((parts, near, heads))
     gathered = kernel_call(merge_body, shape((32, HEAD), F32), 1)(parts)
     gathered = lax.all_gather(gathered, "c", axis=0, tiled=True)
-
+    gathered, weights = lax.optimization_barrier((gathered, weights))
+    swapped = lax.ppermute(weights, "c", [(0, 1), (1, 0)])
+    gathered = lax.all_gather(gathered, y_axes, axis=0)
     terms = kernel_call(
         proj_body,
-        shape((16, 64, 512), BF16),
+        shape((4, 64, 512), BF16),
         3,
         [
-            pltpu.VMEM((32, 4, 16, 128), BF16),
-            pltpu.VMEM((2048, 128), BF16),
-            pltpu.SemaphoreType.DMA(()),
+            pltpu.VMEM((2, 16, 4, 64, 128), BF16),
+            pltpu.VMEM((2048, 512), BF16),
+            pltpu.SemaphoreType.DMA((2,)),
         ],
-        n_far=1,
+        core=c[None],
+        n_far=2,
         grant=LARGE,
-    )(near, inverse, gathered, weights)
-    parts = lax.all_to_all(terms, (*y_axes, "x"), 0, 0)
+    )(near, heads, gathered, weights, swapped)
+    parts = lax.all_to_all(terms, "x", 0, 0)
     w1, w2 = kernel_call(
         unmix_body,
         [shape((2048, 768), BF16), shape((2048, 384), BF16)],
         0,
-        [pltpu.VMEM((32, 4, 144, 128), BF16), pltpu.SemaphoreType.DMA(())],
-        n_far=1,
+        [pltpu.VMEM((2, 16, 4, 144, 128), BF16), pltpu.SemaphoreType.DMA((2,))],
+        core=c[None],
+        n_far=2,
         grant=LARGE,
-    )(weights)
+    )(weights, swapped)
     resid = (stream.astype(F32) + jnp.sum(parts.astype(F32), axis=0)).astype(BF16)
     whole = lax.all_to_all(jnp.broadcast_to(resid[None], (8, 64, 512)), ("yl", "x"), 0, 0)
     terms = kernel_call(

time: 179 us -> 183 us (1.022)
  the two profiles are of different devices: /device:TPU:1 before, /device:TPU:16 now
where the time goes in v7:
time: 183 us; the launch traced here: 182 us
  blocking collectives  101 us (55%)
  Pallas kernels  23.2 us (13%)
  waiting for transfers between devices  23.1 us (13%)
  starting transfers between devices  16 us (9%)
  between operations  13.5 us (7%)
  local copies, waits for them, and re-layouts  3.83 us (2%)
  other arithmetic  1.83 us (1%)
    all_gather x1, blocking collectives, on_device(): mine = jnp.sum(lax.all_gather(mine, 'z', axis=0), axis=0)  37 us
    all_to_all x1, blocking collectives, on_device(): got = lax.all_to_all(pack, y_axes, 0, 0)  14.2 us
    all_to_all x1, blocking collectives, on_device(): parts = lax.all_to_all(terms, ('yl', 'x'), 0, 0)  12.1 us
    all_gather x1, blocking collectives, on_device(): heads = lax.all_gather(heads, y_axes, axis=0)  11.6 us
    all_gather x1, blocking collectives, on_device(): gathered = lax.all_gather(gathered, y_axes, axis=0)  11.5 us
    pallas_call x4, Pallas kernels, kernel_call(): return call if core is None else lambda *args: call(core, *args)  11.1 us
    all_gather x1, waiting for transfers between devices, on_device(): weights = lax.all_gather(got[:, 192:400], 'z', axis=0)  11 us
    all_to_all x1, blocking collectives, on_device(): parts = lax.all_to_all(terms, 'x', 0, 0)  10.7 us
  transfers between devices with their start and end apart: 5, of which 4 were waited for; matrix products, arithmetic and copies ran while one was open for 1% of the time, Pallas kernels for 7%

profile of v7, /device:TPU:16, one launch (start us, length us, event | category | flops | bytes accessed | tf_op | source)
XLA Modules:
  0.0 182.2 jit_solution(8980816391401869129)
XLA Ops:
  6.5 0.0 all-gather.6.cloned.1.call-start
  6.5 1.8 shard_map.100
  8.3 14.2 %all_to_all.25.mine = bf16[4,400,128]{2,1,0:T(8,128)(2,1)S(1)} all-to-all(bf16[4,400,128]{2,1,0:T(8,128)(2,1)} %shard_map.100), channel_id=1, replica_groups=mesh['z'=16,'yh'=2,'yl'=2,'c'=2,'x'=4] {'yh','yl'}, dimensions={0} | all-to-all | bytes 819200 | tf_op jit(solution)/shard_map/all_to_all | solution.py:218
  22.5 0.7 slice.4
  23.2 0.0 all-gather.6.cloned.1.call-update
  23.2 0.7 copy.15
  24.0 0.1 reduce-window.4
  24.1 1.9 %collective-permute-start = (bf16[4,400,128]{2,1,0:T(8,128)(2,1)S(1)}, bf16[4,400,128]{2,1,0:T(8,128)(2,1)S(1)}, u32[]{:S(2)}, u32[]{:S(2)}) collective-permute-start(bf16[4,400,128]{2,1,0:T(8,128)(2,1)S(1)} %all_to_all.25.mine), channel_id=1, source_target_pairs={{0,4},{4,0},{1,5},{5,1},{2,6},{6,2},{3,7},{7,3},{8,12},{12,8},{9,1... | collective-permute-start | bytes 1228808 | tf_op jit(solution)/shard_map/ppermute | solution.py:220
  26.0 0.1 fusion
  26.1 0.7 fusion.1
  26.8 0.1 copy.16.starts
  26.9 0.8 collective-permute-done.other
  27.7 0.2 shard_map.101
  27.9 37.0 %all-gather = f32[1024,128]{1,0:T(8,128)S(1)} all-gather(f32[64,128]{1,0:T(8,128)S(1)} %shard_map.101), channel_id=2, replica_groups=mesh['z'=16,'yh'=2,'yl'=2,'c'=2,'x'=4] {'z'}, dimensions={0}, use_global_device_ids=true | all-gather | bytes 557056 | tf_op jit(solution)/shard_map/all_gather | solution.py:225
  64.9 0.0 copy-start.2
  64.9 0.1 bitcast_divide_fusion
  65.0 1.9 %all_gather.33.marks = f32[2,64,128]{2,1,0:T(8,128)S(1)} all-gather(f32[1,64,128]{2,1,0:T(8,128)S(1)} %bitcast_divide_fusion), channel_id=1, replica_groups=mesh['z'=16,'yh'=2,'yl'=2,'c'=2,'x'=4] {'c'}, dimensions={0}, use_global_device_ids=true | all-gather | bytes 98304 | tf_op jit(solution)/shard_map/all_gather | solution.py:226
  66.9 1.4 shard_map.102
  68.3 7.4 %all-to-all-start.1 = ((f32[16,40,128]{2,1,0:T(8,128)}), f32[16,40,128]{2,1,0:T(8,128)S(1)}, u32[]{:S(2)}, u32[]{:S(2)}) async-start(f32[16,40,128]{2,1,0:T(8,128)} %shard_map.102), calls=%async_computation.1 | async-start | bytes 655360 | tf_op jit(solution)/shard_map/all_to_all | solution.py:228
  75.7 4.5 %shard_map.103 = f32[2,64,128]{2,1,0:T(8,128)S(1)} custom-call(f32[2,64,128]{2,1,0:T(8,128)S(1)} %all_gather.33.marks), custom_call_target="tpu_custom_call" | custom-call | flops 1000000000 | bytes 20000000 | tf_op jit(solution)/shard_map/pallas_call | solution.py:229
  80.2 11.6 %all-gather.1 = f32[8,64,128]{2,1,0:T(8,128)S(1)} all-gather(f32[2,64,128]{2,1,0:T(8,128)S(1)} %shard_map.103), channel_id=3, replica_groups=mesh['z'=16,'yh'=2,'yl'=2,'c'=2,'x'=4] {'yh','yl'}, dimensions={0}, use_global_device_ids=true | all-gather | bytes 327680 | tf_op jit(solution)/shard_map/all_gather | solution.py:235
  91.8 0.0 copy-start
  91.8 0.0 copy-done.2
  91.8 0.5 shard_map.104.near
  92.3 0.0 copy-start.1
  92.3 0.6 copy-done.1
  93.0 7.8 %all-to-all-done.1.parts = f32[16,40,128]{2,1,0:T(8,128)S(1)} async-done(((f32[16,40,128]{2,1,0:T(8,128)}), f32[16,40,128]{2,1,0:T(8,128)S(1)}, u32[]{:S(2)}, u32[]{:S(2)}) %all-to-all-start.1) | async-done | bytes 327712 | tf_op jit(solution)/shard_map/all_to_all | solution.py:228
  100.8 0.2 shard_map.105
  101.0 1.8 %all_gather.36 = f32[64,128]{1,0:T(8,128)S(1)} all-gather(f32[32,128]{1,0:T(8,128)S(1)} %shard_map.105), channel_id=1, replica_groups=mesh['z'=16,'yh'=2,'yl'=2,'c'=2,'x'=4] {'c'}, dimensions={0}, use_global_device_ids=true | all-gather | bytes 49152 | tf_op jit(solution)/shard_map/all_gather | solution.py:239
  102.8 11.0 %all-gather.6.cloned.1.call-done = bf16[64,208,128]{2,1,0:T(8,128)(2,1)} async-done(((bf16[4,208,128]{2,1,0:T(8,128)(2,1)}), bf16[64,208,128]{2,1,0:T(8,128)(2,1)}) %all-gather.6.cloned.1.call-update) | async-done | bytes 3407888 | tf_op jit(solution)/shard_map/all_gather | solution.py:219
  113.8 1.9 %collective-permute-start.1 = (bf16[16,4,208,128]{3,2,1,0:T(8,128)(2,1)}, bf16[16,4,208,128]{3,2,1,0:T(8,128)(2,1)}, u32[]{:S(2)}, u32[]{:S(2)}) collective-permute-start(bf16[16,4,208,128]{3,2,1,0:T(8,128)(2,1)} %bitcast.15), channel_id=1, source_target_pairs={{0,4},{4,0},{1,5},{5,1},{2,6},{6,2},{3,7},{7,3},{8,12},{12,8},{9,1... | collective-permute-start | bytes 10223624 | tf_op jit(solution)/shard_map/ppermute | solution.py:241
  115.7 11.5 %all-gather.3 = f32[256,128]{1,0:T(8,128)} all-gather(f32[64,128]{1,0:T(8,128)S(1)} %all_gather.36), channel_id=5, replica_groups=mesh['z'=16,'yh'=2,'yl'=2,'c'=2,'x'=4] {'yh','yl'}, dimensions={0}, use_global_device_ids=true | all-gather | bytes 163840 | tf_op jit(solution)/shard_map/all_gather | solution.py:242
  127.2 0.0 collective-permute-done.1.other
  127.2 0.0 copy-done
  127.2 0.0 copy-start.4
  127.2 4.4 %shard_map.106 = bf16[4,64,512]{2,1,0:T(8,128)(2,1)} custom-call(s32[1]{0:T(128)} %bitcast.core, f32[4,64,128]{2,1,0:T(8,128)} %copy-done.1, f32[4,2,64,128]{3,2,1,0:T(8,128)} %bitcast.14, f32[4,64,128]{2,1,0:T(8,128)} %bitcast.19, bf16[16,4,208,128]{3,2,1,0:T(8,128)(2,1)} %bitcast.16, bf16[16,4,208,128]{3,2,1,0:T(8,128)(2,1)} %collective-permute-done.1.other), custom_call_target="tpu_custom_call" | custom-call | tf_op jit(solution)/shard_map/pallas_call | solution.py:42
  131.6 10.7 %all_to_all.26 = bf16[4,64,512]{2,1,0:T(8,128)(2,1)S(1)} all-to-all(bf16[4,64,512]{2,1,0:T(8,128)(2,1)} %shard_map.106), channel_id=1, replica_groups=mesh['z'=16,'yh'=2,'yl'=2,'c'=2,'x'=4] {'x'}, dimensions={0} | all-to-all | bytes 524288 | tf_op jit(solution)/shard_map/all_to_all | solution.py:256
  142.3 0.0 copy-done.4
  142.4 0.8 broadcast_in_dim.10
  143.2 4.8 %all-to-all-start.3 = ((bf16[8,64,512]{2,1,0:T(8,128)(2,1)}), bf16[8,64,512]{2,1,0:T(8,128)(2,1)S(1)}, u32[]{:S(2)}, u32[]{:S(2)}) async-start(bf16[8,64,512]{2,1,0:T(8,128)(2,1)} %broadcast_in_dim.10), calls=%async_computation.3 | async-start | bytes 1048576 | tf_op jit(solution)/shard_map/all_to_all | solution.py:267
  148.0 5.1 %shard_map.107 = (bf16[2048,768]{1,0:T(8,128)(2,1)}, bf16[2048,384]{1,0:T(8,128)(2,1)}) custom-call(s32[1]{0:T(128)} %bitcast.core, bf16[16,4,208,128]{3,2,1,0:T(8,128)(2,1)} %bitcast.17, bf16[16,4,208,128]{3,2,1,0:T(8,128)(2,1)} %collective-permute-done.1.other), custom_call_target="tpu_custom_call" | custom-call | tf_op jit(solution)/shard_map/pallas_call | solution.py:42
  153.1 3.6 %all-to-all-done.3.whole = bf16[8,64,512]{2,1,0:T(8,128)(2,1)S(1)} async-done(((bf16[8,64,512]{2,1,0:T(8,128)(2,1)}), bf16[8,64,512]{2,1,0:T(8,128)(2,1)S(1)}, u32[]{:S(2)}, u32[]{:S(2)}) %all-to-all-start.3) | async-done | bytes 524320 | tf_op jit(solution)/shard_map/all_to_all | solution.py:267
  156.7 0.0 copy-start.3
  156.7 0.8 copy-done.3
  157.4 5.1 %shard_map.108 = bf16[8,64,512]{2,1,0:T(8,128)(2,1)} custom-call(bf16[8,64,512]{2,1,0:T(8,128)(2,1)} %copy-done.3, f32[1,2048]{1,0:T(1,128)} %bitcast.22, bf16[2048,768]{1,0:T(8,128)(2,1)} %get-tuple-element.17.far1, bf16[2048,384]{1,0:T(8,128)(2,1)} %get-tuple-element.18.far2), custom_call_target="tpu_custom_call" | custom-call | tf_op jit(solution)/shard_map/pallas_call | solution.py:268
  162.6 12.1 %all_to_all.27 = bf16[8,64,512]{2,1,0:T(8,128)(2,1)S(1)} all-to-all(bf16[8,64,512]{2,1,0:T(8,128)(2,1)} %shard_map.108), channel_id=1, replica_groups=mesh['z'=16,'yh'=2,'yl'=2,'c'=2,'x'=4] {'yl','x'}, dimensions={0} | all-to-all | bytes 1048576 | tf_op jit(solution)/shard_map/all_to_all | solution.py:281
  174.7 0.1 convert_reduce_fusion
  174.7 0.6 add_convert_fusion
  (3 shorter events, 0.1 us)
Async XLA Ops:
  6.5 107.2 %all-gather.6.cloned.1.call-start = ((), (), s32[]{:S(2)}) async-start(), calls=%async_computation.5 | async-start | bytes 3620864 | tf_op jit(solution)/shard_map/all_gather | solution.py:219
  24.1 3.6 %collective-permute-start = (bf16[4,400,128]{2,1,0:T(8,128)(2,1)S(1)}, bf16[4,400,128]{2,1,0:T(8,128)(2,1)S(1)}, u32[]{:S(2)}, u32[]{:S(2)}) collective-permute-start(bf16[4,400,128]{2,1,0:T(8,128)(2,1)S(1)} %all_to_all.25.mine), channel_id=1, source_target_pairs={{0,4},{4,0},{1,5},{5,1},{2,6},{6,2},{3,7},{7,3},{8,12},{12,8},{9,1... | collective-permute-start | bytes 1228808 | tf_op jit(solution)/shard_map/ppermute | solution.py:220
  64.9 26.9 %copy-start.2 = (bf16[64,512]{1,0:T(8,128)(2,1)S(1)}, bf16[64,512]{1,0:T(8,128)(2,1)}, u32[]{:S(2)}) copy-start(bf16[64,512]{1,0:T(8,128)(2,1)} %queries.1) | copy-start | bytes 196612
  68.3 32.5 %all-to-all-start.1 = ((f32[16,40,128]{2,1,0:T(8,128)}), f32[16,40,128]{2,1,0:T(8,128)S(1)}, u32[]{:S(2)}, u32[]{:S(2)}) async-start(f32[16,40,128]{2,1,0:T(8,128)} %shard_map.102), calls=%async_computation.1 | async-start | bytes 655360 | tf_op jit(solution)/shard_map/all_to_all | solution.py:228
  91.8 35.4 %copy-start = (f32[8,64,128]{2,1,0:T(8,128)}, f32[8,64,128]{2,1,0:T(8,128)S(1)}, u32[]{:S(2)}) copy-start(f32[8,64,128]{2,1,0:T(8,128)S(1)} %all-gather.1) | copy-start | bytes 786436
  92.3 0.7 copy-start.1
  113.8 13.4 %collective-permute-start.1 = (bf16[16,4,208,128]{3,2,1,0:T(8,128)(2,1)}, bf16[16,4,208,128]{3,2,1,0:T(8,128)(2,1)}, u32[]{:S(2)}, u32[]{:S(2)}) collective-permute-start(bf16[16,4,208,128]{3,2,1,0:T(8,128)(2,1)} %bitcast.15), channel_id=1, source_target_pairs={{0,4},{4,0},{1,5},{5,1},{2,6},{6,2},{3,7},{7,3},{8,12},{12,8},{9,1... | collective-permute-start | bytes 10223624 | tf_op jit(solution)/shard_map/ppermute | solution.py:241
  127.2 15.1 %copy-start.4 = (bf16[64,512]{1,0:T(8,128)(2,1)S(1)}, bf16[64,512]{1,0:T(8,128)(2,1)}, u32[]{:S(2)}) copy-start(bf16[64,512]{1,0:T(8,128)(2,1)} %param.13) | copy-start | bytes 196612
  143.2 13.5 %all-to-all-start.3 = ((bf16[8,64,512]{2,1,0:T(8,128)(2,1)}), bf16[8,64,512]{2,1,0:T(8,128)(2,1)S(1)}, u32[]{:S(2)}, u32[]{:S(2)}) async-start(bf16[8,64,512]{2,1,0:T(8,128)(2,1)} %broadcast_in_dim.10), calls=%async_computation.3 | async-start | bytes 1048576 | tf_op jit(solution)/shard_map/all_to_all | solution.py:267
  156.7 0.8 copy-start.3
Sparse Core Ops, SparseCore 0:
  23.3 90.3 all-gather.5

commit v8 on v7

--- a/solution.py
+++ b/solution.py
@@ -104,7 +104,9 @@
     mass = jnp.sum(jnp.where(lane == row + 32, stats, 0.0), axis=-1, keepdims=True)
     factor = jnp.exp(peak - jnp.max(peak, axis=0, keepdims=True))
     total = jnp.sum(factor * mass, axis=0)
-    out[...] = jnp.sum(factor * parts[:, 0:32, :], axis=0) / total
+    rows = jnp.sum(factor * parts[:, 0:32, :], axis=0) / total
+    for i in range(8):
+        out[i] = rows
 
 
 def softmax(scores, axis):
@@ -168,22 +170,17 @@
             unmix(raw.at[i], 6 + t, w2, slice(t * 128, t * 128 + 128), c)
 
 
-def proj_body(core, near, heads, gathered, mine, other, out, raw, wo, sems):
-    copies = [
-        pltpu.make_async_copy(far.at[:, :, 0:64], raw.at[i], sems.at[i])
-        for i, far in enumerate((mine, other))
-    ]
-    for copy in copies:
-        copy.start()
+def proj_body(core, near, heads, gathered, mine, other, out, wo):
+    for t in range(4):
+        lanes = slice(t * 128, t * 128 + 128)
+        unmix(mine, t, wo, lanes, core[0])
+        unmix(other, t, wo, lanes, 1 - core[0])
     attn = []
     for h in range(4):
-        mixer = dot(heads[h, 1][:, :64], gathered[h], ((1,), (0,)), HI)
+        rows = jnp.concatenate([gathered[2 * h], gathered[2 * h + 1]], axis=0)
+        mixer = dot(heads[h, 1][:, :64], rows, ((1,), (0,)), HI)
         attn.append(dot(near[h][:, :64], mixer, ((1,), (0,)), HI).astype(BF16))
     attn = jnp.concatenate(attn, axis=-1)
-    for i, c in enumerate((core[0], 1 - core[0])):
-        copies[i].wait()
-        for t in range(4):
-            unmix(raw.at[i], t, wo, slice(t * 128, t * 128 + 128), c)
     spread(dot(attn, wo[...], ((1,), (1,))), out)
 
 
@@ -235,24 +232,20 @@
     heads = lax.all_gather(heads, y_axes, axis=0)
     near = kernel_call(near_body, shape((4, 64, HEAD), F32), 2)(queries, heads)
     parts, near, heads = lax.optimization_barrier((parts, near, heads))
-    gathered = kernel_call(merge_body, shape((32, HEAD), F32), 1)(parts)
-    gathered = lax.all_gather(gathered, "c", axis=0, tiled=True)
-    gathered, weights = lax.optimization_barrier((gathered, weights))
-    swapped = lax.ppermute(weights, "c", [(0, 1), (1, 0)])
-    gathered = lax.all_gather(gathered, y_axes, axis=0)
+    gathered = kernel_call(merge_body, shape((8, 32, HEAD), F32), 1)(parts)
+    gathered = lax.all_to_all(gathered, (*y_axes, "c"), 0, 0)
+    weights, gathered = lax.optimization_barrier((weights, gathered))
+    w_out = weights[:, :, 0:64]
+    swapped = lax.ppermute(w_out, "c", [(0, 1), (1, 0)])
     terms = kernel_call(
         proj_body,
         shape((4, 64, 512), BF16),
-        3,
-        [
-            pltpu.VMEM((2, 16, 4, 64, 128), BF16),
-            pltpu.VMEM((2048, 512), BF16),
-            pltpu.SemaphoreType.DMA((2,)),
-        ],
+        5,
+        [pltpu.VMEM((2048, 512), BF16)],
         core=c[None],
-        n_far=2,
-        grant=LARGE,
-    )(near, heads, gathered, weights, swapped)
+    )(near, heads, gathered, w_out, swapped)
+    terms, weights = lax.optimization_barrier((terms, weights))
+    swapped = lax.ppermute(weights, "c", [(0, 1), (1, 0)])
     parts = lax.all_to_all(terms, "x", 0, 0)
     w1, w2 = kernel_call(
         unmix_body,

time: 183 us -> 176 us (0.962)
  the two profiles are of different devices: /device:TPU:16 before, /device:TPU:1 now
where the time goes in v8:
time: 176 us; the launch traced here: 175 us
  blocking collectives  97.3 us (55%)
  starting transfers between devices  25.7 us (15%)
  Pallas kernels  20.1 us (11%)
  between operations  13.6 us (8%)
  waiting for transfers between devices  10.6 us (6%)
  local copies, waits for them, and re-layouts  5.49 us (3%)
  other arithmetic  1.83 us (1%)
    all_gather x1, blocking collectives, on_device(): mine = jnp.sum(lax.all_gather(mine, 'z', axis=0), axis=0)  31.2 us
    all_to_all x1, blocking collectives, on_device(): gathered = lax.all_to_all(gathered, (*y_axes, 'c'), 0, 0)  13.9 us
    all_to_all x1, blocking collectives, on_device(): parts = lax.all_to_all(terms, ('yl', 'x'), 0, 0)  12.6 us
    all_to_all x1, blocking collectives, on_device(): got = lax.all_to_all(pack, y_axes, 0, 0)  11.3 us
    all_gather x1, blocking collectives, on_device(): heads = lax.all_gather(heads, y_axes, axis=0)  10.6 us
    all_to_all x1, blocking collectives, on_device(): parts = lax.all_to_all(terms, 'x', 0, 0)  10 us
    ppermute x1, starting transfers between devices, on_device(): other = lax.ppermute(got, 'c', [(0, 1), (1, 0)])  8.34 us
    pallas_call x4, Pallas kernels, kernel_call(): return call if core is None else lambda *args: call(core, *args)  7.96 us
  transfers between devices with their start and end apart: 6, of which 4 were waited for; matrix products, arithmetic and copies ran while one was open for 2% of the time, Pallas kernels for 7%

profile of v8, /device:TPU:1, one launch (start us, length us, event | category | flops | bytes accessed | tf_op | source)
XLA Modules:
  0.0 174.6 jit_solution(1310755187731416362)
XLA Ops:
  6.5 0.0 all-gather.5.cloned.1.call-start
  6.5 1.8 %shard_map.100 = bf16[4,400,128]{2,1,0:T(8,128)(2,1)} custom-call(bf16[64,512]{1,0:T(8,128)(2,1)} %queries.1, bf16[64,512]{1,0:T(8,128)(2,1)} %k.1, bf16[64,512]{1,0:T(8,128)(2,1)} %v.1, bf16[16,768]{1,0:T(8,128)(2,1)} %wg.1, bf16[16,768]{1,0:T(8,128)(2,1)} %wu.1, bf16[16,768]{1,0:T(8,128)(2,1)} %bitcast.15, bf16[16,512]{1,0:T(8,128)(2,1)} %bitcast.16), custom_call_target="tpu_custom_call" | custom-call | tf_op jit(solution)/shard_map/pallas_call | solution.py:212
  8.3 11.3 %all_to_all.30.mine = bf16[4,400,128]{2,1,0:T(8,128)(2,1)S(1)} all-to-all(bf16[4,400,128]{2,1,0:T(8,128)(2,1)} %shard_map.100), channel_id=1, replica_groups=mesh['z'=16,'yh'=2,'yl'=2,'c'=2,'x'=4] {'yh','yl'}, dimensions={0} | all-to-all | bytes 819200 | tf_op jit(solution)/shard_map/all_to_all | solution.py:215
  19.6 0.7 slice.8
  20.3 0.0 all-gather.5.cloned.1.call-update
  20.4 0.7 copy.15
  21.1 0.1 reduce-window.4
  21.2 8.3 %collective-permute-start = (bf16[4,400,128]{2,1,0:T(8,128)(2,1)S(1)}, bf16[4,400,128]{2,1,0:T(8,128)(2,1)S(1)}, u32[]{:S(2)}, u32[]{:S(2)}) collective-permute-start(bf16[4,400,128]{2,1,0:T(8,128)(2,1)S(1)} %all_to_all.30.mine), channel_id=1, source_target_pairs={{0,4},{4,0},{1,5},{5,1},{2,6},{6,2},{3,7},{7,3},{8,12},{12,8},{9,1... | collective-permute-start | bytes 1228808 | tf_op jit(solution)/shard_map/ppermute | solution.py:217
  29.6 0.1 fusion
  29.7 0.7 fusion.1
  30.4 0.1 copy.16.starts
  30.5 0.4 collective-permute-done.other
  30.9 0.2 shard_map.101
  31.1 31.2 %all-gather = f32[1024,128]{1,0:T(8,128)S(1)} all-gather(f32[64,128]{1,0:T(8,128)S(1)} %shard_map.101), channel_id=2, replica_groups=mesh['z'=16,'yh'=2,'yl'=2,'c'=2,'x'=4] {'z'}, dimensions={0}, use_global_device_ids=true | all-gather | bytes 557056 | tf_op jit(solution)/shard_map/all_gather | solution.py:222
  62.3 0.0 copy-start
  62.4 0.1 bitcast_divide_fusion
  62.5 7.6 %all_gather.24.marks = f32[2,64,128]{2,1,0:T(8,128)S(1)} all-gather(f32[1,64,128]{2,1,0:T(8,128)S(1)} %bitcast_divide_fusion), channel_id=1, replica_groups=mesh['z'=16,'yh'=2,'yl'=2,'c'=2,'x'=4] {'c'}, dimensions={0}, use_global_device_ids=true | all-gather | bytes 98304 | tf_op jit(solution)/shard_map/all_gather | solution.py:223
  70.1 1.4 shard_map.102
  71.5 6.1 %all-to-all-start.1 = ((f32[16,40,128]{2,1,0:T(8,128)}), f32[16,40,128]{2,1,0:T(8,128)S(1)}, u32[]{:S(2)}, u32[]{:S(2)}) async-start(f32[16,40,128]{2,1,0:T(8,128)} %shard_map.102), calls=%async_computation.1 | async-start | bytes 655360 | tf_op jit(solution)/shard_map/all_to_all | solution.py:225
  77.6 4.5 %shard_map.103 = f32[2,64,128]{2,1,0:T(8,128)S(1)} custom-call(f32[2,64,128]{2,1,0:T(8,128)S(1)} %all_gather.24.marks), custom_call_target="tpu_custom_call" | custom-call | flops 1000000000 | bytes 20000000 | tf_op jit(solution)/shard_map/pallas_call | solution.py:226
  82.2 10.6 %all-gather.1 = f32[8,64,128]{2,1,0:T(8,128)S(1)} all-gather(f32[2,64,128]{2,1,0:T(8,128)S(1)} %shard_map.103), channel_id=3, replica_groups=mesh['z'=16,'yh'=2,'yl'=2,'c'=2,'x'=4] {'yh','yl'}, dimensions={0}, use_global_device_ids=true | all-gather | bytes 327680 | tf_op jit(solution)/shard_map/all_gather | solution.py:232
  92.7 0.0 copy-done
  92.7 0.5 shard_map.104.near
  93.2 0.0 copy-start.2
  93.2 4.6 %all-to-all-done.1.parts = f32[16,40,128]{2,1,0:T(8,128)S(1)} async-done(((f32[16,40,128]{2,1,0:T(8,128)}), f32[16,40,128]{2,1,0:T(8,128)S(1)}, u32[]{:S(2)}, u32[]{:S(2)}) %all-to-all-start.1) | async-done | bytes 327712 | tf_op jit(solution)/shard_map/all_to_all | solution.py:225
  97.9 0.2 shard_map.105
  98.1 13.9 %all_to_all.31.gathered = f32[8,32,128]{2,1,0:T(8,128)S(1)} all-to-all(f32[8,32,128]{2,1,0:T(8,128)S(1)} %shard_map.105), channel_id=1, replica_groups=mesh['z'=16,'yh'=2,'yl'=2,'c'=2,'x'=4] {'yh','yl','c'}, dimensions={0} | all-to-all | bytes 262144 | tf_op jit(solution)/shard_map/all_to_all | solution.py:236
  112.0 0.0 all-gather.5.cloned.1.call-done
  112.0 1.3 slice.7.mine
  113.4 4.8 %collective-permute-start.1 = (bf16[16,4,64,128]{3,2,1,0:T(8,128)(2,1)S(1)}, bf16[16,4,64,128]{3,2,1,0:T(8,128)(2,1)S(1)}, u32[]{:S(2)}, u32[]{:S(2)}) collective-permute-start(bf16[16,4,64,128]{3,2,1,0:T(8,128)(2,1)S(1)} %slice.7.mine), channel_id=1, source_target_pairs={{0,4},{4,0},{1,5},{5,1},{2,6},{6,2},{3,7},{7,3},{8,12},{12,8},{9,1... | collective-permute-start | bytes 3145736 | tf_op jit(solution)/shard_map/ppermute | solution.py:239
  118.2 2.3 %collective-permute-done.1.other = bf16[16,4,64,128]{3,2,1,0:T(8,128)(2,1)S(1)} collective-permute-done((bf16[16,4,64,128]{3,2,1,0:T(8,128)(2,1)S(1)}, bf16[16,4,64,128]{3,2,1,0:T(8,128)(2,1)S(1)}, u32[]{:S(2)}, u32[]{:S(2)}) %collective-permute-start.1) | collective-permute-done | bytes 1048608 | tf_op jit(solution)/shard_map/ppermute | solution.py:239
  120.4 1.3 shard_map.106
  121.7 2.3 %collective-permute-start.2 = (bf16[16,4,208,128]{3,2,1,0:T(8,128)(2,1)}, bf16[16,4,208,128]{3,2,1,0:T(8,128)(2,1)S(1)}, u32[]{:S(2)}, u32[]{:S(2)}) collective-permute-start(bf16[16,4,208,128]{3,2,1,0:T(8,128)(2,1)} %bitcast.8.mine), channel_id=1, source_target_pairs={{0,4},{4,0},{1,5},{5,1},{2,6},{6,2},{3,7},{7,3},{8,12},{12,8},{9,1... | collective-permute-start | bytes 10223624 | tf_op jit(solution)/shard_map/ppermute | solution.py:248
  124.0 10.0 %all_to_all.32 = bf16[4,64,512]{2,1,0:T(8,128)(2,1)S(1)} all-to-all(bf16[4,64,512]{2,1,0:T(8,128)(2,1)S(1)} %shard_map.106), channel_id=1, replica_groups=mesh['z'=16,'yh'=2,'yl'=2,'c'=2,'x'=4] {'x'}, dimensions={0} | all-to-all | bytes 524288 | tf_op jit(solution)/shard_map/all_to_all | solution.py:249
  134.1 0.0 copy-done.2
  134.1 0.8 broadcast_in_dim.10
  135.0 4.1 %all-to-all-start.4 = ((bf16[8,64,512]{2,1,0:T(8,128)(2,1)}), bf16[8,64,512]{2,1,0:T(8,128)(2,1)}, u32[]{:S(2)}, u32[]{:S(2)}) async-start(bf16[8,64,512]{2,1,0:T(8,128)(2,1)} %broadcast_in_dim.10), calls=%async_computation.4 | async-start | bytes 1048576 | tf_op jit(solution)/shard_map/all_to_all | solution.py:260
  139.1 0.0 collective-permute-done.2.other
  139.1 0.0 copy-start.1
  139.1 1.8 %copy-done.1 = bf16[16,4,208,128]{3,2,1,0:T(8,128)(2,1)} copy-done((bf16[16,4,208,128]{3,2,1,0:T(8,128)(2,1)}, bf16[16,4,208,128]{3,2,1,0:T(8,128)(2,1)S(1)}, u32[]{:S(2)}) %copy-start.1) | copy-done | bytes 3407896
  140.9 5.1 %shard_map.107 = (bf16[2048,768]{1,0:T(8,128)(2,1)}, bf16[2048,384]{1,0:T(8,128)(2,1)}) custom-call(s32[1]{0:T(128)} %bitcast.core, bf16[16,4,208,128]{3,2,1,0:T(8,128)(2,1)} %bitcast.8.mine, bf16[16,4,208,128]{3,2,1,0:T(8,128)(2,1)} %copy-done.1), custom_call_target="tpu_custom_call" | custom-call | tf_op jit(solution)/shard_map/pallas_call | solution.py:42
  146.0 3.3 %all-to-all-done.4.whole = bf16[8,64,512]{2,1,0:T(8,128)(2,1)} async-done(((bf16[8,64,512]{2,1,0:T(8,128)(2,1)}), bf16[8,64,512]{2,1,0:T(8,128)(2,1)}, u32[]{:S(2)}, u32[]{:S(2)}) %all-to-all-start.4) | async-done | bytes 524320 | tf_op jit(solution)/shard_map/all_to_all | solution.py:260
  149.3 5.1 %shard_map.108 = bf16[8,64,512]{2,1,0:T(8,128)(2,1)} custom-call(bf16[8,64,512]{2,1,0:T(8,128)(2,1)} %all-to-all-done.4.whole, f32[1,2048]{1,0:T(1,128)} %bitcast.17, bf16[2048,768]{1,0:T(8,128)(2,1)} %get-tuple-element.21.far1, bf16[2048,384]{1,0:T(8,128)(2,1)} %get-tuple-element.22.far2), custom_call_target="tpu_custom_call" | custom-call | tf_op jit(solution)/shard_map/pallas_call | solution.py:261
  154.4 12.6 %all_to_all.33 = bf16[8,64,512]{2,1,0:T(8,128)(2,1)S(1)} all-to-all(bf16[8,64,512]{2,1,0:T(8,128)(2,1)} %shard_map.108), channel_id=1, replica_groups=mesh['z'=16,'yh'=2,'yl'=2,'c'=2,'x'=4] {'yl','x'}, dimensions={0} | all-to-all | bytes 1048576 | tf_op jit(solution)/shard_map/all_to_all | solution.py:274
  167.0 0.1 convert_reduce_fusion
  167.1 0.6 add_convert_fusion
  (3 shorter events, 0.1 us)
Async XLA Ops:
  6.5 105.5 %all-gather.5.cloned.1.call-start = ((), (), s32[]{:S(2)}) async-start(), calls=%async_computation.6 | async-start | bytes 3620864 | tf_op jit(solution)/shard_map/all_gather | solution.py:216
  21.2 9.7 %collective-permute-start = (bf16[4,400,128]{2,1,0:T(8,128)(2,1)S(1)}, bf16[4,400,128]{2,1,0:T(8,128)(2,1)S(1)}, u32[]{:S(2)}, u32[]{:S(2)}) collective-permute-start(bf16[4,400,128]{2,1,0:T(8,128)(2,1)S(1)} %all_to_all.30.mine), channel_id=1, source_target_pairs={{0,4},{4,0},{1,5},{5,1},{2,6},{6,2},{3,7},{7,3},{8,12},{12,8},{9,1... | collective-permute-start | bytes 1228808 | tf_op jit(solution)/shard_map/ppermute | solution.py:217
  62.3 30.4 %copy-start = (bf16[64,512]{1,0:T(8,128)(2,1)S(1)}, bf16[64,512]{1,0:T(8,128)(2,1)}, u32[]{:S(2)}) copy-start(bf16[64,512]{1,0:T(8,128)(2,1)} %queries.1) | copy-start | bytes 196612
  71.5 26.4 %all-to-all-start.1 = ((f32[16,40,128]{2,1,0:T(8,128)}), f32[16,40,128]{2,1,0:T(8,128)S(1)}, u32[]{:S(2)}, u32[]{:S(2)}) async-start(f32[16,40,128]{2,1,0:T(8,128)} %shard_map.102), calls=%async_computation.1 | async-start | bytes 655360 | tf_op jit(solution)/shard_map/all_to_all | solution.py:225
  93.2 40.8 %copy-start.2 = (bf16[64,512]{1,0:T(8,128)(2,1)S(1)}, bf16[64,512]{1,0:T(8,128)(2,1)}, u32[]{:S(2)}) copy-start(bf16[64,512]{1,0:T(8,128)(2,1)} %param.13) | copy-start | bytes 196612
  113.4 7.1 %collective-permute-start.1 = (bf16[16,4,64,128]{3,2,1,0:T(8,128)(2,1)S(1)}, bf16[16,4,64,128]{3,2,1,0:T(8,128)(2,1)S(1)}, u32[]{:S(2)}, u32[]{:S(2)}) collective-permute-start(bf16[16,4,64,128]{3,2,1,0:T(8,128)(2,1)S(1)} %slice.7.mine), channel_id=1, source_target_pairs={{0,4},{4,0},{1,5},{5,1},{2,6},{6,2},{3,7},{7,3},{8,12},{12,8},{9,1... | collective-permute-start | bytes 3145736 | tf_op jit(solution)/shard_map/ppermute | solution.py:239
  121.7 17.4 %collective-permute-start.2 = (bf16[16,4,208,128]{3,2,1,0:T(8,128)(2,1)}, bf16[16,4,208,128]{3,2,1,0:T(8,128)(2,1)S(1)}, u32[]{:S(2)}, u32[]{:S(2)}) collective-permute-start(bf16[16,4,208,128]{3,2,1,0:T(8,128)(2,1)} %bitcast.8.mine), channel_id=1, source_target_pairs={{0,4},{4,0},{1,5},{5,1},{2,6},{6,2},{3,7},{7,3},{8,12},{12,8},{9,1... | collective-permute-start | bytes 10223624 | tf_op jit(solution)/shard_map/ppermute | solution.py:248
  135.0 14.3 %all-to-all-start.4 = ((bf16[8,64,512]{2,1,0:T(8,128)(2,1)}), bf16[8,64,512]{2,1,0:T(8,128)(2,1)}, u32[]{:S(2)}, u32[]{:S(2)}) async-start(bf16[8,64,512]{2,1,0:T(8,128)(2,1)} %broadcast_in_dim.10), calls=%async_computation.4 | async-start | bytes 1048576 | tf_op jit(solution)/shard_map/all_to_all | solution.py:260
  139.1 1.8 %copy-start.1 = (bf16[16,4,208,128]{3,2,1,0:T(8,128)(2,1)}, bf16[16,4,208,128]{3,2,1,0:T(8,128)(2,1)S(1)}, u32[]{:S(2)}) copy-start(bf16[16,4,208,128]{3,2,1,0:T(8,128)(2,1)S(1)} %collective-permute-done.2.other) | copy-start | bytes 10223620
Sparse Core Ops, SparseCore 0:
  20.5 86.8 all-gather.4

commit v9 on v8

--- a/solution.py
+++ b/solution.py
@@ -61,14 +61,20 @@
                 out[y, at : at + 16] = w[:, low : low + 128]
 
 
-def marks_body(core, mine, other, starts, ends, out):
-    c = core[0]
+def marks_body(place, mine, other, lengths, out):
+    c = place[0]
+    row = lax.broadcasted_iota(jnp.int32, (64, 64), 0)
+    lane = lax.broadcasted_iota(jnp.int32, (64, 64), 1)
+    sizes = jnp.broadcast_to(lengths[...], (64, 64)).astype(F32)
+    starts = jnp.sum(jnp.where(lane < row, sizes, 0.0), axis=1, keepdims=True)
+    ends = jnp.sum(jnp.where(lane <= row, sizes, 0.0), axis=1, keepdims=True)
+    starts, ends = (e.astype(jnp.int32) - place[1] * 512 for e in (starts, ends))
     low = pl.multiple_of(c * 64, 64)
     total = None
-    for got, place in ((mine, c), (other, 1 - c)):
+    for got, at_core in ((mine, c), (other, 1 - c)):
         at = lax.broadcasted_iota(jnp.int32, (64, 256), 1)
-        at = at + (at // 64) * 64 + place * 64
-        member = ((at >= starts[...]) & (at < ends[...])).astype(BF16)
+        at = at + (at // 64) * 64 + at_core * 64
+        member = ((at >= starts) & (at < ends)).astype(BF16)
         part = dot(member, got[:, pl.ds(low, 64), :].reshape(256, HEAD), ((1,), (0,)))
         total = part if total is None else total + part
     out[...] = total
@@ -215,9 +221,9 @@
     got = lax.all_to_all(pack, y_axes, 0, 0)
     weights = lax.all_gather(got[:, 192:400], "z", axis=0)
     other = lax.ppermute(got, "c", [(0, 1), (1, 0)])
-    ends = jnp.cumsum(seg_lengths) - z * 512
-    mine = kernel_call(marks_body, shape((64, HEAD), F32), 4, core=c[None])(
-        got, other, (ends - seg_lengths)[:, None], ends[:, None]
+    place = jnp.stack([c, z]).astype(jnp.int32)
+    mine = kernel_call(marks_body, shape((64, HEAD), F32), 3, core=place)(
+        got, other, seg_lengths[None, :]
     )
     mine = jnp.sum(lax.all_gather(mine, "z", axis=0), axis=0)
     marks = lax.all_gather(mine / seg_lengths.astype(F32)[:, None], "c", axis=0)

time: 176 us -> 176 us (level)
  blocking collectives: 97.3 us -> 93.8 us
  waiting for transfers between devices: 10.6 us -> 13.5 us
    all_to_all x1, blocking collectives: 13.9 us -> 11 us  [on_device(): gathered = lax.all_to_all(gathered, (*y_axes, 'c'), 0, 0)]
    all_to_all x1, waiting for transfers between devices: 4.61 us -> 7.24 us  [on_device(): parts = lax.all_to_all(send, 'z', 0, 0)]
  transfers between devices with their start and end apart: 6 -> 6, of which waited for: 4 -> 4; matrix products, arithmetic and copies ran while one was open for 2% -> 1% of each run, Pallas kernels for 7% -> 7%
where the time goes in v9:
time: 176 us; the launch traced here: 175 us
  blocking collectives  93.8 us (53%)
  starting transfers between devices  26.4 us (15%)
  Pallas kernels  20.6 us (12%)
  waiting for transfers between devices  13.5 us (8%)
  between operations  13.5 us (8%)
  local copies, waits for them, and re-layouts  5.29 us (3%)
    all_gather x1, blocking collectives, on_device(): mine = jnp.sum(lax.all_gather(mine, 'z', axis=0), axis=0)  31.5 us
    all_to_all x1, blocking collectives, on_device(): parts = lax.all_to_all(terms, ('yl', 'x'), 0, 0)  12.6 us
    all_to_all x1, blocking collectives, on_device(): got = lax.all_to_all(pack, y_axes, 0, 0)  11.3 us
    all_to_all x1, blocking collectives, on_device(): gathered = lax.all_to_all(gathered, (*y_axes, 'c'), 0, 0)  11 us
    all_gather x1, blocking collectives, on_device(): heads = lax.all_gather(heads, y_axes, axis=0)  10.6 us
    all_to_all x1, blocking collectives, on_device(): parts = lax.all_to_all(terms, 'x', 0, 0)  10 us
    pallas_call x4, Pallas kernels, kernel_call(): return call if core is None else lambda *args: call(core, *args)  8.52 us
    ppermute x1, starting transfers between devices, on_device(): other = lax.ppermute(got, 'c', [(0, 1), (1, 0)])  8.35 us
  transfers between devices with their start and end apart: 6, of which 4 were waited for; matrix products, arithmetic and copies ran while one was open for 1% of the time, Pallas kernels for 7%

profile of v9, /device:TPU:1, one launch (start us, length us, event | category | flops | bytes accessed | tf_op | source)
XLA Modules:
  0.0 174.7 jit_solution(4015890287040009889)
XLA Ops:
  6.5 0.0 all-gather.5.cloned.1.call-start
  6.5 1.8 %shard_map.100 = bf16[4,400,128]{2,1,0:T(8,128)(2,1)} custom-call(bf16[64,512]{1,0:T(8,128)(2,1)} %queries.1, bf16[64,512]{1,0:T(8,128)(2,1)} %k.1, bf16[64,512]{1,0:T(8,128)(2,1)} %v.1, bf16[16,768]{1,0:T(8,128)(2,1)} %wg.1, bf16[16,768]{1,0:T(8,128)(2,1)} %wu.1, bf16[16,768]{1,0:T(8,128)(2,1)} %bitcast.15, bf16[16,512]{1,0:T(8,128)(2,1)} %bitcast.16), custom_call_target="tpu_custom_call" | custom-call | tf_op jit(solution)/shard_map/pallas_call | solution.py:218
  8.3 11.3 %all_to_all.30.mine = bf16[4,400,128]{2,1,0:T(8,128)(2,1)S(1)} all-to-all(bf16[4,400,128]{2,1,0:T(8,128)(2,1)} %shard_map.100), channel_id=1, replica_groups=mesh['z'=16,'yh'=2,'yl'=2,'c'=2,'x'=4] {'yh','yl'}, dimensions={0} | all-to-all | bytes 819200 | tf_op jit(solution)/shard_map/all_to_all | solution.py:221
  19.6 0.7 slice.8
  20.3 0.0 all-gather.5.cloned.1.call-update
  20.3 8.4 %collective-permute-start = (bf16[4,400,128]{2,1,0:T(8,128)(2,1)S(1)}, bf16[4,400,128]{2,1,0:T(8,128)(2,1)S(1)}, u32[]{:S(2)}, u32[]{:S(2)}) collective-permute-start(bf16[4,400,128]{2,1,0:T(8,128)(2,1)S(1)} %all_to_all.30.mine), channel_id=1, source_target_pairs={{0,4},{4,0},{1,5},{5,1},{2,6},{6,2},{3,7},{7,3},{8,12},{12,8},{9,1... | collective-permute-start | bytes 1228808 | tf_op jit(solution)/shard_map/ppermute | solution.py:223
  28.7 0.7 convert_element_type.22
  29.4 0.1 pad_add_fusion.place
  29.4 0.6 collective-permute-done.other
  30.1 0.0 copy-start.1
  30.1 0.7 copy-done.1
  30.7 0.8 shard_map.101
  31.5 31.5 %all-gather = f32[1024,128]{1,0:T(8,128)S(1)} all-gather(f32[64,128]{1,0:T(8,128)S(1)} %shard_map.101), channel_id=2, replica_groups=mesh['z'=16,'yh'=2,'yl'=2,'c'=2,'x'=4] {'z'}, dimensions={0}, use_global_device_ids=true | all-gather | bytes 557056 | tf_op jit(solution)/shard_map/all_gather | solution.py:228
  63.0 0.0 copy-start
  63.1 0.1 bitcast_divide_fusion
  63.1 6.7 %all_gather.24.marks = f32[2,64,128]{2,1,0:T(8,128)S(1)} all-gather(f32[1,64,128]{2,1,0:T(8,128)S(1)} %bitcast_divide_fusion), channel_id=1, replica_groups=mesh['z'=16,'yh'=2,'yl'=2,'c'=2,'x'=4] {'c'}, dimensions={0}, use_global_device_ids=true | all-gather | bytes 98304 | tf_op jit(solution)/shard_map/all_gather | solution.py:229
  69.9 1.4 shard_map.102
  71.3 7.1 %all-to-all-start.1 = ((f32[16,40,128]{2,1,0:T(8,128)}), f32[16,40,128]{2,1,0:T(8,128)S(1)}, u32[]{:S(2)}, u32[]{:S(2)}) async-start(f32[16,40,128]{2,1,0:T(8,128)} %shard_map.102), calls=%async_computation.1 | async-start | bytes 655360 | tf_op jit(solution)/shard_map/all_to_all | solution.py:231
  78.4 4.5 %shard_map.103 = f32[2,64,128]{2,1,0:T(8,128)S(1)} custom-call(f32[2,64,128]{2,1,0:T(8,128)S(1)} %all_gather.24.marks), custom_call_target="tpu_custom_call" | custom-call | flops 1000000000 | bytes 20000000 | tf_op jit(solution)/shard_map/pallas_call | solution.py:232
  82.9 10.6 %all-gather.1 = f32[8,64,128]{2,1,0:T(8,128)S(1)} all-gather(f32[2,64,128]{2,1,0:T(8,128)S(1)} %shard_map.103), channel_id=3, replica_groups=mesh['z'=16,'yh'=2,'yl'=2,'c'=2,'x'=4] {'yh','yl'}, dimensions={0}, use_global_device_ids=true | all-gather | bytes 327680 | tf_op jit(solution)/shard_map/all_gather | solution.py:238
  93.5 0.0 copy-done
  93.5 0.5 shard_map.104.near
  94.0 0.0 copy-start.3
  94.0 7.2 %all-to-all-done.1.parts = f32[16,40,128]{2,1,0:T(8,128)S(1)} async-done(((f32[16,40,128]{2,1,0:T(8,128)}), f32[16,40,128]{2,1,0:T(8,128)S(1)}, u32[]{:S(2)}, u32[]{:S(2)}) %all-to-all-start.1) | async-done | bytes 327712 | tf_op jit(solution)/shard_map/all_to_all | solution.py:231
  101.3 0.2 shard_map.105
  101.5 11.0 %all_to_all.31.gathered = f32[8,32,128]{2,1,0:T(8,128)S(1)} all-to-all(f32[8,32,128]{2,1,0:T(8,128)S(1)} %shard_map.105), channel_id=1, replica_groups=mesh['z'=16,'yh'=2,'yl'=2,'c'=2,'x'=4] {'yh','yl','c'}, dimensions={0} | all-to-all | bytes 262144 | tf_op jit(solution)/shard_map/all_to_all | solution.py:242
  112.5 0.0 all-gather.5.cloned.1.call-done
  112.5 1.3 slice.7.mine
  113.8 4.5 %collective-permute-start.1 = (bf16[16,4,64,128]{3,2,1,0:T(8,128)(2,1)S(1)}, bf16[16,4,64,128]{3,2,1,0:T(8,128)(2,1)S(1)}, u32[]{:S(2)}, u32[]{:S(2)}) collective-permute-start(bf16[16,4,64,128]{3,2,1,0:T(8,128)(2,1)S(1)} %slice.7.mine), channel_id=1, source_target_pairs={{0,4},{4,0},{1,5},{5,1},{2,6},{6,2},{3,7},{7,3},{8,12},{12,8},{9,1... | collective-permute-start | bytes 3145736 | tf_op jit(solution)/shard_map/ppermute | solution.py:245
  118.3 2.3 %collective-permute-done.1.other = bf16[16,4,64,128]{3,2,1,0:T(8,128)(2,1)S(1)} collective-permute-done((bf16[16,4,64,128]{3,2,1,0:T(8,128)(2,1)S(1)}, bf16[16,4,64,128]{3,2,1,0:T(8,128)(2,1)S(1)}, u32[]{:S(2)}, u32[]{:S(2)}) %collective-permute-start.1) | collective-permute-done | bytes 1048608 | tf_op jit(solution)/shard_map/ppermute | solution.py:245
  120.6 1.3 shard_map.106
  121.9 2.3 %collective-permute-start.2 = (bf16[16,4,208,128]{3,2,1,0:T(8,128)(2,1)}, bf16[16,4,208,128]{3,2,1,0:T(8,128)(2,1)S(1)}, u32[]{:S(2)}, u32[]{:S(2)}) collective-permute-start(bf16[16,4,208,128]{3,2,1,0:T(8,128)(2,1)} %bitcast.8.mine), channel_id=1, source_target_pairs={{0,4},{4,0},{1,5},{5,1},{2,6},{6,2},{3,7},{7,3},{8,12},{12,8},{9,1... | collective-permute-start | bytes 10223624 | tf_op jit(solution)/shard_map/ppermute | solution.py:254
  124.2 10.0 %all_to_all.32 = bf16[4,64,512]{2,1,0:T(8,128)(2,1)S(1)} all-to-all(bf16[4,64,512]{2,1,0:T(8,128)(2,1)S(1)} %shard_map.106), channel_id=1, replica_groups=mesh['z'=16,'yh'=2,'yl'=2,'c'=2,'x'=4] {'x'}, dimensions={0} | all-to-all | bytes 524288 | tf_op jit(solution)/shard_map/all_to_all | solution.py:255
  134.2 0.0 copy-done.3
  134.3 0.9 broadcast_in_dim.20
  135.1 4.1 %all-to-all-start.4 = ((bf16[8,64,512]{2,1,0:T(8,128)(2,1)}), bf16[8,64,512]{2,1,0:T(8,128)(2,1)}, u32[]{:S(2)}, u32[]{:S(2)}) async-start(bf16[8,64,512]{2,1,0:T(8,128)(2,1)} %broadcast_in_dim.20), calls=%async_computation.4 | async-start | bytes 1048576 | tf_op jit(solution)/shard_map/all_to_all | solution.py:266
  139.3 0.0 collective-permute-done.2.other
  139.3 0.0 copy-start.2
  139.3 1.8 %copy-done.2 = bf16[16,4,208,128]{3,2,1,0:T(8,128)(2,1)} copy-done((bf16[16,4,208,128]{3,2,1,0:T(8,128)(2,1)}, bf16[16,4,208,128]{3,2,1,0:T(8,128)(2,1)S(1)}, u32[]{:S(2)}) %copy-start.2) | copy-done | bytes 3407896
  141.0 5.1 %shard_map.107 = (bf16[2048,768]{1,0:T(8,128)(2,1)}, bf16[2048,384]{1,0:T(8,128)(2,1)}) custom-call(s32[1]{0:T(128)} %bitcast.core, bf16[16,4,208,128]{3,2,1,0:T(8,128)(2,1)} %bitcast.8.mine, bf16[16,4,208,128]{3,2,1,0:T(8,128)(2,1)} %copy-done.2), custom_call_target="tpu_custom_call" | custom-call | tf_op jit(solution)/shard_map/pallas_call | solution.py:42
  146.1 3.3 %all-to-all-done.4.whole = bf16[8,64,512]{2,1,0:T(8,128)(2,1)} async-done(((bf16[8,64,512]{2,1,0:T(8,128)(2,1)}), bf16[8,64,512]{2,1,0:T(8,128)(2,1)}, u32[]{:S(2)}, u32[]{:S(2)}) %all-to-all-start.4) | async-done | bytes 524320 | tf_op jit(solution)/shard_map/all_to_all | solution.py:266
  149.5 5.1 %shard_map.108 = bf16[8,64,512]{2,1,0:T(8,128)(2,1)} custom-call(bf16[8,64,512]{2,1,0:T(8,128)(2,1)} %all-to-all-done.4.whole, f32[1,2048]{1,0:T(1,128)} %bitcast.17, bf16[2048,768]{1,0:T(8,128)(2,1)} %get-tuple-element.21.far1, bf16[2048,384]{1,0:T(8,128)(2,1)} %get-tuple-element.22.far2), custom_call_target="tpu_custom_call" | custom-call | tf_op jit(solution)/shard_map/pallas_call | solution.py:267
  154.6 12.6 %all_to_all.33 = bf16[8,64,512]{2,1,0:T(8,128)(2,1)S(1)} all-to-all(bf16[8,64,512]{2,1,0:T(8,128)(2,1)} %shard_map.108), channel_id=1, replica_groups=mesh['z'=16,'yh'=2,'yl'=2,'c'=2,'x'=4] {'yl','x'}, dimensions={0} | all-to-all | bytes 1048576 | tf_op jit(solution)/shard_map/all_to_all | solution.py:280
  167.2 0.1 convert_reduce_fusion
  167.3 0.6 add_convert_fusion
  (3 shorter events, 0.1 us)
Async XLA Ops:
  6.5 106.0 %all-gather.5.cloned.1.call-start = ((), (), s32[]{:S(2)}) async-start(), calls=%async_computation.6 | async-start | bytes 3620864 | tf_op jit(solution)/shard_map/all_gather | solution.py:222
  20.3 9.7 %collective-permute-start = (bf16[4,400,128]{2,1,0:T(8,128)(2,1)S(1)}, bf16[4,400,128]{2,1,0:T(8,128)(2,1)S(1)}, u32[]{:S(2)}, u32[]{:S(2)}) collective-permute-start(bf16[4,400,128]{2,1,0:T(8,128)(2,1)S(1)} %all_to_all.30.mine), channel_id=1, source_target_pairs={{0,4},{4,0},{1,5},{5,1},{2,6},{6,2},{3,7},{7,3},{8,12},{12,8},{9,1... | collective-permute-start | bytes 1228808 | tf_op jit(solution)/shard_map/ppermute | solution.py:223
  30.1 0.7 copy-start.1
  63.0 30.5 %copy-start = (bf16[64,512]{1,0:T(8,128)(2,1)S(1)}, bf16[64,512]{1,0:T(8,128)(2,1)}, u32[]{:S(2)}) copy-start(bf16[64,512]{1,0:T(8,128)(2,1)} %queries.1) | copy-start | bytes 196612
  71.3 30.0 %all-to-all-start.1 = ((f32[16,40,128]{2,1,0:T(8,128)}), f32[16,40,128]{2,1,0:T(8,128)S(1)}, u32[]{:S(2)}, u32[]{:S(2)}) async-start(f32[16,40,128]{2,1,0:T(8,128)} %shard_map.102), calls=%async_computation.1 | async-start | bytes 655360 | tf_op jit(solution)/shard_map/all_to_all | solution.py:231
  94.0 40.2 %copy-start.3 = (bf16[64,512]{1,0:T(8,128)(2,1)S(1)}, bf16[64,512]{1,0:T(8,128)(2,1)}, u32[]{:S(2)}) copy-start(bf16[64,512]{1,0:T(8,128)(2,1)} %param.13) | copy-start | bytes 196612
  113.8 6.8 %collective-permute-start.1 = (bf16[16,4,64,128]{3,2,1,0:T(8,128)(2,1)S(1)}, bf16[16,4,64,128]{3,2,1,0:T(8,128)(2,1)S(1)}, u32[]{:S(2)}, u32[]{:S(2)}) collective-permute-start(bf16[16,4,64,128]{3,2,1,0:T(8,128)(2,1)S(1)} %slice.7.mine), channel_id=1, source_target_pairs={{0,4},{4,0},{1,5},{5,1},{2,6},{6,2},{3,7},{7,3},{8,12},{12,8},{9,1... | collective-permute-start | bytes 3145736 | tf_op jit(solution)/shard_map/ppermute | solution.py:245
  121.9 17.4 %collective-permute-start.2 = (bf16[16,4,208,128]{3,2,1,0:T(8,128)(2,1)}, bf16[16,4,208,128]{3,2,1,0:T(8,128)(2,1)S(1)}, u32[]{:S(2)}, u32[]{:S(2)}) collective-permute-start(bf16[16,4,208,128]{3,2,1,0:T(8,128)(2,1)} %bitcast.8.mine), channel_id=1, source_target_pairs={{0,4},{4,0},{1,5},{5,1},{2,6},{6,2},{3,7},{7,3},{8,12},{12,8},{9,1... | collective-permute-start | bytes 10223624 | tf_op jit(solution)/shard_map/ppermute | solution.py:254
  135.1 14.4 %all-to-all-start.4 = ((bf16[8,64,512]{2,1,0:T(8,128)(2,1)}), bf16[8,64,512]{2,1,0:T(8,128)(2,1)}, u32[]{:S(2)}, u32[]{:S(2)}) async-start(bf16[8,64,512]{2,1,0:T(8,128)(2,1)} %broadcast_in_dim.20), calls=%async_computation.4 | async-start | bytes 1048576 | tf_op jit(solution)/shard_map/all_to_all | solution.py:266
  139.3 1.8 %copy-start.2 = (bf16[16,4,208,128]{3,2,1,0:T(8,128)(2,1)}, bf16[16,4,208,128]{3,2,1,0:T(8,128)(2,1)S(1)}, u32[]{:S(2)}) copy-start(bf16[16,4,208,128]{3,2,1,0:T(8,128)(2,1)S(1)} %collective-permute-done.2.other) | copy-start | bytes 10223620
Sparse Core Ops, SparseCore 0:
  20.5 87.1 all-gather.4

commit v10 on v6

--- a/solution.py
+++ b/solution.py
@@ -17,6 +17,9 @@
 BF16 = jnp.bfloat16
 SMALL = 24 << 20
 LARGE = 60 << 20
+SLICE = (0, 1, 1, 0)
+SWAP = ((0, 1), (1, 0))
+PAIR = ((0, 3), (3, 0), (1, 2), (2, 1))
 
 
 def dot(a, b, dims, precision=None):
@@ -54,23 +57,36 @@
         out[y, 128:192] = v[:, tile]
         out[y, 192:208] = wo[:, tile]
         for t in range(3):
-            low = ((y % 2) * 3 + t) * 128
+            low = (SLICE[y] * 3 + t) * 128
             for i, w in enumerate((wg, wu, wd)):
                 at = 208 + (3 * i + t) * 16
                 out[y, at : at + 16] = w[:, low : low + 128]
 
 
-def marks_body(core, mine, other, starts, ends, out):
-    c = core[0]
+def marks_body(place, mine, other, lengths, out):
+    c = place[0]
+    row = lax.broadcasted_iota(jnp.int32, (64, 64), 0)
+    lane = lax.broadcasted_iota(jnp.int32, (64, 64), 1)
+    sizes = jnp.broadcast_to(lengths[...], (64, 64)).astype(F32)
+    starts = jnp.sum(jnp.where(lane < row, sizes, 0.0), axis=1, keepdims=True)
+    ends = jnp.sum(jnp.where(lane <= row, sizes, 0.0), axis=1, keepdims=True)
+    starts, ends = (e.astype(jnp.int32) - place[1] * 512 for e in (starts, ends))
     low = pl.multiple_of(c * 64, 64)
     total = None
-    for got, place in ((mine, c), (other, 1 - c)):
+    for got, at_core in ((mine, c), (other, 1 - c)):
         at = lax.broadcasted_iota(jnp.int32, (64, 256), 1)
-        at = at + (at // 64) * 64 + place * 64
-        member = ((at >= starts[...]) & (at < ends[...])).astype(BF16)
+        at = at + (at // 64) * 64 + at_core * 64
+        member = ((at >= starts) & (at < ends)).astype(BF16)
         part = dot(member, got[:, pl.ds(low, 64), :].reshape(256, HEAD), ((1,), (0,)))
         total = part if total is None else total + part
     out[...] = total
+
+
+def shard_body(half, got, out):
+    for y in range(4):
+        out[y * 16 : y * 16 + 16] = got[y, 192:208]
+    for i in range(2):
+        out[64 + i * 144 : 208 + i * 144] = got[half[0] * 2 + i, 208:352]
 
 
 def far_body(core, mine, other, marks, out):
@@ -139,33 +155,37 @@
             out[y * 4 + x] = terms[y * 64 : y * 64 + 64, x * 512 : x * 512 + 512].astype(BF16)
 
 
-def unmix(weights, tile, dest, lanes):
-    for z in range(16):
-        for c in range(2):
+def unmix_body(place, mine, mine_core, pair, pair_core, w1, w2, raw, sems):
+    c, half = place[0], place[1]
+    fars = (mine, mine_core, pair, pair_core)
+    copies = [
+        pltpu.make_async_copy(far, raw.at[i], sems.at[i]) for i, far in enumerate(fars)
+    ]
+    for copy in copies:
+        copy.start()
+    sources = ((half, c), (half, 1 - c), (1 - half, c), (1 - half, 1 - c))
+    for i, (h, core) in enumerate(sources):
+        copies[i].wait()
+        for z in range(16):
+            for y in range(2):
+                low = pl.multiple_of((z * 8 + h * 4 + y * 2 + core) * 16, 16)
+                for t in range(9):
+                    at = y * 144 + t * 16
+                    rows = raw[i, z, at : at + 16, :]
+                    if t < 6:
+                        w1[pl.ds(low, 16), t * 128 : t * 128 + 128] = rows
+                    else:
+                        w2[pl.ds(low, 16), t * 128 - 768 : t * 128 - 640] = rows
+
+
+def proj_body(place, near, inverse, gathered, mine, other, out, wo):
+    for blocks, core in ((mine, place[0]), (other, 1 - place[0])):
+        for z in range(16):
             for y in range(4):
-                low = (z * 8 + y * 2 + c) * 16
-                dest[low : low + 16, lanes] = weights[
-                    z * 2 + c, y, tile * 16 : tile * 16 + 16, :
-                ]
-
-
-def unmix_body(weights, w1, w2, raw, sem):
-    copy = pltpu.make_async_copy(weights.at[:, :, 16:160], raw, sem)
-    copy.start()
-    copy.wait()
-    for t in range(6):
-        unmix(raw, t, w1, slice(t * 128, t * 128 + 128))
-    for t in range(3):
-        unmix(raw, 6 + t, w2, slice(t * 128, t * 128 + 128))
-
-
-def proj_body(near, inverse, gathered, weights, out, raw, wo, sem):
-    copy = pltpu.make_async_copy(weights.at[:, :, 0:16], raw, sem)
-    copy.start()
+                low = pl.multiple_of((z * 8 + y * 2 + core) * 16, 16)
+                wo[pl.ds(low, 16), :] = blocks[z, y * 16 : y * 16 + 16, :]
     mixer = dot(inverse[...], gathered[...], ((1,), (0,)), HI)
     attn = dot(near[...], mixer, ((1,), (0,)), HI).astype(BF16)
-    copy.wait()
-    unmix(raw, 0, wo, slice(0, 128))
     spread(dot(attn, wo[...], ((1,), (1,))), out)
 
 
@@ -198,11 +218,13 @@
         queries, keys, values, w_gate, w_up, w_down.T, w_out.T
     )
     got = lax.all_to_all(pack, y_axes, 0, 0)
-    weights = lax.all_gather(got[:, 192:352], ("z", "c"), axis=0)
-    other = lax.ppermute(got, "c", [(0, 1), (1, 0)])
-    ends = jnp.cumsum(seg_lengths) - z * 512
-    mine = kernel_call(marks_body, shape((64, HEAD), F32), 4, core=c[None])(
-        got, other, (ends - seg_lengths)[:, None], ends[:, None]
+    yh = lax.axis_index("yh")
+    place = jnp.stack([c, z, yh]).astype(jnp.int32)
+    shard = kernel_call(shard_body, shape((352, 128), BF16), 1, core=yh[None])(got)
+    weights = lax.all_gather(shard, "z", axis=0)
+    other = lax.ppermute(got, "c", SWAP)
+    mine = kernel_call(marks_body, shape((64, HEAD), F32), 3, core=place)(
+        got, other, seg_lengths[None, :]
     )
     mine = jnp.sum(lax.all_gather(mine, "z", axis=0), axis=0)
     marks = lax.all_gather(mine / seg_lengths.astype(F32)[:, None], "c", axis=0)
@@ -214,30 +236,30 @@
         2,
         cost=pl.CostEstimate(flops=10**9, bytes_accessed=2 * 10**7, transcendentals=0),
     )(got, marks)
+    w_out, ffn = weights[:, 0:64], weights[:, 64:352]
+    w_other = lax.ppermute(w_out, "c", SWAP)
+    pair = lax.ppermute(ffn, y_axes, PAIR)
+    parts, near, inverse, w_other, ffn = lax.optimization_barrier(
+        (parts, near, inverse, w_other, ffn)
+    )
     gathered = kernel_call(merge_body, shape((32, HEAD), F32), 1)(parts)
     gathered = lax.all_gather(gathered, "c", axis=0, tiled=True)
-
     terms = kernel_call(
-        proj_body,
-        shape((16, 64, 512), BF16),
-        3,
-        [
-            pltpu.VMEM((32, 4, 16, 128), BF16),
-            pltpu.VMEM((2048, 128), BF16),
-            pltpu.SemaphoreType.DMA(()),
-        ],
-        n_far=1,
-        grant=LARGE,
-    )(near, inverse, gathered, weights)
+        proj_body, shape((16, 64, 512), BF16), 5, [pltpu.VMEM((2048, 128), BF16)], core=place
+    )(near, inverse, gathered, w_out, w_other)
     parts = lax.all_to_all(terms, (*y_axes, "x"), 0, 0)
+    ffn, pair, terms = lax.optimization_barrier((ffn, pair, terms))
+    ffn_core = lax.ppermute(ffn, "c", SWAP)
+    pair_core = lax.ppermute(pair, "c", SWAP)
     w1, w2 = kernel_call(
         unmix_body,
         [shape((2048, 768), BF16), shape((2048, 384), BF16)],
         0,
-        [pltpu.VMEM((32, 4, 144, 128), BF16), pltpu.SemaphoreType.DMA(())],
-        n_far=1,
+        [pltpu.VMEM((4, 16, 288, 128), BF16), pltpu.SemaphoreType.DMA((4,))],
+        core=jnp.stack([c, yh]).astype(jnp.int32),
+        n_far=4,
         grant=LARGE,
-    )(weights)
+    )(ffn, ffn_core, pair, pair_core)
     resid = (stream.astype(F32) + jnp.sum(parts.astype(F32), axis=0)).astype(BF16)
     whole = lax.all_to_all(jnp.broadcast_to(resid[None], (8, 64, 512)), ("yl", "x"), 0, 0)
     terms = kernel_call(

time: 179 us -> 184 us (1.028)
  blocking collectives: 91.8 us -> 51.3 us
  starting transfers between devices: 18 us -> 49.9 us
  waiting for transfers between devices: 27.3 us -> 40.8 us
    all_to_all x2 -> x0, blocking collectives: 34.7 us -> none  [the longest x1 23.6 us: on_device(): parts = lax.all_to_all(terms, (*y_axes, 'x'), 0, 0)]
    ppermute x1 -> x5, starting transfers between devices: 8.34 us -> 29.1 us  [the longest x1 10.5 us: on_device(): w_other = lax.ppermute(w_out, 'c', SWAP)]
    all_to_all x0 -> x2, waiting for transfers between devices: none -> 17.2 us  [the longest x1 11.2 us: on_device(): parts = lax.all_to_all(terms, (*y_axes, 'x'), 0, 0)]
    all_to_all x1, waiting for transfers between devices: 15.8 us -> 0.04 us  [on_device(): parts = lax.all_to_all(send, 'z', 0, 0)]
    all_gather x1, waiting for transfers between devices: 7.05 us -> 18.9 us  [on_device(): weights = lax.all_gather(shard, 'z', axis=0)]
    all_to_all x0 -> x2, starting transfers between devices: none -> 9.73 us  [the longest x1 5.01 us: on_device(): got = lax.all_to_all(pack, y_axes, 0, 0)]
    pallas_call x2 -> x5, Pallas kernels: 1.58 us -> 10.6 us  [kernel_call(): return call if core is None else lambda *args: call(core, *args)]
    pallas_call x2 -> x0, Pallas kernels: 8.86 us -> none  [the longest x1 5.34 us: on_device(): kernel_call(unmix_body, [shape((2048, 768), BF16), shape((2048, 384), BF1...]
  transfers between devices with their start and end apart: 4 -> 10, of which waited for: 4 -> 5; matrix products, arithmetic and copies ran while one was open for 1% -> 2% of each run, Pallas kernels for 7% -> 8%
where the time goes in v10:
time: 184 us
  blocking collectives  51.3 us (28%)
  starting transfers between devices  49.9 us (27%)
  waiting for transfers between devices  40.8 us (22%)
  Pallas kernels  22.2 us (12%)
  between operations  13.6 us (7%)
  local copies, waits for them, and re-layouts  3.98 us (2%)
    all_gather x1, blocking collectives, on_device(): mine = jnp.sum(lax.all_gather(mine, 'z', axis=0), axis=0)  31.4 us
    all_gather x1, waiting for transfers between devices, on_device(): weights = lax.all_gather(shard, 'z', axis=0)  18.9 us
    all_to_all x1, blocking collectives, on_device(): parts = lax.all_to_all(terms, ('yl', 'x'), 0, 0)  12.3 us
    all_to_all x1, waiting for transfers between devices, on_device(): parts = lax.all_to_all(terms, (*y_axes, 'x'), 0, 0)  11.2 us
    pallas_call x5, Pallas kernels, kernel_call(): return call if core is None else lambda *args: call(core, *args)  10.6 us
    ppermute x1, starting transfers between devices, on_device(): w_other = lax.ppermute(w_out, 'c', SWAP)  10.5 us
    ppermute x1, starting transfers between devices, on_device(): other = lax.ppermute(got, 'c', SWAP)  8.35 us
    all_to_all x1, starting transfers between devices, on_device(): parts = lax.all_to_all(send, 'z', 0, 0)  7.53 us
  transfers between devices with their start and end apart: 10, of which 5 were waited for; matrix products, arithmetic and copies ran while one was open for 2% of the time, Pallas kernels for 8%

profile of v10, /device:TPU:1, one launch (start us, length us, event | category | flops | bytes accessed | tf_op | source)
XLA Modules:
  0.0 183.5 jit_solution(1856980164875165273)
XLA Ops:
  6.5 0.0 copy-start
  6.5 1.7 shard_map.100
  8.3 5.0 %all-to-all-start = ((bf16[4,352,128]{2,1,0:T(8,128)(2,1)}), bf16[4,352,128]{2,1,0:T(8,128)(2,1)S(1)}, u32[]{:S(2)}, u32[]{:S(2)}) async-start(bf16[4,352,128]{2,1,0:T(8,128)(2,1)} %shard_map.100), calls=%async_computation | async-start | bytes 720896 | tf_op jit(solution)/shard_map/all_to_all | solution.py:220
  13.3 0.0 all-gather.4.cloned.1.call-start
  13.3 6.1 %all-to-all-done.mine.got = bf16[4,352,128]{2,1,0:T(8,128)(2,1)S(1)} async-done(((bf16[4,352,128]{2,1,0:T(8,128)(2,1)}), bf16[4,352,128]{2,1,0:T(8,128)(2,1)S(1)}, u32[]{:S(2)}, u32[]{:S(2)}) %all-to-all-start) | async-done | bytes 360480 | tf_op jit(solution)/shard_map/all_to_all | solution.py:220
  19.3 0.6 shard_map.104
  20.0 0.0 all-gather.4.cloned.1.call-update
  20.0 8.4 %collective-permute-start = (bf16[4,352,128]{2,1,0:T(8,128)(2,1)S(1)}, bf16[4,352,128]{2,1,0:T(8,128)(2,1)S(1)}, u32[]{:S(2)}, u32[]{:S(2)}) collective-permute-start(bf16[4,352,128]{2,1,0:T(8,128)(2,1)S(1)} %all-to-all-done.mine.got), channel_id=1, source_target_pairs={{0,4},{4,0},{1,5},{5,1},{2,6},{6,2},{3,7},{7,3},{8,12},{12,8},{9,1... | collective-permute-start | bytes 1081352 | tf_op jit(solution)/shard_map/ppermute | solution.py:225
  28.4 0.0 copy-done
  28.4 0.1 pad_add_fusion.place
  28.5 1.2 collective-permute-done.other
  29.7 0.8 shard_map.101
  30.4 31.4 %all-gather = f32[1024,128]{1,0:T(8,128)S(1)} all-gather(f32[64,128]{1,0:T(8,128)S(1)} %shard_map.101), channel_id=2, replica_groups=mesh['z'=16,'yh'=2,'yl'=2,'c'=2,'x'=4] {'z'}, dimensions={0}, use_global_device_ids=true | all-gather | bytes 557056 | tf_op jit(solution)/shard_map/all_gather | solution.py:229
  61.9 0.1 bitcast_divide_fusion
  62.0 5.8 %all_gather.21.marks = f32[2,64,128]{2,1,0:T(8,128)S(1)} all-gather(f32[1,64,128]{2,1,0:T(8,128)S(1)} %bitcast_divide_fusion), channel_id=1, replica_groups=mesh['z'=16,'yh'=2,'yl'=2,'c'=2,'x'=4] {'c'}, dimensions={0}, use_global_device_ids=true | all-gather | bytes 98304 | tf_op jit(solution)/shard_map/all_gather | solution.py:230
  67.7 1.4 shard_map.102
  69.1 7.5 %all-to-all-start.1 = ((f32[16,40,128]{2,1,0:T(8,128)}), f32[16,40,128]{2,1,0:T(8,128)S(1)}, u32[]{:S(2)}, u32[]{:S(2)}) async-start(f32[16,40,128]{2,1,0:T(8,128)} %shard_map.102), calls=%async_computation.1 | async-start | bytes 655360 | tf_op jit(solution)/shard_map/all_to_all | solution.py:232
  76.7 18.9 %all-gather.4.cloned.1.call-done = bf16[5632,128]{1,0:T(8,128)(2,1)} async-done(((bf16[352,128]{1,0:T(8,128)(2,1)}), bf16[5632,128]{1,0:T(8,128)(2,1)}) %all-gather.4.cloned.1.call-update) | async-done | bytes 1441808 | tf_op jit(solution)/shard_map/all_gather | solution.py:224
  95.6 1.3 slice.9.mine
  96.9 0.0 copy-start.1
  96.9 4.7 %collective-permute-start.2 = (bf16[16,288,128]{2,1,0:T(8,128)(2,1)S(1)}, bf16[16,288,128]{2,1,0:T(8,128)(2,1)}, u32[]{:S(2)}, u32[]{:S(2)}) collective-permute-start(bf16[16,288,128]{2,1,0:T(8,128)(2,1)S(1)} %slice.9.mine), channel_id=1, source_target_pairs={{0,24},{24,0},{8,16},{16,8},{1,25},{25,1},{9,17},{17,9},{2,26},{26... | collective-permute-start | bytes 3538952 | tf_op jit(solution)/shard_map/ppermute | solution.py:241
  101.7 1.0 slice.8.mine
  102.6 10.5 %collective-permute-start.1 = (bf16[16,64,128]{2,1,0:T(8,128)(2,1)S(1)}, bf16[16,64,128]{2,1,0:T(8,128)(2,1)S(1)}, u32[]{:S(2)}, u32[]{:S(2)}) collective-permute-start(bf16[16,64,128]{2,1,0:T(8,128)(2,1)S(1)} %slice.8.mine), channel_id=1, source_target_pairs={{0,4},{4,0},{1,5},{5,1},{2,6},{6,2},{3,7},{7,3},{8,12},{12,8},{9,1... | collective-permute-start | bytes 786440 | tf_op jit(solution)/shard_map/ppermute | solution.py:240
  113.2 4.5 %shard_map.103 = (f32[256,64]{1,0:T(8,128)S(1)}, f32[64,64]{1,0:T(8,128)S(1)}) custom-call(bf16[4,352,128]{2,1,0:T(8,128)(2,1)S(1)} %all-to-all-done.mine.got, f32[2,64,128]{2,1,0:T(8,128)S(1)} %all_gather.21.marks), custom_call_target="tpu_custom_call" | custom-call | flops 1000000000 | bytes 20000000 | tf_op jit(solution)/shard_map/pallas_call | solution.py:233
  117.7 0.0 all-to-all-done.1.parts
  117.7 0.0 collective-permute-done.1.other
  117.7 0.2 shard_map.105
  117.9 1.8 all_gather.24.gathered
  119.8 2.5 %shard_map.106 = bf16[16,64,512]{2,1,0:T(8,128)(2,1)} custom-call(s32[3]{0:T(128)S(1)} %pad_add_fusion.place, f32[256,64]{1,0:T(8,128)S(1)} %get-tuple-element.18.near, f32[64,64]{1,0:T(8,128)S(1)} %get-tuple-element.19.inverse, f32[64,128]{1,0:T(8,128)S(1)} %all_gather.24.gathered, bf16[16,64,128]{2,1,0:T(8,128)(2,1)S(1)} %slice.8.mine, ...), custom_call_target="tpu_custom_call" | custom-call | tf_op jit(solution)/shard_map/pallas_call | solution.py:45
  122.2 0.0 copy-start.3
  122.2 4.7 %all-to-all-start.2 = ((bf16[16,64,512]{2,1,0:T(8,128)(2,1)}), bf16[16,64,512]{2,1,0:T(8,128)(2,1)S(1)}, u32[]{:S(2)}, u32[]{:S(2)}) async-start(bf16[16,64,512]{2,1,0:T(8,128)(2,1)} %shard_map.106), calls=%async_computation.2 | async-start | bytes 2097152 | tf_op jit(solution)/shard_map/all_to_all | solution.py:250
  127.0 0.0 collective-permute-done.2.pair
  127.0 0.0 copy-done.1
  127.0 3.6 %collective-permute-start.3 = (bf16[16,288,128]{2,1,0:T(8,128)(2,1)S(1)}, bf16[16,288,128]{2,1,0:T(8,128)(2,1)}, u32[]{:S(2)}, u32[]{:S(2)}) collective-permute-start(bf16[16,288,128]{2,1,0:T(8,128)(2,1)S(1)} %slice.9.mine), channel_id=1, source_target_pairs={{0,4},{4,0},{1,5},{5,1},{2,6},{6,2},{3,7},{7,3},{8,12},{12,8},{9,1... | collective-permute-start | bytes 3538952 | tf_op jit(solution)/shard_map/ppermute | solution.py:252
  130.6 1.9 %collective-permute-start.4 = (bf16[16,288,128]{2,1,0:T(8,128)(2,1)}, bf16[16,288,128]{2,1,0:T(8,128)(2,1)}, u32[]{:S(2)}, u32[]{:S(2)}) collective-permute-start(bf16[16,288,128]{2,1,0:T(8,128)(2,1)} %collective-permute-done.2.pair), channel_id=1, source_target_pairs={{0,4},{4,0},{1,5},{5,1},{2,6},{6,2},{3,7},{7,3},{8,12},{12,8},{9,1... | collective-permute-start | bytes 3538952 | tf_op jit(solution)/shard_map/ppermute | solution.py:253
  132.5 11.2 %all-to-all-done.2 = bf16[16,64,512]{2,1,0:T(8,128)(2,1)S(1)} async-done(((bf16[16,64,512]{2,1,0:T(8,128)(2,1)}), bf16[16,64,512]{2,1,0:T(8,128)(2,1)S(1)}, u32[]{:S(2)}, u32[]{:S(2)}) %all-to-all-start.2) | async-done | bytes 1048608 | tf_op jit(solution)/shard_map/all_to_all | solution.py:250
  143.7 0.1 convert_reduce_fusion
  143.8 0.0 copy-done.3
  143.9 0.8 broadcast_in_dim.7
  144.7 3.5 %all-to-all-start.3 = ((bf16[8,64,512]{2,1,0:T(8,128)(2,1)}), bf16[8,64,512]{2,1,0:T(8,128)(2,1)S(1)}, u32[]{:S(2)}, u32[]{:S(2)}) async-start(bf16[8,64,512]{2,1,0:T(8,128)(2,1)} %broadcast_in_dim.7), calls=%async_computation.3 | async-start | bytes 1048576 | tf_op jit(solution)/shard_map/all_to_all | solution.py:264
  148.2 0.7 pad_add_fusion.1.place
  148.9 0.0 collective-permute-done.3.mine_core
  148.9 0.0 collective-permute-done.4.pair_core
  148.9 5.4 %shard_map.107 = (bf16[2048,768]{1,0:T(8,128)(2,1)}, bf16[2048,384]{1,0:T(8,128)(2,1)}) custom-call(s32[2]{0:T(128)} %pad_add_fusion.1.place, bf16[16,288,128]{2,1,0:T(8,128)(2,1)} %copy-done.1, bf16[16,288,128]{2,1,0:T(8,128)(2,1)} %collective-permute-done.3.mine_core, bf16[16,288,128]{2,1,0:T(8,128)(2,1)} %collective-permute-done.2.pair, ...), custom_call_target="tpu_custom_call" | custom-call | tf_op jit(solution)/shard_map/pallas_call | solution.py:45
  154.2 3.5 %all-to-all-done.3.whole = bf16[8,64,512]{2,1,0:T(8,128)(2,1)S(1)} async-done(((bf16[8,64,512]{2,1,0:T(8,128)(2,1)}), bf16[8,64,512]{2,1,0:T(8,128)(2,1)S(1)}, u32[]{:S(2)}, u32[]{:S(2)}) %all-to-all-start.3) | async-done | bytes 524320 | tf_op jit(solution)/shard_map/all_to_all | solution.py:264
  157.7 0.0 copy-start.2
  157.7 0.8 copy-done.2
  158.5 5.2 %shard_map.108 = bf16[8,64,512]{2,1,0:T(8,128)(2,1)} custom-call(bf16[8,64,512]{2,1,0:T(8,128)(2,1)} %copy-done.2, f32[1,2048]{1,0:T(1,128)} %bitcast.17, bf16[2048,768]{1,0:T(8,128)(2,1)} %get-tuple-element.25.far1, bf16[2048,384]{1,0:T(8,128)(2,1)} %get-tuple-element.26.far2), custom_call_target="tpu_custom_call" | custom-call | tf_op jit(solution)/shard_map/pallas_call | solution.py:265
  163.7 12.3 %all_to_all.25 = bf16[8,64,512]{2,1,0:T(8,128)(2,1)S(1)} all-to-all(bf16[8,64,512]{2,1,0:T(8,128)(2,1)} %shard_map.108), channel_id=1, replica_groups=mesh['z'=16,'yh'=2,'yl'=2,'c'=2,'x'=4] {'yl','x'}, dimensions={0} | all-to-all | bytes 1048576 | tf_op jit(solution)/shard_map/all_to_all | solution.py:278
  175.9 0.1 convert_reduce_fusion.1
  176.0 0.6 add_convert_fusion
  (3 shorter events, 0.1 us)
Async XLA Ops:
  6.5 21.8 %copy-start = (s32[64]{0:T(128)S(1)}, s32[64]{0:T(128)}, u32[]{:S(2)}) copy-start(s32[64]{0:T(128)} %param.14) | copy-start | bytes 772
  8.3 11.1 %all-to-all-start = ((bf16[4,352,128]{2,1,0:T(8,128)(2,1)}), bf16[4,352,128]{2,1,0:T(8,128)(2,1)S(1)}, u32[]{:S(2)}, u32[]{:S(2)}) async-start(bf16[4,352,128]{2,1,0:T(8,128)(2,1)} %shard_map.100), calls=%async_computation | async-start | bytes 720896 | tf_op jit(solution)/shard_map/all_to_all | solution.py:220
  13.3 82.3 %all-gather.4.cloned.1.call-start = ((), (), s32[]{:S(2)}) async-start(), calls=%async_computation.5 | async-start | bytes 1531904 | tf_op jit(solution)/shard_map/all_gather | solution.py:224
  20.0 9.6 %collective-permute-start = (bf16[4,352,128]{2,1,0:T(8,128)(2,1)S(1)}, bf16[4,352,128]{2,1,0:T(8,128)(2,1)S(1)}, u32[]{:S(2)}, u32[]{:S(2)}) collective-permute-start(bf16[4,352,128]{2,1,0:T(8,128)(2,1)S(1)} %all-to-all-done.mine.got), channel_id=1, source_target_pairs={{0,4},{4,0},{1,5},{5,1},{2,6},{6,2},{3,7},{7,3},{8,12},{12,8},{9,1... | collective-permute-start | bytes 1081352 | tf_op jit(solution)/shard_map/ppermute | solution.py:225
  69.1 48.6 %all-to-all-start.1 = ((f32[16,40,128]{2,1,0:T(8,128)}), f32[16,40,128]{2,1,0:T(8,128)S(1)}, u32[]{:S(2)}, u32[]{:S(2)}) async-start(f32[16,40,128]{2,1,0:T(8,128)} %shard_map.102), calls=%async_computation.1 | async-start | bytes 655360 | tf_op jit(solution)/shard_map/all_to_all | solution.py:232
  96.9 30.1 %copy-start.1 = (bf16[16,288,128]{2,1,0:T(8,128)(2,1)}, bf16[16,288,128]{2,1,0:T(8,128)(2,1)S(1)}, u32[]{:S(2)}) copy-start(bf16[16,288,128]{2,1,0:T(8,128)(2,1)S(1)} %slice.9.mine) | copy-start | bytes 3538948
  96.9 30.0 %collective-permute-start.2 = (bf16[16,288,128]{2,1,0:T(8,128)(2,1)S(1)}, bf16[16,288,128]{2,1,0:T(8,128)(2,1)}, u32[]{:S(2)}, u32[]{:S(2)}) collective-permute-start(bf16[16,288,128]{2,1,0:T(8,128)(2,1)S(1)} %slice.9.mine), channel_id=1, source_target_pairs={{0,24},{24,0},{8,16},{16,8},{1,25},{25,1},{9,17},{17,9},{2,26},{26... | collective-permute-start | bytes 3538952 | tf_op jit(solution)/shard_map/ppermute | solution.py:241
  102.6 15.1 %collective-permute-start.1 = (bf16[16,64,128]{2,1,0:T(8,128)(2,1)S(1)}, bf16[16,64,128]{2,1,0:T(8,128)(2,1)S(1)}, u32[]{:S(2)}, u32[]{:S(2)}) collective-permute-start(bf16[16,64,128]{2,1,0:T(8,128)(2,1)S(1)} %slice.8.mine), channel_id=1, source_target_pairs={{0,4},{4,0},{1,5},{5,1},{2,6},{6,2},{3,7},{7,3},{8,12},{12,8},{9,1... | collective-permute-start | bytes 786440 | tf_op jit(solution)/shard_map/ppermute | solution.py:240
  122.2 21.6 %copy-start.3 = (bf16[64,512]{1,0:T(8,128)(2,1)S(1)}, bf16[64,512]{1,0:T(8,128)(2,1)}, u32[]{:S(2)}) copy-start(bf16[64,512]{1,0:T(8,128)(2,1)} %param.13) | copy-start | bytes 196612
  122.2 21.4 %all-to-all-start.2 = ((bf16[16,64,512]{2,1,0:T(8,128)(2,1)}), bf16[16,64,512]{2,1,0:T(8,128)(2,1)S(1)}, u32[]{:S(2)}, u32[]{:S(2)}) async-start(bf16[16,64,512]{2,1,0:T(8,128)(2,1)} %shard_map.106), calls=%async_computation.2 | async-start | bytes 2097152 | tf_op jit(solution)/shard_map/all_to_all | solution.py:250
  127.0 21.9 %collective-permute-start.3 = (bf16[16,288,128]{2,1,0:T(8,128)(2,1)S(1)}, bf16[16,288,128]{2,1,0:T(8,128)(2,1)}, u32[]{:S(2)}, u32[]{:S(2)}) collective-permute-start(bf16[16,288,128]{2,1,0:T(8,128)(2,1)S(1)} %slice.9.mine), channel_id=1, source_target_pairs={{0,4},{4,0},{1,5},{5,1},{2,6},{6,2},{3,7},{7,3},{8,12},{12,8},{9,1... | collective-permute-start | bytes 3538952 | tf_op jit(solution)/shard_map/ppermute | solution.py:252
  130.6 18.3 %collective-permute-start.4 = (bf16[16,288,128]{2,1,0:T(8,128)(2,1)}, bf16[16,288,128]{2,1,0:T(8,128)(2,1)}, u32[]{:S(2)}, u32[]{:S(2)}) collective-permute-start(bf16[16,288,128]{2,1,0:T(8,128)(2,1)} %collective-permute-done.2.pair), channel_id=1, source_target_pairs={{0,4},{4,0},{1,5},{5,1},{2,6},{6,2},{3,7},{7,3},{8,12},{12,8},{9,1... | collective-permute-start | bytes 3538952 | tf_op jit(solution)/shard_map/ppermute | solution.py:253
  144.7 13.0 %all-to-all-start.3 = ((bf16[8,64,512]{2,1,0:T(8,128)(2,1)}), bf16[8,64,512]{2,1,0:T(8,128)(2,1)S(1)}, u32[]{:S(2)}, u32[]{:S(2)}) async-start(bf16[8,64,512]{2,1,0:T(8,128)(2,1)} %broadcast_in_dim.7), calls=%async_computation.3 | async-start | bytes 1048576 | tf_op jit(solution)/shard_map/all_to_all | solution.py:264
  157.7 0.8 copy-start.2
Sparse Core Ops, SparseCore 0:
  20.1 75.3 all-gather.3

commit v11 on v9

--- a/solution.py
+++ b/solution.py
@@ -65,7 +65,7 @@
     c = place[0]
     row = lax.broadcasted_iota(jnp.int32, (64, 64), 0)
     lane = lax.broadcasted_iota(jnp.int32, (64, 64), 1)
-    sizes = jnp.broadcast_to(lengths[...], (64, 64)).astype(F32)
+    sizes = jnp.broadcast_to(lengths[...], (64, 64))
     starts = jnp.sum(jnp.where(lane < row, sizes, 0.0), axis=1, keepdims=True)
     ends = jnp.sum(jnp.where(lane <= row, sizes, 0.0), axis=1, keepdims=True)
     starts, ends = (e.astype(jnp.int32) - place[1] * 512 for e in (starts, ends))
@@ -221,12 +221,13 @@
     got = lax.all_to_all(pack, y_axes, 0, 0)
     weights = lax.all_gather(got[:, 192:400], "z", axis=0)
     other = lax.ppermute(got, "c", [(0, 1), (1, 0)])
+    lengths = seg_lengths.astype(F32)
     place = jnp.stack([c, z]).astype(jnp.int32)
     mine = kernel_call(marks_body, shape((64, HEAD), F32), 3, core=place)(
-        got, other, seg_lengths[None, :]
+        got, other, lengths[None, :]
     )
     mine = jnp.sum(lax.all_gather(mine, "z", axis=0), axis=0)
-    marks = lax.all_gather(mine / seg_lengths.astype(F32)[:, None], "c", axis=0)
+    marks = lax.all_gather(mine / lengths[:, None], "c", axis=0)
     send = kernel_call(far_body, shape((16, 40, HEAD), F32), 3, core=c[None])(got, other, marks)
     parts = lax.all_to_all(send, "z", 0, 0)
     heads = kernel_call(

time: 176 us -> 176 us (level)
  no operation moved by 1% of the time
where the time goes in v11:
time: 176 us; the launch traced here: 175 us
  blocking collectives  94.9 us (54%)
  starting transfers between devices  26.4 us (15%)
  Pallas kernels  20.6 us (12%)
  between operations  13.5 us (8%)
  waiting for transfers between devices  13 us (7%)
  local copies, waits for them, and re-layouts  4.63 us (3%)
    all_gather x1, blocking collectives, on_device(): mine = jnp.sum(lax.all_gather(mine, 'z', axis=0), axis=0)  32.9 us
    all_to_all x1, blocking collectives, on_device(): parts = lax.all_to_all(terms, ('yl', 'x'), 0, 0)  12.6 us
    all_to_all x1, blocking collectives, on_device(): gathered = lax.all_to_all(gathered, (*y_axes, 'c'), 0, 0)  12.1 us
    all_to_all x1, blocking collectives, on_device(): got = lax.all_to_all(pack, y_axes, 0, 0)  11.3 us
    all_gather x1, blocking collectives, on_device(): heads = lax.all_gather(heads, y_axes, axis=0)  10.6 us
    all_to_all x1, blocking collectives, on_device(): parts = lax.all_to_all(terms, 'x', 0, 0)  9.7 us
    pallas_call x4, Pallas kernels, kernel_call(): return call if core is None else lambda *args: call(core, *args)  8.52 us
    ppermute x1, starting transfers between devices, on_device(): other = lax.ppermute(got, 'c', [(0, 1), (1, 0)])  8.35 us
  transfers between devices with their start and end apart: 6, of which 4 were waited for; matrix products, arithmetic and copies ran while one was open for 1% of the time, Pallas kernels for 7%

profile of v11, /device:TPU:1, one launch (start us, length us, event | category | flops | bytes accessed | tf_op | source)
XLA Modules:
  0.0 174.7 jit_solution(6972995507670351247)
XLA Ops:
  6.5 0.0 all-gather.5.cloned.1.call-start
  6.5 1.8 %shard_map.100 = bf16[4,400,128]{2,1,0:T(8,128)(2,1)} custom-call(bf16[64,512]{1,0:T(8,128)(2,1)} %queries.1, bf16[64,512]{1,0:T(8,128)(2,1)} %k.1, bf16[64,512]{1,0:T(8,128)(2,1)} %v.1, bf16[16,768]{1,0:T(8,128)(2,1)} %wg.1, bf16[16,768]{1,0:T(8,128)(2,1)} %wu.1, bf16[16,768]{1,0:T(8,128)(2,1)} %bitcast.15, bf16[16,512]{1,0:T(8,128)(2,1)} %bitcast.16), custom_call_target="tpu_custom_call" | custom-call | tf_op jit(solution)/shard_map/pallas_call | solution.py:218
  8.3 11.3 %all_to_all.30.mine = bf16[4,400,128]{2,1,0:T(8,128)(2,1)S(1)} all-to-all(bf16[4,400,128]{2,1,0:T(8,128)(2,1)} %shard_map.100), channel_id=1, replica_groups=mesh['z'=16,'yh'=2,'yl'=2,'c'=2,'x'=4] {'yh','yl'}, dimensions={0} | all-to-all | bytes 819200 | tf_op jit(solution)/shard_map/all_to_all | solution.py:221
  19.6 0.7 slice.8
  20.3 0.0 all-gather.5.cloned.1.call-update
  20.3 8.4 %collective-permute-start = (bf16[4,400,128]{2,1,0:T(8,128)(2,1)S(1)}, bf16[4,400,128]{2,1,0:T(8,128)(2,1)S(1)}, u32[]{:S(2)}, u32[]{:S(2)}) collective-permute-start(bf16[4,400,128]{2,1,0:T(8,128)(2,1)S(1)} %all_to_all.30.mine), channel_id=1, source_target_pairs={{0,4},{4,0},{1,5},{5,1},{2,6},{6,2},{3,7},{7,3},{8,12},{12,8},{9,1... | collective-permute-start | bytes 1228808 | tf_op jit(solution)/shard_map/ppermute | solution.py:223
  28.7 0.1 pad_add_fusion.place
  28.8 0.7 fusion
  29.4 0.6 collective-permute-done.other
  30.1 0.8 shard_map.101
  30.8 32.9 %all-gather = f32[1024,128]{1,0:T(8,128)S(1)} all-gather(f32[64,128]{1,0:T(8,128)S(1)} %shard_map.101), channel_id=2, replica_groups=mesh['z'=16,'yh'=2,'yl'=2,'c'=2,'x'=4] {'z'}, dimensions={0}, use_global_device_ids=true | all-gather | bytes 557056 | tf_op jit(solution)/shard_map/all_gather | solution.py:229
  63.8 0.0 copy-start
  63.8 0.1 bitcast_divide_fusion
  63.9 5.7 %all_gather.24.marks = f32[2,64,128]{2,1,0:T(8,128)S(1)} all-gather(f32[1,64,128]{2,1,0:T(8,128)S(1)} %bitcast_divide_fusion), channel_id=1, replica_groups=mesh['z'=16,'yh'=2,'yl'=2,'c'=2,'x'=4] {'c'}, dimensions={0}, use_global_device_ids=true | all-gather | bytes 98304 | tf_op jit(solution)/shard_map/all_gather | solution.py:230
  69.5 1.4 shard_map.102
  70.9 7.0 %all-to-all-start.1 = ((f32[16,40,128]{2,1,0:T(8,128)}), f32[16,40,128]{2,1,0:T(8,128)S(1)}, u32[]{:S(2)}, u32[]{:S(2)}) async-start(f32[16,40,128]{2,1,0:T(8,128)} %shard_map.102), calls=%async_computation.1 | async-start | bytes 655360 | tf_op jit(solution)/shard_map/all_to_all | solution.py:232
  78.0 4.5 %shard_map.103 = f32[2,64,128]{2,1,0:T(8,128)S(1)} custom-call(f32[2,64,128]{2,1,0:T(8,128)S(1)} %all_gather.24.marks), custom_call_target="tpu_custom_call" | custom-call | flops 1000000000 | bytes 20000000 | tf_op jit(solution)/shard_map/pallas_call | solution.py:233
  82.5 10.6 %all-gather.1 = f32[8,64,128]{2,1,0:T(8,128)S(1)} all-gather(f32[2,64,128]{2,1,0:T(8,128)S(1)} %shard_map.103), channel_id=3, replica_groups=mesh['z'=16,'yh'=2,'yl'=2,'c'=2,'x'=4] {'yh','yl'}, dimensions={0}, use_global_device_ids=true | all-gather | bytes 327680 | tf_op jit(solution)/shard_map/all_gather | solution.py:239
  93.1 0.0 copy-done
  93.1 0.5 shard_map.104.near
  93.6 0.0 copy-start.2
  93.6 6.8 %all-to-all-done.1.parts = f32[16,40,128]{2,1,0:T(8,128)S(1)} async-done(((f32[16,40,128]{2,1,0:T(8,128)}), f32[16,40,128]{2,1,0:T(8,128)S(1)}, u32[]{:S(2)}, u32[]{:S(2)}) %all-to-all-start.1) | async-done | bytes 327712 | tf_op jit(solution)/shard_map/all_to_all | solution.py:232
  100.4 0.2 shard_map.105
  100.6 12.1 %all_to_all.31.gathered = f32[8,32,128]{2,1,0:T(8,128)S(1)} all-to-all(f32[8,32,128]{2,1,0:T(8,128)S(1)} %shard_map.105), channel_id=1, replica_groups=mesh['z'=16,'yh'=2,'yl'=2,'c'=2,'x'=4] {'yh','yl','c'}, dimensions={0} | all-to-all | bytes 262144 | tf_op jit(solution)/shard_map/all_to_all | solution.py:243
  112.7 0.0 all-gather.5.cloned.1.call-done
  112.7 1.3 slice.7.mine
  114.1 4.6 %collective-permute-start.1 = (bf16[16,4,64,128]{3,2,1,0:T(8,128)(2,1)S(1)}, bf16[16,4,64,128]{3,2,1,0:T(8,128)(2,1)S(1)}, u32[]{:S(2)}, u32[]{:S(2)}) collective-permute-start(bf16[16,4,64,128]{3,2,1,0:T(8,128)(2,1)S(1)} %slice.7.mine), channel_id=1, source_target_pairs={{0,4},{4,0},{1,5},{5,1},{2,6},{6,2},{3,7},{7,3},{8,12},{12,8},{9,1... | collective-permute-start | bytes 3145736 | tf_op jit(solution)/shard_map/ppermute | solution.py:246
  118.6 2.3 %collective-permute-done.1.other = bf16[16,4,64,128]{3,2,1,0:T(8,128)(2,1)S(1)} collective-permute-done((bf16[16,4,64,128]{3,2,1,0:T(8,128)(2,1)S(1)}, bf16[16,4,64,128]{3,2,1,0:T(8,128)(2,1)S(1)}, u32[]{:S(2)}, u32[]{:S(2)}) %collective-permute-start.1) | collective-permute-done | bytes 1048608 | tf_op jit(solution)/shard_map/ppermute | solution.py:246
  120.9 1.3 shard_map.106
  122.2 2.3 %collective-permute-start.2 = (bf16[16,4,208,128]{3,2,1,0:T(8,128)(2,1)}, bf16[16,4,208,128]{3,2,1,0:T(8,128)(2,1)S(1)}, u32[]{:S(2)}, u32[]{:S(2)}) collective-permute-start(bf16[16,4,208,128]{3,2,1,0:T(8,128)(2,1)} %bitcast.8.mine), channel_id=1, source_target_pairs={{0,4},{4,0},{1,5},{5,1},{2,6},{6,2},{3,7},{7,3},{8,12},{12,8},{9,1... | collective-permute-start | bytes 10223624 | tf_op jit(solution)/shard_map/ppermute | solution.py:255
  124.4 9.7 %all_to_all.32 = bf16[4,64,512]{2,1,0:T(8,128)(2,1)S(1)} all-to-all(bf16[4,64,512]{2,1,0:T(8,128)(2,1)S(1)} %shard_map.106), channel_id=1, replica_groups=mesh['z'=16,'yh'=2,'yl'=2,'c'=2,'x'=4] {'x'}, dimensions={0} | all-to-all | bytes 524288 | tf_op jit(solution)/shard_map/all_to_all | solution.py:256
  134.2 0.0 copy-done.2
  134.2 0.9 broadcast_in_dim.20
  135.1 4.1 %all-to-all-start.4 = ((bf16[8,64,512]{2,1,0:T(8,128)(2,1)}), bf16[8,64,512]{2,1,0:T(8,128)(2,1)}, u32[]{:S(2)}, u32[]{:S(2)}) async-start(bf16[8,64,512]{2,1,0:T(8,128)(2,1)} %broadcast_in_dim.20), calls=%async_computation.4 | async-start | bytes 1048576 | tf_op jit(solution)/shard_map/all_to_all | solution.py:267
  139.2 0.0 collective-permute-done.2.other
  139.2 0.0 copy-start.1
  139.2 1.8 %copy-done.1 = bf16[16,4,208,128]{3,2,1,0:T(8,128)(2,1)} copy-done((bf16[16,4,208,128]{3,2,1,0:T(8,128)(2,1)}, bf16[16,4,208,128]{3,2,1,0:T(8,128)(2,1)S(1)}, u32[]{:S(2)}) %copy-start.1) | copy-done | bytes 3407896
  141.0 5.1 %shard_map.107 = (bf16[2048,768]{1,0:T(8,128)(2,1)}, bf16[2048,384]{1,0:T(8,128)(2,1)}) custom-call(s32[1]{0:T(128)} %bitcast.core, bf16[16,4,208,128]{3,2,1,0:T(8,128)(2,1)} %bitcast.8.mine, bf16[16,4,208,128]{3,2,1,0:T(8,128)(2,1)} %copy-done.1), custom_call_target="tpu_custom_call" | custom-call | tf_op jit(solution)/shard_map/pallas_call | solution.py:42
  146.1 3.3 %all-to-all-done.4.whole = bf16[8,64,512]{2,1,0:T(8,128)(2,1)} async-done(((bf16[8,64,512]{2,1,0:T(8,128)(2,1)}), bf16[8,64,512]{2,1,0:T(8,128)(2,1)}, u32[]{:S(2)}, u32[]{:S(2)}) %all-to-all-start.4) | async-done | bytes 524320 | tf_op jit(solution)/shard_map/all_to_all | solution.py:267
  149.4 5.1 %shard_map.108 = bf16[8,64,512]{2,1,0:T(8,128)(2,1)} custom-call(bf16[8,64,512]{2,1,0:T(8,128)(2,1)} %all-to-all-done.4.whole, f32[1,2048]{1,0:T(1,128)} %bitcast.17, bf16[2048,768]{1,0:T(8,128)(2,1)} %get-tuple-element.21.far1, bf16[2048,384]{1,0:T(8,128)(2,1)} %get-tuple-element.22.far2), custom_call_target="tpu_custom_call" | custom-call | tf_op jit(solution)/shard_map/pallas_call | solution.py:268
  154.5 12.6 %all_to_all.33 = bf16[8,64,512]{2,1,0:T(8,128)(2,1)S(1)} all-to-all(bf16[8,64,512]{2,1,0:T(8,128)(2,1)} %shard_map.108), channel_id=1, replica_groups=mesh['z'=16,'yh'=2,'yl'=2,'c'=2,'x'=4] {'yl','x'}, dimensions={0} | all-to-all | bytes 1048576 | tf_op jit(solution)/shard_map/all_to_all | solution.py:281
  167.1 0.1 convert_reduce_fusion
  167.2 0.6 add_convert_fusion
  (3 shorter events, 0.1 us)
Async XLA Ops:
  6.5 106.2 %all-gather.5.cloned.1.call-start = ((), (), s32[]{:S(2)}) async-start(), calls=%async_computation.6 | async-start | bytes 3620864 | tf_op jit(solution)/shard_map/all_gather | solution.py:222
  20.3 9.7 %collective-permute-start = (bf16[4,400,128]{2,1,0:T(8,128)(2,1)S(1)}, bf16[4,400,128]{2,1,0:T(8,128)(2,1)S(1)}, u32[]{:S(2)}, u32[]{:S(2)}) collective-permute-start(bf16[4,400,128]{2,1,0:T(8,128)(2,1)S(1)} %all_to_all.30.mine), channel_id=1, source_target_pairs={{0,4},{4,0},{1,5},{5,1},{2,6},{6,2},{3,7},{7,3},{8,12},{12,8},{9,1... | collective-permute-start | bytes 1228808 | tf_op jit(solution)/shard_map/ppermute | solution.py:223
  63.8 29.3 %copy-start = (bf16[64,512]{1,0:T(8,128)(2,1)S(1)}, bf16[64,512]{1,0:T(8,128)(2,1)}, u32[]{:S(2)}) copy-start(bf16[64,512]{1,0:T(8,128)(2,1)} %queries.1) | copy-start | bytes 196612
  70.9 29.5 %all-to-all-start.1 = ((f32[16,40,128]{2,1,0:T(8,128)}), f32[16,40,128]{2,1,0:T(8,128)S(1)}, u32[]{:S(2)}, u32[]{:S(2)}) async-start(f32[16,40,128]{2,1,0:T(8,128)} %shard_map.102), calls=%async_computation.1 | async-start | bytes 655360 | tf_op jit(solution)/shard_map/all_to_all | solution.py:232
  93.6 40.6 %copy-start.2 = (bf16[64,512]{1,0:T(8,128)(2,1)S(1)}, bf16[64,512]{1,0:T(8,128)(2,1)}, u32[]{:S(2)}) copy-start(bf16[64,512]{1,0:T(8,128)(2,1)} %param.13) | copy-start | bytes 196612
  114.1 6.8 %collective-permute-start.1 = (bf16[16,4,64,128]{3,2,1,0:T(8,128)(2,1)S(1)}, bf16[16,4,64,128]{3,2,1,0:T(8,128)(2,1)S(1)}, u32[]{:S(2)}, u32[]{:S(2)}) collective-permute-start(bf16[16,4,64,128]{3,2,1,0:T(8,128)(2,1)S(1)} %slice.7.mine), channel_id=1, source_target_pairs={{0,4},{4,0},{1,5},{5,1},{2,6},{6,2},{3,7},{7,3},{8,12},{12,8},{9,1... | collective-permute-start | bytes 3145736 | tf_op jit(solution)/shard_map/ppermute | solution.py:246
  122.2 17.1 %collective-permute-start.2 = (bf16[16,4,208,128]{3,2,1,0:T(8,128)(2,1)}, bf16[16,4,208,128]{3,2,1,0:T(8,128)(2,1)S(1)}, u32[]{:S(2)}, u32[]{:S(2)}) collective-permute-start(bf16[16,4,208,128]{3,2,1,0:T(8,128)(2,1)} %bitcast.8.mine), channel_id=1, source_target_pairs={{0,4},{4,0},{1,5},{5,1},{2,6},{6,2},{3,7},{7,3},{8,12},{12,8},{9,1... | collective-permute-start | bytes 10223624 | tf_op jit(solution)/shard_map/ppermute | solution.py:255
  135.1 14.4 %all-to-all-start.4 = ((bf16[8,64,512]{2,1,0:T(8,128)(2,1)}), bf16[8,64,512]{2,1,0:T(8,128)(2,1)}, u32[]{:S(2)}, u32[]{:S(2)}) async-start(bf16[8,64,512]{2,1,0:T(8,128)(2,1)} %broadcast_in_dim.20), calls=%async_computation.4 | async-start | bytes 1048576 | tf_op jit(solution)/shard_map/all_to_all | solution.py:267
  139.2 1.8 %copy-start.1 = (bf16[16,4,208,128]{3,2,1,0:T(8,128)(2,1)}, bf16[16,4,208,128]{3,2,1,0:T(8,128)(2,1)S(1)}, u32[]{:S(2)}) copy-start(bf16[16,4,208,128]{3,2,1,0:T(8,128)(2,1)S(1)} %collective-permute-done.2.other) | copy-start | bytes 10223620
Sparse Core Ops, SparseCore 0:
  20.5 87.1 all-gather.4

commit v12 on v11

--- a/solution.py
+++ b/solution.py
@@ -2,6 +2,7 @@
 
 import jax
 import jax.numpy as jnp
+import numpy as np
 from jax import lax
 from jax.experimental import pallas as pl
 from jax.experimental.pallas import tpu as pltpu
@@ -176,18 +177,28 @@
             unmix(raw.at[i], 6 + t, w2, slice(t * 128, t * 128 + 128), c)
 
 
-def proj_body(core, near, heads, gathered, mine, other, out, wo):
-    for t in range(4):
-        lanes = slice(t * 128, t * 128 + 128)
-        unmix(mine, t, wo, lanes, core[0])
-        unmix(other, t, wo, lanes, 1 - core[0])
-    attn = []
+def attn_body(near, heads, gathered, out):
     for h in range(4):
         rows = jnp.concatenate([gathered[2 * h], gathered[2 * h + 1]], axis=0)
         mixer = dot(heads[h, 1][:, :64], rows, ((1,), (0,)), HI)
-        attn.append(dot(near[h][:, :64], mixer, ((1,), (0,)), HI).astype(BF16))
-    attn = jnp.concatenate(attn, axis=-1)
-    spread(dot(attn, wo[...], ((1,), (1,))), out)
+        attn = dot(near[h][:, :64], mixer, ((1,), (0,)), HI)
+        out[:, h * HEAD : h * HEAD + HEAD] = attn.astype(BF16)
+
+
+def proj_body(core, mine, other, weights, out, raw, wo, sem):
+    copy = pltpu.make_async_copy(weights.at[:, :, 0:64], raw, sem)
+    copy.start()
+    copy.wait()
+    for z in range(16):
+        for y in range(4):
+            low = (z * 4 + y) * 16
+            for t in range(4):
+                lanes = slice(t * 128, t * 128 + 128)
+                wo[low : low + 16, lanes] = raw[z, y, t * 16 : t * 16 + 16, :]
+    for attn, c in ((mine, core[0]), (other, 1 - core[0])):
+        terms = dot(attn[...], wo[...], ((1,), (1,)))
+        for x in range(4):
+            out[c * 4 + x] = terms[:, x * 256 : x * 256 + 256].astype(BF16)
 
 
 def ffn_body(whole, gain, far1, far2, out, normed, w1, w2, sems):
@@ -241,19 +252,25 @@
     parts, near, heads = lax.optimization_barrier((parts, near, heads))
     gathered = kernel_call(merge_body, shape((8, 32, HEAD), F32), 1)(parts)
     gathered = lax.all_to_all(gathered, (*y_axes, "c"), 0, 0)
-    weights, gathered = lax.optimization_barrier((weights, gathered))
-    w_out = weights[:, :, 0:64]
-    swapped = lax.ppermute(w_out, "c", [(0, 1), (1, 0)])
+    attn = kernel_call(attn_body, shape((64, 512), BF16), 3)(near, heads, gathered)
+    attn_other = lax.ppermute(attn, "c", [(0, 1), (1, 0)])
+    weights, attn_other = lax.optimization_barrier((weights, attn_other))
     terms = kernel_call(
         proj_body,
-        shape((4, 64, 512), BF16),
-        5,
-        [pltpu.VMEM((2048, 512), BF16)],
+        shape((8, 64, 256), BF16),
+        2,
+        [
+            pltpu.VMEM((16, 4, 64, 128), BF16),
+            pltpu.VMEM((1024, 512), BF16),
+            pltpu.SemaphoreType.DMA(()),
+        ],
         core=c[None],
-    )(near, heads, gathered, w_out, swapped)
+        n_far=1,
+        grant=LARGE,
+    )(attn, attn_other, weights)
     terms, weights = lax.optimization_barrier((terms, weights))
     swapped = lax.ppermute(weights, "c", [(0, 1), (1, 0)])
-    parts = lax.all_to_all(terms, "x", 0, 0)
+    parts = lax.all_to_all(terms, ("c", "x"), 0, 0)
     w1, w2 = kernel_call(
         unmix_body,
         [shape((2048, 768), BF16), shape((2048, 384), BF16)],
@@ -263,7 +280,12 @@
         n_far=2,
         grant=LARGE,
     )(weights, swapped)
-    resid = (stream.astype(F32) + jnp.sum(parts.astype(F32), axis=0)).astype(BF16)
+    halves = jnp.sum(parts.reshape(2, 4, 64, 256).astype(F32), axis=1)
+    at = np.arange(256, dtype=np.int32)
+    at = (at // 16) * 32 + at % 16 + 16 * np.arange(2, dtype=np.int32)[:, None]
+    order = (at[:, :, None] == jnp.arange(512, dtype=jnp.int32)).astype(F32)
+    proj = jnp.einsum("ctk,ckf->tf", halves, order, precision=HI, preferred_element_type=F32)
+    resid = (stream.astype(F32) + proj).astype(BF16)
     whole = lax.all_to_all(jnp.broadcast_to(resid[None], (8, 64, 512)), ("yl", "x"), 0, 0)
     terms = kernel_call(
         ffn_body,

time: 176 us -> 177 us (level)
  Pallas kernels: 20.6 us -> 23.8 us
  local copies, waits for them, and re-layouts: 4.63 us -> 2.2 us
  starting transfers between devices: 26.4 us -> 24.6 us
    pallas_call x4, Pallas kernels: 8.52 us -> 11.2 us  [kernel_call(): return call if core is None else lambda *args: call(core, *args)]
    all_to_all x1, waiting for transfers between devices: 3.33 us -> 5.2 us  [on_device(): lax.all_to_all(jnp.broadcast_to(resid[None], (8, 64, 512)), ('yl', 'x'),...]
    ppermute x1, starting transfers between devices: 4.55 us -> 2.77 us  [on_device(): attn_other = lax.ppermute(attn, 'c', [(0, 1), (1, 0)])]
  transfers between devices with their start and end apart: 6 -> 6, of which waited for: 4 -> 4; matrix products, arithmetic and copies ran while one was open for 1% -> 2% of each run, Pallas kernels for 7% -> 7%
where the time goes in v12:
time: 177 us; the launch traced here: 176 us
  blocking collectives  95.6 us (54%)
  starting transfers between devices  24.6 us (14%)
  Pallas kernels  23.8 us (13%)
  waiting for transfers between devices  13.5 us (8%)
  between operations  13.5 us (8%)
  local copies, waits for them, and re-layouts  2.2 us (1%)
    all_gather x1, blocking collectives, on_device(): mine = jnp.sum(lax.all_gather(mine, 'z', axis=0), axis=0)  32.9 us
    all_to_all x1, blocking collectives, on_device(): parts = lax.all_to_all(terms, ('yl', 'x'), 0, 0)  12.5 us
    all_to_all x1, blocking collectives, on_device(): gathered = lax.all_to_all(gathered, (*y_axes, 'c'), 0, 0)  12.1 us
    all_to_all x1, blocking collectives, on_device(): got = lax.all_to_all(pack, y_axes, 0, 0)  11.3 us
    pallas_call x4, Pallas kernels, kernel_call(): return call if core is None else lambda *args: call(core, *args)  11.2 us
    all_gather x1, blocking collectives, on_device(): heads = lax.all_gather(heads, y_axes, axis=0)  10.6 us
    all_to_all x1, blocking collectives, on_device(): parts = lax.all_to_all(terms, ('c', 'x'), 0, 0)  10.5 us
    ppermute x1, starting transfers between devices, on_device(): other = lax.ppermute(got, 'c', [(0, 1), (1, 0)])  8.35 us
  transfers between devices with their start and end apart: 6, of which 4 were waited for; matrix products, arithmetic and copies ran while one was open for 2% of the time, Pallas kernels for 7%

profile of v12, /device:TPU:1, one launch (start us, length us, event | category | flops | bytes accessed | tf_op | source)
XLA Modules:
  0.0 176.2 jit_solution(15912337719838421543)
XLA Ops:
  6.5 0.0 all-gather.5.cloned.1.call-start
  6.5 1.7 shard_map.109
  8.3 11.3 %all_to_all.30.mine = bf16[4,400,128]{2,1,0:T(8,128)(2,1)S(1)} all-to-all(bf16[4,400,128]{2,1,0:T(8,128)(2,1)} %shard_map.109), channel_id=1, replica_groups=mesh['z'=16,'yh'=2,'yl'=2,'c'=2,'x'=4] {'yh','yl'}, dimensions={0} | all-to-all | bytes 819200 | tf_op jit(solution)/shard_map/all_to_all | solution.py:232
  19.6 0.7 slice.4
  20.3 0.0 all-gather.5.cloned.1.call-update
  20.3 8.4 %collective-permute-start = (bf16[4,400,128]{2,1,0:T(8,128)(2,1)S(1)}, bf16[4,400,128]{2,1,0:T(8,128)(2,1)S(1)}, u32[]{:S(2)}, u32[]{:S(2)}) collective-permute-start(bf16[4,400,128]{2,1,0:T(8,128)(2,1)S(1)} %all_to_all.30.mine), channel_id=1, source_target_pairs={{0,4},{4,0},{1,5},{5,1},{2,6},{6,2},{3,7},{7,3},{8,12},{12,8},{9,1... | collective-permute-start | bytes 1228808 | tf_op jit(solution)/shard_map/ppermute | solution.py:234
  28.7 0.1 pad_add_fusion.place
  28.8 0.7 fusion.3
  29.4 0.6 collective-permute-done.other
  30.0 0.8 shard_map.110
  30.8 32.9 %all-gather = f32[1024,128]{1,0:T(8,128)S(1)} all-gather(f32[64,128]{1,0:T(8,128)S(1)} %shard_map.110), channel_id=2, replica_groups=mesh['z'=16,'yh'=2,'yl'=2,'c'=2,'x'=4] {'z'}, dimensions={0}, use_global_device_ids=true | all-gather | bytes 557056 | tf_op jit(solution)/shard_map/all_gather | solution.py:240
  63.8 0.0 copy-start.1
  63.8 0.1 bitcast_divide_fusion
  63.9 5.7 %all_gather.24.marks = f32[2,64,128]{2,1,0:T(8,128)S(1)} all-gather(f32[1,64,128]{2,1,0:T(8,128)S(1)} %bitcast_divide_fusion), channel_id=1, replica_groups=mesh['z'=16,'yh'=2,'yl'=2,'c'=2,'x'=4] {'c'}, dimensions={0}, use_global_device_ids=true | all-gather | bytes 98304 | tf_op jit(solution)/shard_map/all_gather | solution.py:241
  69.5 1.4 shard_map.111
  70.9 7.0 %all-to-all-start.1 = ((f32[16,40,128]{2,1,0:T(8,128)}), f32[16,40,128]{2,1,0:T(8,128)S(1)}, u32[]{:S(2)}, u32[]{:S(2)}) async-start(f32[16,40,128]{2,1,0:T(8,128)} %shard_map.111), calls=%async_computation.1 | async-start | bytes 655360 | tf_op jit(solution)/shard_map/all_to_all | solution.py:243
  78.0 4.5 %shard_map.112 = f32[2,64,128]{2,1,0:T(8,128)S(1)} custom-call(f32[2,64,128]{2,1,0:T(8,128)S(1)} %all_gather.24.marks), custom_call_target="tpu_custom_call" | custom-call | flops 1000000000 | bytes 20000000 | tf_op jit(solution)/shard_map/pallas_call | solution.py:244
  82.5 0.0 copy-start.4
  82.5 10.6 %all-gather.1 = f32[8,64,128]{2,1,0:T(8,128)S(1)} all-gather(f32[2,64,128]{2,1,0:T(8,128)S(1)} %shard_map.112), channel_id=3, replica_groups=mesh['z'=16,'yh'=2,'yl'=2,'c'=2,'x'=4] {'yh','yl'}, dimensions={0}, use_global_device_ids=true | all-gather | bytes 327680 | tf_op jit(solution)/shard_map/all_gather | solution.py:250
  93.1 0.0 copy-done.1
  93.1 0.5 shard_map.113.near
  93.6 6.8 %all-to-all-done.1.parts = f32[16,40,128]{2,1,0:T(8,128)S(1)} async-done(((f32[16,40,128]{2,1,0:T(8,128)}), f32[16,40,128]{2,1,0:T(8,128)S(1)}, u32[]{:S(2)}, u32[]{:S(2)}) %all-to-all-start.1) | async-done | bytes 327712 | tf_op jit(solution)/shard_map/all_to_all | solution.py:243
  100.4 0.2 shard_map.114
  100.6 12.1 %all_to_all.31.gathered = f32[8,32,128]{2,1,0:T(8,128)S(1)} all-to-all(f32[8,32,128]{2,1,0:T(8,128)S(1)} %shard_map.114), channel_id=1, replica_groups=mesh['z'=16,'yh'=2,'yl'=2,'c'=2,'x'=4] {'yh','yl','c'}, dimensions={0} | all-to-all | bytes 262144 | tf_op jit(solution)/shard_map/all_to_all | solution.py:254
  112.7 0.5 shard_map.115.mine
  113.2 0.0 copy-start
  113.2 2.8 %collective-permute-start.1 = (bf16[64,512]{1,0:T(8,128)(2,1)S(1)}, bf16[64,512]{1,0:T(8,128)(2,1)S(1)}, u32[]{:S(2)}, u32[]{:S(2)}) collective-permute-start(bf16[64,512]{1,0:T(8,128)(2,1)S(1)} %shard_map.115.mine), channel_id=1, source_target_pairs={{0,4},{4,0},{1,5},{5,1},{2,6},{6,2},{3,7},{7,3},{8,12},{12,8},{9,1... | collective-permute-start | bytes 196616 | tf_op jit(solution)/shard_map/ppermute | solution.py:256
  116.0 0.9 collective-permute-done.1.other
  116.9 0.0 copy-start.3
  116.9 0.0 all-gather.5.cloned.1.call-done
  116.9 0.0 copy-start.2
  116.9 0.0 copy-done
  116.9 0.6 copy-done.3
  117.5 3.9 %shard_map.116 = bf16[8,64,256]{2,1,0:T(8,128)(2,1)} custom-call(s32[1]{0:T(128)} %bitcast.core, bf16[64,512]{1,0:T(8,128)(2,1)} %copy-done, bf16[64,512]{1,0:T(8,128)(2,1)} %copy-done.3, bf16[16,4,208,128]{3,2,1,0:T(8,128)(2,1)} %bitcast.24), custom_call_target="tpu_custom_call" | custom-call | tf_op jit(solution)/shard_map/pallas_call | solution.py:43
  121.5 0.0 copy-done.2
  121.5 2.3 %collective-permute-start.2 = (bf16[16,4,208,128]{3,2,1,0:T(8,128)(2,1)S(1)}, bf16[16,4,208,128]{3,2,1,0:T(8,128)(2,1)}, u32[]{:S(2)}, u32[]{:S(2)}) collective-permute-start(bf16[16,4,208,128]{3,2,1,0:T(8,128)(2,1)S(1)} %bitcast.26), channel_id=1, source_target_pairs={{0,4},{4,0},{1,5},{5,1},{2,6},{6,2},{3,7},{7,3},{8,12},{12,8},{9,1... | collective-permute-start | bytes 10223624 | tf_op jit(solution)/shard_map/ppermute | solution.py:272
  123.7 10.5 %all_to_all.32 = bf16[8,64,256]{2,1,0:T(8,128)(2,1)S(1)} all-to-all(bf16[8,64,256]{2,1,0:T(8,128)(2,1)} %shard_map.116), channel_id=1, replica_groups=mesh['z'=16,'yh'=2,'yl'=2,'c'=2,'x'=4] {'c','x'}, dimensions={0} | all-to-all | bytes 524288 | tf_op jit(solution)/shard_map/all_to_all | solution.py:273
  134.3 0.0 copy-done.4
  134.3 1.4 fusion.1
  135.7 0.8 broadcast_in_dim.10
  136.5 4.1 %all-to-all-start.4 = ((bf16[8,64,512]{2,1,0:T(8,128)(2,1)}), bf16[8,64,512]{2,1,0:T(8,128)(2,1)}, u32[]{:S(2)}, u32[]{:S(2)}) async-start(bf16[8,64,512]{2,1,0:T(8,128)(2,1)} %broadcast_in_dim.10), calls=%async_computation.4 | async-start | bytes 1048576 | tf_op jit(solution)/shard_map/all_to_all | solution.py:289
  140.7 0.0 collective-permute-done.2.other
  140.7 5.1 %shard_map.117 = (bf16[2048,768]{1,0:T(8,128)(2,1)}, bf16[2048,384]{1,0:T(8,128)(2,1)}) custom-call(s32[1]{0:T(128)} %bitcast.core, bf16[16,4,208,128]{3,2,1,0:T(8,128)(2,1)} %bitcast.25, bf16[16,4,208,128]{3,2,1,0:T(8,128)(2,1)} %collective-permute-done.2.other), custom_call_target="tpu_custom_call" | custom-call | tf_op jit(solution)/shard_map/pallas_call | solution.py:43
  145.8 5.2 %all-to-all-done.4.whole = bf16[8,64,512]{2,1,0:T(8,128)(2,1)} async-done(((bf16[8,64,512]{2,1,0:T(8,128)(2,1)}), bf16[8,64,512]{2,1,0:T(8,128)(2,1)}, u32[]{:S(2)}, u32[]{:S(2)}) %all-to-all-start.4) | async-done | bytes 524320 | tf_op jit(solution)/shard_map/all_to_all | solution.py:289
  151.0 5.1 %shard_map.118 = bf16[8,64,512]{2,1,0:T(8,128)(2,1)} custom-call(bf16[8,64,512]{2,1,0:T(8,128)(2,1)} %all-to-all-done.4.whole, f32[1,2048]{1,0:T(1,128)} %bitcast.30, bf16[2048,768]{1,0:T(8,128)(2,1)} %get-tuple-element.21.far1, bf16[2048,384]{1,0:T(8,128)(2,1)} %get-tuple-element.22.far2), custom_call_target="tpu_custom_call" | custom-call | tf_op jit(solution)/shard_map/pallas_call | solution.py:290
  156.1 12.5 %all_to_all.33 = bf16[8,64,512]{2,1,0:T(8,128)(2,1)S(1)} all-to-all(bf16[8,64,512]{2,1,0:T(8,128)(2,1)} %shard_map.118), channel_id=1, replica_groups=mesh['z'=16,'yh'=2,'yl'=2,'c'=2,'x'=4] {'yl','x'}, dimensions={0} | all-to-all | bytes 1048576 | tf_op jit(solution)/shard_map/all_to_all | solution.py:303
  168.6 0.1 convert_reduce_fusion
  168.7 0.6 add_convert_fusion
  (2 shorter events, 0.1 us)
Async XLA Ops:
  6.5 110.4 %all-gather.5.cloned.1.call-start = ((), (), s32[]{:S(2)}) async-start(), calls=%async_computation.6 | async-start | bytes 3620864 | tf_op jit(solution)/shard_map/all_gather | solution.py:233
  20.3 9.7 %collective-permute-start = (bf16[4,400,128]{2,1,0:T(8,128)(2,1)S(1)}, bf16[4,400,128]{2,1,0:T(8,128)(2,1)S(1)}, u32[]{:S(2)}, u32[]{:S(2)}) collective-permute-start(bf16[4,400,128]{2,1,0:T(8,128)(2,1)S(1)} %all_to_all.30.mine), channel_id=1, source_target_pairs={{0,4},{4,0},{1,5},{5,1},{2,6},{6,2},{3,7},{7,3},{8,12},{12,8},{9,1... | collective-permute-start | bytes 1228808 | tf_op jit(solution)/shard_map/ppermute | solution.py:234
  63.8 29.3 %copy-start.1 = (bf16[64,512]{1,0:T(8,128)(2,1)S(1)}, bf16[64,512]{1,0:T(8,128)(2,1)}, u32[]{:S(2)}) copy-start(bf16[64,512]{1,0:T(8,128)(2,1)} %queries.1) | copy-start | bytes 196612
  70.9 29.4 %all-to-all-start.1 = ((f32[16,40,128]{2,1,0:T(8,128)}), f32[16,40,128]{2,1,0:T(8,128)S(1)}, u32[]{:S(2)}, u32[]{:S(2)}) async-start(f32[16,40,128]{2,1,0:T(8,128)} %shard_map.111), calls=%async_computation.1 | async-start | bytes 655360 | tf_op jit(solution)/shard_map/all_to_all | solution.py:243
  82.5 51.8 %copy-start.4 = (s32[2,256]{1,0:T(2,128)S(1)}, s32[2,256]{1,0:T(2,128)}, u32[]{:S(2)}) copy-start(s32[2,256]{1,0:T(2,128)} %constant.25) | copy-start | bytes 6148
  113.2 3.7 %copy-start = (bf16[64,512]{1,0:T(8,128)(2,1)}, bf16[64,512]{1,0:T(8,128)(2,1)S(1)}, u32[]{:S(2)}) copy-start(bf16[64,512]{1,0:T(8,128)(2,1)S(1)} %shard_map.115.mine) | copy-start | bytes 196612
  113.2 3.7 %collective-permute-start.1 = (bf16[64,512]{1,0:T(8,128)(2,1)S(1)}, bf16[64,512]{1,0:T(8,128)(2,1)S(1)}, u32[]{:S(2)}, u32[]{:S(2)}) collective-permute-start(bf16[64,512]{1,0:T(8,128)(2,1)S(1)} %shard_map.115.mine), channel_id=1, source_target_pairs={{0,4},{4,0},{1,5},{5,1},{2,6},{6,2},{3,7},{7,3},{8,12},{12,8},{9,1... | collective-permute-start | bytes 196616 | tf_op jit(solution)/shard_map/ppermute | solution.py:256
  116.9 0.6 copy-start.3
  116.9 4.6 %copy-start.2 = (bf16[64,208,128]{2,1,0:T(8,128)(2,1)S(1)}, bf16[64,208,128]{2,1,0:T(8,128)(2,1)}, u32[]{:S(2)}) copy-start(bf16[64,208,128]{2,1,0:T(8,128)(2,1)} %all-gather.5.cloned.1.call-done) | copy-start | bytes 10223620
  121.5 19.2 %collective-permute-start.2 = (bf16[16,4,208,128]{3,2,1,0:T(8,128)(2,1)S(1)}, bf16[16,4,208,128]{3,2,1,0:T(8,128)(2,1)}, u32[]{:S(2)}, u32[]{:S(2)}) collective-permute-start(bf16[16,4,208,128]{3,2,1,0:T(8,128)(2,1)S(1)} %bitcast.26), channel_id=1, source_target_pairs={{0,4},{4,0},{1,5},{5,1},{2,6},{6,2},{3,7},{7,3},{8,12},{12,8},{9,1... | collective-permute-start | bytes 10223624 | tf_op jit(solution)/shard_map/ppermute | solution.py:272
  136.5 14.4 %all-to-all-start.4 = ((bf16[8,64,512]{2,1,0:T(8,128)(2,1)}), bf16[8,64,512]{2,1,0:T(8,128)(2,1)}, u32[]{:S(2)}, u32[]{:S(2)}) async-start(bf16[8,64,512]{2,1,0:T(8,128)(2,1)} %broadcast_in_dim.10), calls=%async_computation.4 | async-start | bytes 1048576 | tf_op jit(solution)/shard_map/all_to_all | solution.py:289
Sparse Core Ops, SparseCore 0:
  20.5 87.1 all-gather.4

commit v13 on v12

--- a/solution.py
+++ b/solution.py
@@ -185,20 +185,18 @@
         out[:, h * HEAD : h * HEAD + HEAD] = attn.astype(BF16)
 
 
-def proj_body(core, mine, other, weights, out, raw, wo, sem):
-    copy = pltpu.make_async_copy(weights.at[:, :, 0:64], raw, sem)
-    copy.start()
-    copy.wait()
+def proj_body(core, mine, other, weights, out, wo):
     for z in range(16):
         for y in range(4):
             low = (z * 4 + y) * 16
             for t in range(4):
                 lanes = slice(t * 128, t * 128 + 128)
-                wo[low : low + 16, lanes] = raw[z, y, t * 16 : t * 16 + 16, :]
-    for attn, c in ((mine, core[0]), (other, 1 - core[0])):
-        terms = dot(attn[...], wo[...], ((1,), (1,)))
+                wo[low : low + 16, lanes] = weights[z, y, t * 16 : t * 16 + 16, :]
+    attn = jnp.concatenate([mine[...], other[...]], axis=0)
+    terms = dot(attn, wo[...], ((1,), (1,)))
+    for i, c in enumerate((core[0], 1 - core[0])):
         for x in range(4):
-            out[c * 4 + x] = terms[:, x * 256 : x * 256 + 256].astype(BF16)
+            out[c * 4 + x] = terms[i * 64 : i * 64 + 64, x * 256 : x * 256 + 256].astype(BF16)
 
 
 def ffn_body(whole, gain, far1, far2, out, normed, w1, w2, sems):
@@ -255,19 +253,21 @@
     attn = kernel_call(attn_body, shape((64, 512), BF16), 3)(near, heads, gathered)
     attn_other = lax.ppermute(attn, "c", [(0, 1), (1, 0)])
     weights, attn_other = lax.optimization_barrier((weights, attn_other))
-    terms = kernel_call(
+    block = pl.BlockSpec(memory_space=pltpu.VMEM)
+    terms = pl.pallas_call(
         proj_body,
-        shape((8, 64, 256), BF16),
-        2,
-        [
-            pltpu.VMEM((16, 4, 64, 128), BF16),
-            pltpu.VMEM((1024, 512), BF16),
-            pltpu.SemaphoreType.DMA(()),
+        grid=(1,),
+        out_shape=shape((8, 64, 256), BF16),
+        in_specs=[
+            pl.BlockSpec(memory_space=pltpu.SMEM),
+            block,
+            block,
+            pl.BlockSpec((16, 4, 64, 128), lambda i: (0, 0, 0, 0)),
         ],
-        core=c[None],
-        n_far=1,
-        grant=LARGE,
-    )(attn, attn_other, weights)
+        out_specs=block,
+        scratch_shapes=[pltpu.VMEM((1024, 512), BF16)],
+        compiler_params=pltpu.CompilerParams(vmem_limit_bytes=SMALL),
+    )(c[None], attn, attn_other, weights)
     terms, weights = lax.optimization_barrier((terms, weights))
     swapped = lax.ppermute(weights, "c", [(0, 1), (1, 0)])
     parts = lax.all_to_all(terms, ("c", "x"), 0, 0)

time: 177 us -> 173 us (0.977)
  Pallas kernels: 23.8 us -> 21.6 us
  waiting for transfers between devices: 13.5 us -> 11.6 us
    pallas_call x4 -> x3, Pallas kernels: 11.2 us -> 7.24 us  [kernel_call(): return call if core is None else lambda *args: call(core, *args)]
    all_to_all x1, waiting for transfers between devices: 5.2 us -> 3.42 us  [on_device(): lax.all_to_all(jnp.broadcast_to(resid[None], (8, 64, 512)), ('yl', 'x'),...]
  transfers between devices with their start and end apart: 6 -> 6, of which waited for: 4 -> 4; matrix products, arithmetic and copies ran while one was open for 2% -> 1% of each run, Pallas kernels for 7% -> 8%
where the time goes in v13:
time: 173 us; the launch traced here: 172 us
  blocking collectives  95.7 us (55%)
  starting transfers between devices  24.6 us (14%)
  Pallas kernels  21.6 us (12%)
  between operations  13.6 us (8%)
  waiting for transfers between devices  11.6 us (7%)
  local copies, waits for them, and re-layouts  3.33 us (2%)
    all_gather x1, blocking collectives, on_device(): mine = jnp.sum(lax.all_gather(mine, 'z', axis=0), axis=0)  32.9 us
    all_to_all x1, blocking collectives, on_device(): parts = lax.all_to_all(terms, ('yl', 'x'), 0, 0)  12.6 us
    all_to_all x1, blocking collectives, on_device(): gathered = lax.all_to_all(gathered, (*y_axes, 'c'), 0, 0)  12.1 us
    all_to_all x1, blocking collectives, on_device(): got = lax.all_to_all(pack, y_axes, 0, 0)  11.3 us
    all_gather x1, blocking collectives, on_device(): heads = lax.all_gather(heads, y_axes, axis=0)  10.7 us
    all_to_all x1, blocking collectives, on_device(): parts = lax.all_to_all(terms, ('c', 'x'), 0, 0)  10.4 us
    ppermute x1, starting transfers between devices, on_device(): other = lax.ppermute(got, 'c', [(0, 1), (1, 0)])  8.35 us
    pallas_call x3, Pallas kernels, kernel_call(): return call if core is None else lambda *args: call(core, *args)  7.24 us
  transfers between devices with their start and end apart: 6, of which 4 were waited for; matrix products, arithmetic and copies ran while one was open for 1% of the time, Pallas kernels for 8%

profile of v13, /device:TPU:1, one launch (start us, length us, event | category | flops | bytes accessed | tf_op | source)
XLA Modules:
  0.0 172.4 jit_solution(7217563641695678499)
XLA Ops:
  6.5 0.0 all-gather.5.cloned.1.call-start
  6.5 1.7 %shard_map.109 = bf16[4,400,128]{2,1,0:T(8,128)(2,1)} custom-call(bf16[64,512]{1,0:T(8,128)(2,1)} %queries.1, bf16[64,512]{1,0:T(8,128)(2,1)} %k.1, bf16[64,512]{1,0:T(8,128)(2,1)} %v.1, bf16[16,768]{1,0:T(8,128)(2,1)} %wg.1, bf16[16,768]{1,0:T(8,128)(2,1)} %wu.1, bf16[16,768]{1,0:T(8,128)(2,1)} %bitcast.25, bf16[16,512]{1,0:T(8,128)(2,1)} %bitcast.26), custom_call_target="tpu_custom_call" | custom-call | tf_op jit(solution)/shard_map/pallas_call | solution.py:227
  8.3 11.3 %all_to_all.30.mine = bf16[4,400,128]{2,1,0:T(8,128)(2,1)S(1)} all-to-all(bf16[4,400,128]{2,1,0:T(8,128)(2,1)} %shard_map.109), channel_id=1, replica_groups=mesh['z'=16,'yh'=2,'yl'=2,'c'=2,'x'=4] {'yh','yl'}, dimensions={0} | all-to-all | bytes 819200 | tf_op jit(solution)/shard_map/all_to_all | solution.py:230
  19.6 0.7 slice.4
  20.3 0.0 all-gather.5.cloned.1.call-update
  20.3 8.4 %collective-permute-start = (bf16[4,400,128]{2,1,0:T(8,128)(2,1)S(1)}, bf16[4,400,128]{2,1,0:T(8,128)(2,1)S(1)}, u32[]{:S(2)}, u32[]{:S(2)}) collective-permute-start(bf16[4,400,128]{2,1,0:T(8,128)(2,1)S(1)} %all_to_all.30.mine), channel_id=1, source_target_pairs={{0,4},{4,0},{1,5},{5,1},{2,6},{6,2},{3,7},{7,3},{8,12},{12,8},{9,1... | collective-permute-start | bytes 1228808 | tf_op jit(solution)/shard_map/ppermute | solution.py:232
  28.7 0.1 pad_add_fusion.place
  28.8 0.7 fusion.3
  29.4 0.6 collective-permute-done.other
  30.0 0.8 shard_map.110
  30.8 32.9 %all-gather = f32[1024,128]{1,0:T(8,128)S(1)} all-gather(f32[64,128]{1,0:T(8,128)S(1)} %shard_map.110), channel_id=2, replica_groups=mesh['z'=16,'yh'=2,'yl'=2,'c'=2,'x'=4] {'z'}, dimensions={0}, use_global_device_ids=true | all-gather | bytes 557056 | tf_op jit(solution)/shard_map/all_gather | solution.py:238
  63.7 0.0 copy-start
  63.8 0.1 bitcast_divide_fusion
  63.9 5.7 %all_gather.24.marks = f32[2,64,128]{2,1,0:T(8,128)S(1)} all-gather(f32[1,64,128]{2,1,0:T(8,128)S(1)} %bitcast_divide_fusion), channel_id=1, replica_groups=mesh['z'=16,'yh'=2,'yl'=2,'c'=2,'x'=4] {'c'}, dimensions={0}, use_global_device_ids=true | all-gather | bytes 98304 | tf_op jit(solution)/shard_map/all_gather | solution.py:239
  69.5 1.4 shard_map.111
  70.9 7.0 %all-to-all-start.1 = ((f32[16,40,128]{2,1,0:T(8,128)}), f32[16,40,128]{2,1,0:T(8,128)S(1)}, u32[]{:S(2)}, u32[]{:S(2)}) async-start(f32[16,40,128]{2,1,0:T(8,128)} %shard_map.111), calls=%async_computation.1 | async-start | bytes 655360 | tf_op jit(solution)/shard_map/all_to_all | solution.py:241
  78.0 4.5 %shard_map.112 = f32[2,64,128]{2,1,0:T(8,128)S(1)} custom-call(f32[2,64,128]{2,1,0:T(8,128)S(1)} %all_gather.24.marks), custom_call_target="tpu_custom_call" | custom-call | flops 1000000000 | bytes 20000000 | tf_op jit(solution)/shard_map/pallas_call | solution.py:242
  82.5 0.0 copy-start.2
  82.5 0.0 copy-start.3
  82.5 10.7 %all-gather.1 = f32[8,64,128]{2,1,0:T(8,128)S(1)} all-gather(f32[2,64,128]{2,1,0:T(8,128)S(1)} %shard_map.112), channel_id=3, replica_groups=mesh['z'=16,'yh'=2,'yl'=2,'c'=2,'x'=4] {'yh','yl'}, dimensions={0}, use_global_device_ids=true | all-gather | bytes 327680 | tf_op jit(solution)/shard_map/all_gather | solution.py:248
  93.2 0.0 copy-done
  93.2 0.5 shard_map.113.near
  93.7 6.6 %all-to-all-done.1.parts = f32[16,40,128]{2,1,0:T(8,128)S(1)} async-done(((f32[16,40,128]{2,1,0:T(8,128)}), f32[16,40,128]{2,1,0:T(8,128)S(1)}, u32[]{:S(2)}, u32[]{:S(2)}) %all-to-all-start.1) | async-done | bytes 327712 | tf_op jit(solution)/shard_map/all_to_all | solution.py:241
  100.4 0.2 shard_map.114
  100.6 12.1 %all_to_all.31.gathered = f32[8,32,128]{2,1,0:T(8,128)S(1)} all-to-all(f32[8,32,128]{2,1,0:T(8,128)S(1)} %shard_map.114), channel_id=1, replica_groups=mesh['z'=16,'yh'=2,'yl'=2,'c'=2,'x'=4] {'yh','yl','c'}, dimensions={0} | all-to-all | bytes 262144 | tf_op jit(solution)/shard_map/all_to_all | solution.py:252
  112.7 0.5 shard_map.115.mine
  113.2 2.8 %collective-permute-start.1 = (bf16[64,512]{1,0:T(8,128)(2,1)S(1)}, bf16[64,512]{1,0:T(8,128)(2,1)S(1)}, u32[]{:S(2)}, u32[]{:S(2)}) collective-permute-start(bf16[64,512]{1,0:T(8,128)(2,1)S(1)} %shard_map.115.mine), channel_id=1, source_target_pairs={{0,4},{4,0},{1,5},{5,1},{2,6},{6,2},{3,7},{7,3},{8,12},{12,8},{9,1... | collective-permute-start | bytes 196616 | tf_op jit(solution)/shard_map/ppermute | solution.py:254
  116.0 0.9 collective-permute-done.1.other
  116.9 0.0 all-gather.5.cloned.1.call-done
  116.9 1.7 %shard_map.116 = bf16[8,64,256]{2,1,0:T(8,128)(2,1)S(1)} custom-call(s32[1]{0:T(128)} %bitcast.core, bf16[64,512]{1,0:T(8,128)(2,1)S(1)} %shard_map.115.mine, bf16[64,512]{1,0:T(8,128)(2,1)S(1)} %collective-permute-done.1.other, bf16[16,4,208,128]{3,2,1,0:T(8,128)(2,1)} %bitcast.8.weights.mine), custom_call_target="tpu_custom_call" | custom-call | tf_op jit(solution)/shard_map/pallas_call | solution.py:257
  118.6 2.3 %collective-permute-start.2 = (bf16[16,4,208,128]{3,2,1,0:T(8,128)(2,1)}, bf16[16,4,208,128]{3,2,1,0:T(8,128)(2,1)S(1)}, u32[]{:S(2)}, u32[]{:S(2)}) collective-permute-start(bf16[16,4,208,128]{3,2,1,0:T(8,128)(2,1)} %bitcast.8.weights.mine), channel_id=1, source_target_pairs={{0,4},{4,0},{1,5},{5,1},{2,6},{6,2},{3,7},{7,3},{8,12},{12,8},{9,1... | collective-permute-start | bytes 10223624 | tf_op jit(solution)/shard_map/ppermute | solution.py:272
  120.9 10.4 %all_to_all.32 = bf16[8,64,256]{2,1,0:T(8,128)(2,1)S(1)} all-to-all(bf16[8,64,256]{2,1,0:T(8,128)(2,1)S(1)} %shard_map.116), channel_id=1, replica_groups=mesh['z'=16,'yh'=2,'yl'=2,'c'=2,'x'=4] {'c','x'}, dimensions={0} | all-to-all | bytes 524288 | tf_op jit(solution)/shard_map/all_to_all | solution.py:273
  131.3 0.0 copy-done.2
  131.3 0.0 copy-done.3
  131.3 0.6 fusion.1
  131.9 0.9 broadcast_in_dim.10
  132.7 4.1 %all-to-all-start.4 = ((bf16[8,64,512]{2,1,0:T(8,128)(2,1)}), bf16[8,64,512]{2,1,0:T(8,128)(2,1)}, u32[]{:S(2)}, u32[]{:S(2)}) async-start(bf16[8,64,512]{2,1,0:T(8,128)(2,1)} %broadcast_in_dim.10), calls=%async_computation.4 | async-start | bytes 1048576 | tf_op jit(solution)/shard_map/all_to_all | solution.py:289
  136.9 0.0 collective-permute-done.2.other
  136.9 0.0 copy-start.1
  136.9 1.8 %copy-done.1 = bf16[16,4,208,128]{3,2,1,0:T(8,128)(2,1)} copy-done((bf16[16,4,208,128]{3,2,1,0:T(8,128)(2,1)}, bf16[16,4,208,128]{3,2,1,0:T(8,128)(2,1)S(1)}, u32[]{:S(2)}) %copy-start.1) | copy-done | bytes 3407896
  138.7 5.1 %shard_map.117 = (bf16[2048,768]{1,0:T(8,128)(2,1)}, bf16[2048,384]{1,0:T(8,128)(2,1)}) custom-call(s32[1]{0:T(128)} %bitcast.core, bf16[16,4,208,128]{3,2,1,0:T(8,128)(2,1)} %bitcast.8.weights.mine, bf16[16,4,208,128]{3,2,1,0:T(8,128)(2,1)} %copy-done.1), custom_call_target="tpu_custom_call" | custom-call | tf_op jit(solution)/shard_map/pallas_call | solution.py:43
  143.7 3.4 %all-to-all-done.4.whole = bf16[8,64,512]{2,1,0:T(8,128)(2,1)} async-done(((bf16[8,64,512]{2,1,0:T(8,128)(2,1)}), bf16[8,64,512]{2,1,0:T(8,128)(2,1)}, u32[]{:S(2)}, u32[]{:S(2)}) %all-to-all-start.4) | async-done | bytes 524320 | tf_op jit(solution)/shard_map/all_to_all | solution.py:289
  147.2 5.1 %shard_map.118 = bf16[8,64,512]{2,1,0:T(8,128)(2,1)} custom-call(bf16[8,64,512]{2,1,0:T(8,128)(2,1)} %all-to-all-done.4.whole, f32[1,2048]{1,0:T(1,128)} %bitcast.27, bf16[2048,768]{1,0:T(8,128)(2,1)} %get-tuple-element.21.far1, bf16[2048,384]{1,0:T(8,128)(2,1)} %get-tuple-element.22.far2), custom_call_target="tpu_custom_call" | custom-call | tf_op jit(solution)/shard_map/pallas_call | solution.py:290
  152.3 12.6 %all_to_all.33 = bf16[8,64,512]{2,1,0:T(8,128)(2,1)S(1)} all-to-all(bf16[8,64,512]{2,1,0:T(8,128)(2,1)} %shard_map.118), channel_id=1, replica_groups=mesh['z'=16,'yh'=2,'yl'=2,'c'=2,'x'=4] {'yl','x'}, dimensions={0} | all-to-all | bytes 1048576 | tf_op jit(solution)/shard_map/all_to_all | solution.py:303
  164.8 0.1 convert_reduce_fusion
  164.9 0.6 add_convert_fusion
  (2 shorter events, 0.1 us)
Async XLA Ops:
  6.5 110.3 %all-gather.5.cloned.1.call-start = ((), (), s32[]{:S(2)}) async-start(), calls=%async_computation.6 | async-start | bytes 3620864 | tf_op jit(solution)/shard_map/all_gather | solution.py:231
  20.3 9.7 %collective-permute-start = (bf16[4,400,128]{2,1,0:T(8,128)(2,1)S(1)}, bf16[4,400,128]{2,1,0:T(8,128)(2,1)S(1)}, u32[]{:S(2)}, u32[]{:S(2)}) collective-permute-start(bf16[4,400,128]{2,1,0:T(8,128)(2,1)S(1)} %all_to_all.30.mine), channel_id=1, source_target_pairs={{0,4},{4,0},{1,5},{5,1},{2,6},{6,2},{3,7},{7,3},{8,12},{12,8},{9,1... | collective-permute-start | bytes 1228808 | tf_op jit(solution)/shard_map/ppermute | solution.py:232
  63.7 29.5 %copy-start = (bf16[64,512]{1,0:T(8,128)(2,1)S(1)}, bf16[64,512]{1,0:T(8,128)(2,1)}, u32[]{:S(2)}) copy-start(bf16[64,512]{1,0:T(8,128)(2,1)} %queries.1) | copy-start | bytes 196612
  70.9 29.5 %all-to-all-start.1 = ((f32[16,40,128]{2,1,0:T(8,128)}), f32[16,40,128]{2,1,0:T(8,128)S(1)}, u32[]{:S(2)}, u32[]{:S(2)}) async-start(f32[16,40,128]{2,1,0:T(8,128)} %shard_map.111), calls=%async_computation.1 | async-start | bytes 655360 | tf_op jit(solution)/shard_map/all_to_all | solution.py:241
  82.5 48.8 %copy-start.2 = (bf16[64,512]{1,0:T(8,128)(2,1)S(1)}, bf16[64,512]{1,0:T(8,128)(2,1)}, u32[]{:S(2)}) copy-start(bf16[64,512]{1,0:T(8,128)(2,1)} %param.14) | copy-start | bytes 196612
  82.5 48.8 %copy-start.3 = (s32[2,256]{1,0:T(2,128)S(1)}, s32[2,256]{1,0:T(2,128)}, u32[]{:S(2)}) copy-start(s32[2,256]{1,0:T(2,128)} %constant.25) | copy-start | bytes 6148
  113.2 3.7 %collective-permute-start.1 = (bf16[64,512]{1,0:T(8,128)(2,1)S(1)}, bf16[64,512]{1,0:T(8,128)(2,1)S(1)}, u32[]{:S(2)}, u32[]{:S(2)}) collective-permute-start(bf16[64,512]{1,0:T(8,128)(2,1)S(1)} %shard_map.115.mine), channel_id=1, source_target_pairs={{0,4},{4,0},{1,5},{5,1},{2,6},{6,2},{3,7},{7,3},{8,12},{12,8},{9,1... | collective-permute-start | bytes 196616 | tf_op jit(solution)/shard_map/ppermute | solution.py:254
  118.6 18.3 %collective-permute-start.2 = (bf16[16,4,208,128]{3,2,1,0:T(8,128)(2,1)}, bf16[16,4,208,128]{3,2,1,0:T(8,128)(2,1)S(1)}, u32[]{:S(2)}, u32[]{:S(2)}) collective-permute-start(bf16[16,4,208,128]{3,2,1,0:T(8,128)(2,1)} %bitcast.8.weights.mine), channel_id=1, source_target_pairs={{0,4},{4,0},{1,5},{5,1},{2,6},{6,2},{3,7},{7,3},{8,12},{12,8},{9,1... | collective-permute-start | bytes 10223624 | tf_op jit(solution)/shard_map/ppermute | solution.py:272
  132.7 14.4 %all-to-all-start.4 = ((bf16[8,64,512]{2,1,0:T(8,128)(2,1)}), bf16[8,64,512]{2,1,0:T(8,128)(2,1)}, u32[]{:S(2)}, u32[]{:S(2)}) async-start(bf16[8,64,512]{2,1,0:T(8,128)(2,1)} %broadcast_in_dim.10), calls=%async_computation.4 | async-start | bytes 1048576 | tf_op jit(solution)/shard_map/all_to_all | solution.py:289
  136.9 1.8 %copy-start.1 = (bf16[16,4,208,128]{3,2,1,0:T(8,128)(2,1)}, bf16[16,4,208,128]{3,2,1,0:T(8,128)(2,1)S(1)}, u32[]{:S(2)}) copy-start(bf16[16,4,208,128]{3,2,1,0:T(8,128)(2,1)S(1)} %collective-permute-done.2.other) | copy-start | bytes 10223620
Sparse Core Ops, SparseCore 0:
  20.4 87.1 all-gather.4

commit v14 on v13

--- a/solution.py
+++ b/solution.py
@@ -142,11 +142,12 @@
     out[1] = jnp.concatenate([approx, jnp.zeros_like(approx)], axis=-1)
 
 
-def near_body(queries, heads, out):
-    for h in range(4):
-        query = queries[:, h * HEAD : h * HEAD + HEAD].astype(F32)
-        near = softmax(dot(query, heads[h, 0], ((1,), (1,)), HI) * SCALE, -1)
-        out[h] = jnp.concatenate([near, jnp.zeros_like(near)], axis=-1)
+def near_body(mine, other, heads, out):
+    for i, queries in enumerate((mine, other)):
+        for h in range(4):
+            query = queries[:, h * HEAD : h * HEAD + HEAD].astype(F32)
+            near = softmax(dot(query, heads[h, 0], ((1,), (1,)), HI) * SCALE, -1)
+            out[h, i * 64 : i * 64 + 64] = jnp.concatenate([near, jnp.zeros_like(near)], axis=-1)
 
 
 def spread(terms, out):
@@ -185,15 +186,14 @@
         out[:, h * HEAD : h * HEAD + HEAD] = attn.astype(BF16)
 
 
-def proj_body(core, mine, other, weights, out, wo):
+def proj_body(core, attn, weights, out, wo):
     for z in range(16):
         for y in range(4):
             low = (z * 4 + y) * 16
             for t in range(4):
                 lanes = slice(t * 128, t * 128 + 128)
                 wo[low : low + 16, lanes] = weights[z, y, t * 16 : t * 16 + 16, :]
-    attn = jnp.concatenate([mine[...], other[...]], axis=0)
-    terms = dot(attn, wo[...], ((1,), (1,)))
+    terms = dot(attn[...], wo[...], ((1,), (1,)))
     for i, c in enumerate((core[0], 1 - core[0])):
         for x in range(4):
             out[c * 4 + x] = terms[i * 64 : i * 64 + 64, x * 256 : x * 256 + 256].astype(BF16)
@@ -246,13 +246,13 @@
         cost=pl.CostEstimate(flops=10**9, bytes_accessed=2 * 10**7, transcendentals=0),
     )(marks)
     heads = lax.all_gather(heads, y_axes, axis=0)
-    near = kernel_call(near_body, shape((4, 64, HEAD), F32), 2)(queries, heads)
+    queries_other = lax.ppermute(queries, "c", [(0, 1), (1, 0)])
+    near = kernel_call(near_body, shape((4, 128, HEAD), F32), 3)(queries, queries_other, heads)
     parts, near, heads = lax.optimization_barrier((parts, near, heads))
     gathered = kernel_call(merge_body, shape((8, 32, HEAD), F32), 1)(parts)
     gathered = lax.all_to_all(gathered, (*y_axes, "c"), 0, 0)
-    attn = kernel_call(attn_body, shape((64, 512), BF16), 3)(near, heads, gathered)
-    attn_other = lax.ppermute(attn, "c", [(0, 1), (1, 0)])
-    weights, attn_other = lax.optimization_barrier((weights, attn_other))
+    attn = kernel_call(attn_body, shape((128, 512), BF16), 3)(near, heads, gathered)
+    weights, attn = lax.optimization_barrier((weights, attn))
     block = pl.BlockSpec(memory_space=pltpu.VMEM)
     terms = pl.pallas_call(
         proj_body,
@@ -261,13 +261,12 @@
         in_specs=[
             pl.BlockSpec(memory_space=pltpu.SMEM),
             block,
-            block,
             pl.BlockSpec((16, 4, 64, 128), lambda i: (0, 0, 0, 0)),
         ],
         out_specs=block,
         scratch_shapes=[pltpu.VMEM((1024, 512), BF16)],
         compiler_params=pltpu.CompilerParams(vmem_limit_bytes=SMALL),
-    )(c[None], attn, attn_other, weights)
+    )(c[None], attn, weights)
     terms, weights = lax.optimization_barrier((terms, weights))
     swapped = lax.ppermute(weights, "c", [(0, 1), (1, 0)])
     parts = lax.all_to_all(terms, ("c", "x"), 0, 0)

time: 173 us -> 172 us (level)
  waiting for transfers between devices: 11.6 us -> 8.19 us
    all_to_all x1, waiting for transfers between devices: 6.64 us -> 4.19 us  [on_device(): parts = lax.all_to_all(send, 'z', 0, 0)]
  transfers between devices with their start and end apart: 6 -> 6, of which waited for: 4 -> 3; matrix products, arithmetic and copies ran while one was open for 1% -> 1% of each run, Pallas kernels for 8% -> 8%
where the time goes in v14:
time: 172 us; the launch traced here: 171 us
  blocking collectives  95.4 us (55%)
  starting transfers between devices  25.9 us (15%)
  Pallas kernels  22 us (13%)
  between operations  13.6 us (8%)
  waiting for transfers between devices  8.19 us (5%)
  local copies, waits for them, and re-layouts  3.32 us (2%)
    all_gather x1, blocking collectives, on_device(): mine = jnp.sum(lax.all_gather(mine, 'z', axis=0), axis=0)  32.9 us
    all_to_all x1, blocking collectives, on_device(): parts = lax.all_to_all(terms, ('yl', 'x'), 0, 0)  12.6 us
    all_to_all x1, blocking collectives, on_device(): gathered = lax.all_to_all(gathered, (*y_axes, 'c'), 0, 0)  12 us
    all_to_all x1, blocking collectives, on_device(): got = lax.all_to_all(pack, y_axes, 0, 0)  11.3 us
    all_gather x1, blocking collectives, on_device(): heads = lax.all_gather(heads, y_axes, axis=0)  10.6 us
    all_to_all x1, blocking collectives, on_device(): parts = lax.all_to_all(terms, ('c', 'x'), 0, 0)  10.3 us
    ppermute x1, starting transfers between devices, on_device(): other = lax.ppermute(got, 'c', [(0, 1), (1, 0)])  8.35 us
    pallas_call x3, Pallas kernels, kernel_call(): return call if core is None else lambda *args: call(core, *args)  7.24 us
  transfers between devices with their start and end apart: 6, of which 3 were waited for; matrix products, arithmetic and copies ran while one was open for 1% of the time, Pallas kernels for 8%

profile of v14, /device:TPU:1, one launch (start us, length us, event | category | flops | bytes accessed | tf_op | source)
XLA Modules:
  0.0 170.5 jit_solution(17441784148011116570)
XLA Ops:
  6.5 0.0 copy-start
  6.5 0.0 all-gather.5.cloned.1.call-start
  6.5 1.8 %shard_map.109 = bf16[4,400,128]{2,1,0:T(8,128)(2,1)} custom-call(bf16[64,512]{1,0:T(8,128)(2,1)} %mine.1, bf16[64,512]{1,0:T(8,128)(2,1)} %k.1, bf16[64,512]{1,0:T(8,128)(2,1)} %v.1, bf16[16,768]{1,0:T(8,128)(2,1)} %wg.1, bf16[16,768]{1,0:T(8,128)(2,1)} %wu.1, bf16[16,768]{1,0:T(8,128)(2,1)} %bitcast.25, bf16[16,512]{1,0:T(8,128)(2,1)} %bitcast.26), custom_call_target="tpu_custom_call" | custom-call | tf_op jit(solution)/shard_map/pallas_call | solution.py:227
  8.3 11.3 %all_to_all.30.mine = bf16[4,400,128]{2,1,0:T(8,128)(2,1)S(1)} all-to-all(bf16[4,400,128]{2,1,0:T(8,128)(2,1)} %shard_map.109), channel_id=1, replica_groups=mesh['z'=16,'yh'=2,'yl'=2,'c'=2,'x'=4] {'yh','yl'}, dimensions={0} | all-to-all | bytes 819200 | tf_op jit(solution)/shard_map/all_to_all | solution.py:230
  19.6 0.7 slice.4
  20.3 0.0 all-gather.5.cloned.1.call-update
  20.4 8.4 %collective-permute-start = (bf16[4,400,128]{2,1,0:T(8,128)(2,1)S(1)}, bf16[4,400,128]{2,1,0:T(8,128)(2,1)S(1)}, u32[]{:S(2)}, u32[]{:S(2)}) collective-permute-start(bf16[4,400,128]{2,1,0:T(8,128)(2,1)S(1)} %all_to_all.30.mine), channel_id=1, source_target_pairs={{0,4},{4,0},{1,5},{5,1},{2,6},{6,2},{3,7},{7,3},{8,12},{12,8},{9,1... | collective-permute-start | bytes 1228808 | tf_op jit(solution)/shard_map/ppermute | solution.py:232
  28.7 0.1 pad_add_fusion.place
  28.8 0.7 fusion.3
  29.5 0.6 collective-permute-done.other
  30.1 0.8 shard_map.110
  30.8 32.9 %all-gather.1 = f32[1024,128]{1,0:T(8,128)S(1)} all-gather(f32[64,128]{1,0:T(8,128)S(1)} %shard_map.110), channel_id=3, replica_groups=mesh['z'=16,'yh'=2,'yl'=2,'c'=2,'x'=4] {'z'}, dimensions={0}, use_global_device_ids=true | all-gather | bytes 557056 | tf_op jit(solution)/shard_map/all_gather | solution.py:238
  63.8 0.1 bitcast_divide_fusion
  63.9 5.7 %all_gather.26.marks = f32[2,64,128]{2,1,0:T(8,128)S(1)} all-gather(f32[1,64,128]{2,1,0:T(8,128)S(1)} %bitcast_divide_fusion), channel_id=1, replica_groups=mesh['z'=16,'yh'=2,'yl'=2,'c'=2,'x'=4] {'c'}, dimensions={0}, use_global_device_ids=true | all-gather | bytes 98304 | tf_op jit(solution)/shard_map/all_gather | solution.py:239
  69.6 1.4 shard_map.111
  71.0 7.0 %all-to-all-start.1 = ((f32[16,40,128]{2,1,0:T(8,128)}), f32[16,40,128]{2,1,0:T(8,128)S(1)}, u32[]{:S(2)}, u32[]{:S(2)}) async-start(f32[16,40,128]{2,1,0:T(8,128)} %shard_map.111), calls=%async_computation.1 | async-start | bytes 655360 | tf_op jit(solution)/shard_map/all_to_all | solution.py:241
  78.0 0.0 copy-done
  78.0 2.5 %collective-permute-start.1 = (bf16[64,512]{1,0:T(8,128)(2,1)S(1)}, bf16[64,512]{1,0:T(8,128)(2,1)S(1)}, u32[]{:S(2)}, u32[]{:S(2)}) collective-permute-start(bf16[64,512]{1,0:T(8,128)(2,1)S(1)} %copy-done), channel_id=1, source_target_pairs={{0,4},{4,0},{1,5},{5,1},{2,6},{6,2},{3,7},{7,3},{8,12},{12,8},{9,1... | collective-permute-start | bytes 196616 | tf_op jit(solution)/shard_map/ppermute | solution.py:249
  80.5 4.5 %shard_map.112 = f32[2,64,128]{2,1,0:T(8,128)S(1)} custom-call(f32[2,64,128]{2,1,0:T(8,128)S(1)} %all_gather.26.marks), custom_call_target="tpu_custom_call" | custom-call | flops 1000000000 | bytes 20000000 | tf_op jit(solution)/shard_map/pallas_call | solution.py:242
  85.1 10.6 %all-gather.2 = f32[8,64,128]{2,1,0:T(8,128)S(1)} all-gather(f32[2,64,128]{2,1,0:T(8,128)S(1)} %shard_map.112), channel_id=4, replica_groups=mesh['z'=16,'yh'=2,'yl'=2,'c'=2,'x'=4] {'yh','yl'}, dimensions={0}, use_global_device_ids=true | all-gather | bytes 327680 | tf_op jit(solution)/shard_map/all_gather | solution.py:248
  95.7 0.0 collective-permute-done.1.other
  95.7 0.0 copy-start.2
  95.7 0.0 copy-start.3
  95.7 0.7 shard_map.113.near
  96.4 4.2 %all-to-all-done.1.parts = f32[16,40,128]{2,1,0:T(8,128)S(1)} async-done(((f32[16,40,128]{2,1,0:T(8,128)}), f32[16,40,128]{2,1,0:T(8,128)S(1)}, u32[]{:S(2)}, u32[]{:S(2)}) %all-to-all-start.1) | async-done | bytes 327712 | tf_op jit(solution)/shard_map/all_to_all | solution.py:241
  100.6 0.2 shard_map.114
  100.8 12.0 %all_to_all.31.gathered = f32[8,32,128]{2,1,0:T(8,128)S(1)} all-to-all(f32[8,32,128]{2,1,0:T(8,128)S(1)} %shard_map.114), channel_id=1, replica_groups=mesh['z'=16,'yh'=2,'yl'=2,'c'=2,'x'=4] {'yh','yl','c'}, dimensions={0} | all-to-all | bytes 262144 | tf_op jit(solution)/shard_map/all_to_all | solution.py:253
  112.8 0.7 shard_map.115.attn
  113.5 0.0 all-gather.5.cloned.1.call-done
  113.5 1.7 %shard_map.116 = bf16[8,64,256]{2,1,0:T(8,128)(2,1)S(1)} custom-call(s32[1]{0:T(128)} %bitcast.core, bf16[128,512]{1,0:T(8,128)(2,1)S(1)} %shard_map.115.attn, bf16[16,4,208,128]{3,2,1,0:T(8,128)(2,1)} %bitcast.3.weights.mine), custom_call_target="tpu_custom_call" | custom-call | tf_op jit(solution)/shard_map/pallas_call | solution.py:257
  115.3 3.8 %collective-permute-start.2 = (bf16[16,4,208,128]{3,2,1,0:T(8,128)(2,1)}, bf16[16,4,208,128]{3,2,1,0:T(8,128)(2,1)S(1)}, u32[]{:S(2)}, u32[]{:S(2)}) collective-permute-start(bf16[16,4,208,128]{3,2,1,0:T(8,128)(2,1)} %bitcast.3.weights.mine), channel_id=1, source_target_pairs={{0,4},{4,0},{1,5},{5,1},{2,6},{6,2},{3,7},{7,3},{8,12},{12,8},{9,1... | collective-permute-start | bytes 10223624 | tf_op jit(solution)/shard_map/ppermute | solution.py:271
  119.1 10.3 %all_to_all.32 = bf16[8,64,256]{2,1,0:T(8,128)(2,1)S(1)} all-to-all(bf16[8,64,256]{2,1,0:T(8,128)(2,1)S(1)} %shard_map.116), channel_id=1, replica_groups=mesh['z'=16,'yh'=2,'yl'=2,'c'=2,'x'=4] {'c','x'}, dimensions={0} | all-to-all | bytes 524288 | tf_op jit(solution)/shard_map/all_to_all | solution.py:272
  129.5 0.0 copy-done.2
  129.5 0.0 copy-done.3
  129.5 0.6 fusion.1
  130.0 0.9 broadcast_in_dim.10
  130.9 4.1 %all-to-all-start.4 = ((bf16[8,64,512]{2,1,0:T(8,128)(2,1)}), bf16[8,64,512]{2,1,0:T(8,128)(2,1)}, u32[]{:S(2)}, u32[]{:S(2)}) async-start(bf16[8,64,512]{2,1,0:T(8,128)(2,1)} %broadcast_in_dim.10), calls=%async_computation.4 | async-start | bytes 1048576 | tf_op jit(solution)/shard_map/all_to_all | solution.py:288
  135.0 0.0 collective-permute-done.2.other
  135.1 0.0 copy-start.1
  135.1 1.8 %copy-done.1 = bf16[16,4,208,128]{3,2,1,0:T(8,128)(2,1)} copy-done((bf16[16,4,208,128]{3,2,1,0:T(8,128)(2,1)}, bf16[16,4,208,128]{3,2,1,0:T(8,128)(2,1)S(1)}, u32[]{:S(2)}) %copy-start.1) | copy-done | bytes 3407896
  136.8 5.1 %shard_map.117 = (bf16[2048,768]{1,0:T(8,128)(2,1)}, bf16[2048,384]{1,0:T(8,128)(2,1)}) custom-call(s32[1]{0:T(128)} %bitcast.core, bf16[16,4,208,128]{3,2,1,0:T(8,128)(2,1)} %bitcast.3.weights.mine, bf16[16,4,208,128]{3,2,1,0:T(8,128)(2,1)} %copy-done.1), custom_call_target="tpu_custom_call" | custom-call | tf_op jit(solution)/shard_map/pallas_call | solution.py:43
  141.9 3.3 %all-to-all-done.4.whole = bf16[8,64,512]{2,1,0:T(8,128)(2,1)} async-done(((bf16[8,64,512]{2,1,0:T(8,128)(2,1)}), bf16[8,64,512]{2,1,0:T(8,128)(2,1)}, u32[]{:S(2)}, u32[]{:S(2)}) %all-to-all-start.4) | async-done | bytes 524320 | tf_op jit(solution)/shard_map/all_to_all | solution.py:288
  145.3 5.1 %shard_map.118 = bf16[8,64,512]{2,1,0:T(8,128)(2,1)} custom-call(bf16[8,64,512]{2,1,0:T(8,128)(2,1)} %all-to-all-done.4.whole, f32[1,2048]{1,0:T(1,128)} %bitcast.27, bf16[2048,768]{1,0:T(8,128)(2,1)} %get-tuple-element.21.far1, bf16[2048,384]{1,0:T(8,128)(2,1)} %get-tuple-element.22.far2), custom_call_target="tpu_custom_call" | custom-call | tf_op jit(solution)/shard_map/pallas_call | solution.py:289
  150.4 12.6 %all_to_all.33 = bf16[8,64,512]{2,1,0:T(8,128)(2,1)S(1)} all-to-all(bf16[8,64,512]{2,1,0:T(8,128)(2,1)} %shard_map.118), channel_id=1, replica_groups=mesh['z'=16,'yh'=2,'yl'=2,'c'=2,'x'=4] {'yl','x'}, dimensions={0} | all-to-all | bytes 1048576 | tf_op jit(solution)/shard_map/all_to_all | solution.py:302
  162.9 0.1 convert_reduce_fusion
  163.0 0.6 add_convert_fusion
  (2 shorter events, 0.1 us)
Async XLA Ops:
  6.5 71.5 %copy-start = (bf16[64,512]{1,0:T(8,128)(2,1)S(1)}, bf16[64,512]{1,0:T(8,128)(2,1)}, u32[]{:S(2)}) copy-start(bf16[64,512]{1,0:T(8,128)(2,1)} %mine.1) | copy-start | bytes 196612
  6.5 107.0 %all-gather.5.cloned.1.call-start = ((), (), s32[]{:S(2)}) async-start(), calls=%async_computation.6 | async-start | bytes 3620864 | tf_op jit(solution)/shard_map/all_gather | solution.py:231
  20.4 9.7 %collective-permute-start = (bf16[4,400,128]{2,1,0:T(8,128)(2,1)S(1)}, bf16[4,400,128]{2,1,0:T(8,128)(2,1)S(1)}, u32[]{:S(2)}, u32[]{:S(2)}) collective-permute-start(bf16[4,400,128]{2,1,0:T(8,128)(2,1)S(1)} %all_to_all.30.mine), channel_id=1, source_target_pairs={{0,4},{4,0},{1,5},{5,1},{2,6},{6,2},{3,7},{7,3},{8,12},{12,8},{9,1... | collective-permute-start | bytes 1228808 | tf_op jit(solution)/shard_map/ppermute | solution.py:232
  71.0 29.6 %all-to-all-start.1 = ((f32[16,40,128]{2,1,0:T(8,128)}), f32[16,40,128]{2,1,0:T(8,128)S(1)}, u32[]{:S(2)}, u32[]{:S(2)}) async-start(f32[16,40,128]{2,1,0:T(8,128)} %shard_map.111), calls=%async_computation.1 | async-start | bytes 655360 | tf_op jit(solution)/shard_map/all_to_all | solution.py:241
  78.0 17.6 %collective-permute-start.1 = (bf16[64,512]{1,0:T(8,128)(2,1)S(1)}, bf16[64,512]{1,0:T(8,128)(2,1)S(1)}, u32[]{:S(2)}, u32[]{:S(2)}) collective-permute-start(bf16[64,512]{1,0:T(8,128)(2,1)S(1)} %copy-done), channel_id=1, source_target_pairs={{0,4},{4,0},{1,5},{5,1},{2,6},{6,2},{3,7},{7,3},{8,12},{12,8},{9,1... | collective-permute-start | bytes 196616 | tf_op jit(solution)/shard_map/ppermute | solution.py:249
  95.7 33.8 %copy-start.2 = (bf16[64,512]{1,0:T(8,128)(2,1)S(1)}, bf16[64,512]{1,0:T(8,128)(2,1)}, u32[]{:S(2)}) copy-start(bf16[64,512]{1,0:T(8,128)(2,1)} %param.14) | copy-start | bytes 196612
  95.7 33.8 %copy-start.3 = (s32[2,256]{1,0:T(2,128)S(1)}, s32[2,256]{1,0:T(2,128)}, u32[]{:S(2)}) copy-start(s32[2,256]{1,0:T(2,128)} %constant.25) | copy-start | bytes 6148
  115.3 19.8 %collective-permute-start.2 = (bf16[16,4,208,128]{3,2,1,0:T(8,128)(2,1)}, bf16[16,4,208,128]{3,2,1,0:T(8,128)(2,1)S(1)}, u32[]{:S(2)}, u32[]{:S(2)}) collective-permute-start(bf16[16,4,208,128]{3,2,1,0:T(8,128)(2,1)} %bitcast.3.weights.mine), channel_id=1, source_target_pairs={{0,4},{4,0},{1,5},{5,1},{2,6},{6,2},{3,7},{7,3},{8,12},{12,8},{9,1... | collective-permute-start | bytes 10223624 | tf_op jit(solution)/shard_map/ppermute | solution.py:271
  130.9 14.4 %all-to-all-start.4 = ((bf16[8,64,512]{2,1,0:T(8,128)(2,1)}), bf16[8,64,512]{2,1,0:T(8,128)(2,1)}, u32[]{:S(2)}, u32[]{:S(2)}) async-start(bf16[8,64,512]{2,1,0:T(8,128)(2,1)} %broadcast_in_dim.10), calls=%async_computation.4 | async-start | bytes 1048576 | tf_op jit(solution)/shard_map/all_to_all | solution.py:288
  135.1 1.8 %copy-start.1 = (bf16[16,4,208,128]{3,2,1,0:T(8,128)(2,1)}, bf16[16,4,208,128]{3,2,1,0:T(8,128)(2,1)S(1)}, u32[]{:S(2)}) copy-start(bf16[16,4,208,128]{3,2,1,0:T(8,128)(2,1)S(1)} %collective-permute-done.2.other) | copy-start | bytes 10223620
Sparse Core Ops, SparseCore 0:
  20.5 87.0 all-gather.4

commit v15 on v14

--- a/solution.py
+++ b/solution.py
@@ -159,23 +159,22 @@
 def unmix(blocks, tile, dest, lanes, c):
     for z in range(16):
         for y in range(4):
-            low = pl.multiple_of((z * 8 + y * 2 + c) * 16, 16)
-            dest[pl.ds(low, 16), lanes] = blocks[z, y, tile * 16 : tile * 16 + 16, :]
-
-
-def unmix_body(core, mine, other, w1, w2, raw, sems):
+            low = (z * 8 + y * 2 + c) * 16
+            dest[low : low + 16, lanes] = blocks[z, y, tile * 16 : tile * 16 + 16, :]
+
+
+def unmix_body(cores, w1, w2, raw, sems):
     copies = [
-        pltpu.make_async_copy(far.at[:, :, 64:208], raw.at[i], sems.at[i])
-        for i, far in enumerate((mine, other))
+        pltpu.make_async_copy(cores.at[c, :, :, 64:208], raw.at[c], sems.at[c]) for c in range(2)
     ]
     for copy in copies:
         copy.start()
-    for i, c in enumerate((core[0], 1 - core[0])):
-        copies[i].wait()
+    for c in range(2):
+        copies[c].wait()
         for t in range(6):
-            unmix(raw.at[i], t, w1, slice(t * 128, t * 128 + 128), c)
+            unmix(raw.at[c], t, w1, slice(t * 128, t * 128 + 128), c)
         for t in range(3):
-            unmix(raw.at[i], 6 + t, w2, slice(t * 128, t * 128 + 128), c)
+            unmix(raw.at[c], 6 + t, w2, slice(t * 128, t * 128 + 128), c)
 
 
 def attn_body(near, heads, gathered, out):
@@ -265,20 +264,18 @@
         ],
         out_specs=block,
         scratch_shapes=[pltpu.VMEM((1024, 512), BF16)],
-        compiler_params=pltpu.CompilerParams(vmem_limit_bytes=SMALL),
+        compiler_params=pltpu.CompilerParams(vmem_limit_bytes=LARGE),
     )(c[None], attn, weights)
-    terms, weights = lax.optimization_barrier((terms, weights))
-    swapped = lax.ppermute(weights, "c", [(0, 1), (1, 0)])
+    cores = lax.all_gather(weights, "c", axis=0)
     parts = lax.all_to_all(terms, ("c", "x"), 0, 0)
     w1, w2 = kernel_call(
         unmix_body,
         [shape((2048, 768), BF16), shape((2048, 384), BF16)],
         0,
         [pltpu.VMEM((2, 16, 4, 144, 128), BF16), pltpu.SemaphoreType.DMA((2,))],
-        core=c[None],
-        n_far=2,
+        n_far=1,
         grant=LARGE,
-    )(weights, swapped)
+    )(cores)
     halves = jnp.sum(parts.reshape(2, 4, 64, 256).astype(F32), axis=1)
     at = np.arange(256, dtype=np.int32)
     at = (at // 16) * 32 + at % 16 + 16 * np.arange(2, dtype=np.int32)[:, None]

time: 172 us -> 176 us (1.023)
  waiting for transfers between devices: 8.19 us -> 13.7 us
  starting transfers between devices: 25.9 us -> 21.6 us
  blocking collectives: 95.4 us -> 98.3 us
    all_gather x0 -> x1, waiting for transfers between devices: none -> 8.83 us  [on_device(): cores = lax.all_gather(weights, 'c', axis=0)]
    pallas_call x3 -> x2, Pallas kernels: 7.24 us -> 2.15 us  [kernel_call(): return call if core is None else lambda *args: call(core, *args)]
    pallas_call x0 -> x1, Pallas kernels: none -> 5.02 us  [on_device(): kernel_call(unmix_body, [shape((2048, 768), BF16), shape((2048, 384), BF1...]
    ppermute x1 -> x0, starting transfers between devices: 3.81 us -> none  [on_device(): swapped = lax.ppermute(weights, 'c', [(0, 1), (1, 0)])]
    all_to_all x1, waiting for transfers between devices: 3.35 us -> 0.01 us  [on_device(): lax.all_to_all(jnp.broadcast_to(resid[None], (8, 64, 512)), ('yl', 'x'),...]
  transfers between devices with their start and end apart: 6 -> 6, of which waited for: 3 -> 3; matrix products, arithmetic and copies ran while one was open for 1% -> 1% of each run, Pallas kernels for 8% -> 9%
where the time goes in v15:
time: 176 us; the launch traced here: 175 us
  blocking collectives  98.3 us (56%)
  Pallas kernels  22.8 us (13%)
  starting transfers between devices  21.6 us (12%)
  waiting for transfers between devices  13.7 us (8%)
  between operations  13.6 us (8%)
  local copies, waits for them, and re-layouts  2.92 us (2%)
    all_gather x1, blocking collectives, on_device(): mine = jnp.sum(lax.all_gather(mine, 'z', axis=0), axis=0)  32.9 us
    all_to_all x1, blocking collectives, on_device(): parts = lax.all_to_all(terms, ('yl', 'x'), 0, 0)  14.1 us
    all_to_all x1, blocking collectives, on_device(): gathered = lax.all_to_all(gathered, (*y_axes, 'c'), 0, 0)  11.9 us
    all_to_all x1, blocking collectives, on_device(): parts = lax.all_to_all(terms, ('c', 'x'), 0, 0)  11.8 us
    all_to_all x1, blocking collectives, on_device(): got = lax.all_to_all(pack, y_axes, 0, 0)  11.3 us
    all_gather x1, blocking collectives, on_device(): heads = lax.all_gather(heads, y_axes, axis=0)  10.6 us
    all_gather x1, waiting for transfers between devices, on_device(): cores = lax.all_gather(weights, 'c', axis=0)  8.83 us
    ppermute x1, starting transfers between devices, on_device(): other = lax.ppermute(got, 'c', [(0, 1), (1, 0)])  8.35 us
  transfers between devices with their start and end apart: 6, of which 3 were waited for; matrix products, arithmetic and copies ran while one was open for 1% of the time, Pallas kernels for 9%

profile of v15, /device:TPU:1, one launch (start us, length us, event | category | flops | bytes accessed | tf_op | source)
XLA Modules:
  0.0 175.0 jit_solution(13405385212631189135)
XLA Ops:
  6.5 0.0 copy-start.1
  6.5 0.0 all-gather.7.cloned.1.call-start
  6.5 1.8 %shard_map.109 = bf16[4,400,128]{2,1,0:T(8,128)(2,1)} custom-call(bf16[64,512]{1,0:T(8,128)(2,1)} %mine.1, bf16[64,512]{1,0:T(8,128)(2,1)} %k.1, bf16[64,512]{1,0:T(8,128)(2,1)} %v.1, bf16[16,768]{1,0:T(8,128)(2,1)} %wg.1, bf16[16,768]{1,0:T(8,128)(2,1)} %wu.1, bf16[16,768]{1,0:T(8,128)(2,1)} %bitcast.29, bf16[16,512]{1,0:T(8,128)(2,1)} %bitcast.30), custom_call_target="tpu_custom_call" | custom-call | tf_op jit(solution)/shard_map/pallas_call | solution.py:226
  8.3 11.3 %all_to_all.30.mine = bf16[4,400,128]{2,1,0:T(8,128)(2,1)S(1)} all-to-all(bf16[4,400,128]{2,1,0:T(8,128)(2,1)} %shard_map.109), channel_id=1, replica_groups=mesh['z'=16,'yh'=2,'yl'=2,'c'=2,'x'=4] {'yh','yl'}, dimensions={0} | all-to-all | bytes 819200 | tf_op jit(solution)/shard_map/all_to_all | solution.py:229
  19.7 0.7 slice.4
  20.4 0.0 all-gather.7.cloned.1.call-update
  20.4 8.4 %collective-permute-start = (bf16[4,400,128]{2,1,0:T(8,128)(2,1)S(1)}, bf16[4,400,128]{2,1,0:T(8,128)(2,1)S(1)}, u32[]{:S(2)}, u32[]{:S(2)}) collective-permute-start(bf16[4,400,128]{2,1,0:T(8,128)(2,1)S(1)} %all_to_all.30.mine), channel_id=1, source_target_pairs={{0,4},{4,0},{1,5},{5,1},{2,6},{6,2},{3,7},{7,3},{8,12},{12,8},{9,1... | collective-permute-start | bytes 1228808 | tf_op jit(solution)/shard_map/ppermute | solution.py:231
  28.7 0.1 pad_add_fusion.place
  28.8 0.7 fusion.3
  29.5 0.6 collective-permute-done.other
  30.1 0.8 shard_map.110
  30.8 32.9 %all-gather.1 = f32[1024,128]{1,0:T(8,128)S(1)} all-gather(f32[64,128]{1,0:T(8,128)S(1)} %shard_map.110), channel_id=3, replica_groups=mesh['z'=16,'yh'=2,'yl'=2,'c'=2,'x'=4] {'z'}, dimensions={0}, use_global_device_ids=true | all-gather | bytes 557056 | tf_op jit(solution)/shard_map/all_gather | solution.py:237
  63.8 0.1 bitcast_divide_fusion
  63.9 5.7 %all_gather.32.marks = f32[2,64,128]{2,1,0:T(8,128)S(1)} all-gather(f32[1,64,128]{2,1,0:T(8,128)S(1)} %bitcast_divide_fusion), channel_id=1, replica_groups=mesh['z'=16,'yh'=2,'yl'=2,'c'=2,'x'=4] {'c'}, dimensions={0}, use_global_device_ids=true | all-gather | bytes 98304 | tf_op jit(solution)/shard_map/all_gather | solution.py:238
  69.6 1.4 shard_map.111
  71.0 7.0 %all-to-all-start.1 = ((f32[16,40,128]{2,1,0:T(8,128)}), f32[16,40,128]{2,1,0:T(8,128)S(1)}, u32[]{:S(2)}, u32[]{:S(2)}) async-start(f32[16,40,128]{2,1,0:T(8,128)} %shard_map.111), calls=%async_computation.1 | async-start | bytes 655360 | tf_op jit(solution)/shard_map/all_to_all | solution.py:240
  78.0 0.0 all-gather.9.cloned.1.call-start
  78.0 0.0 copy-done.1
  78.1 2.5 %collective-permute-start.1 = (bf16[64,512]{1,0:T(8,128)(2,1)S(1)}, bf16[64,512]{1,0:T(8,128)(2,1)S(1)}, u32[]{:S(2)}, u32[]{:S(2)}) collective-permute-start(bf16[64,512]{1,0:T(8,128)(2,1)S(1)} %copy-done.1), channel_id=1, source_target_pairs={{0,4},{4,0},{1,5},{5,1},{2,6},{6,2},{3,7},{7,3},{8,12},{12,8},{9,1... | collective-permute-start | bytes 196616 | tf_op jit(solution)/shard_map/ppermute | solution.py:248
  80.6 4.5 %shard_map.112 = f32[2,64,128]{2,1,0:T(8,128)S(1)} custom-call(f32[2,64,128]{2,1,0:T(8,128)S(1)} %all_gather.32.marks), custom_call_target="tpu_custom_call" | custom-call | flops 1000000000 | bytes 20000000 | tf_op jit(solution)/shard_map/pallas_call | solution.py:241
  85.1 10.6 %all-gather.2 = f32[8,64,128]{2,1,0:T(8,128)S(1)} all-gather(f32[2,64,128]{2,1,0:T(8,128)S(1)} %shard_map.112), channel_id=4, replica_groups=mesh['z'=16,'yh'=2,'yl'=2,'c'=2,'x'=4] {'yh','yl'}, dimensions={0}, use_global_device_ids=true | all-gather | bytes 327680 | tf_op jit(solution)/shard_map/all_gather | solution.py:247
  95.7 0.0 collective-permute-done.1.other
  95.7 0.7 shard_map.113.near
  96.4 4.2 %all-to-all-done.1.parts = f32[16,40,128]{2,1,0:T(8,128)S(1)} async-done(((f32[16,40,128]{2,1,0:T(8,128)}), f32[16,40,128]{2,1,0:T(8,128)S(1)}, u32[]{:S(2)}, u32[]{:S(2)}) %all-to-all-start.1) | async-done | bytes 327712 | tf_op jit(solution)/shard_map/all_to_all | solution.py:240
  100.6 0.2 shard_map.114
  100.8 11.9 %all_to_all.31.gathered = f32[8,32,128]{2,1,0:T(8,128)S(1)} all-to-all(f32[8,32,128]{2,1,0:T(8,128)S(1)} %shard_map.114), channel_id=1, replica_groups=mesh['z'=16,'yh'=2,'yl'=2,'c'=2,'x'=4] {'yh','yl','c'}, dimensions={0} | all-to-all | bytes 262144 | tf_op jit(solution)/shard_map/all_to_all | solution.py:252
  112.8 0.7 shard_map.115.attn
  113.5 0.0 copy-start
  113.5 0.0 all-gather.7.cloned.1.call-done
  113.5 0.0 copy-start.3
  113.5 0.0 copy-start.4
  113.5 0.0 all-gather.9.cloned.1.call-update
  113.6 0.6 copy-done
  114.1 2.5 %shard_map.116 = bf16[8,64,256]{2,1,0:T(8,128)(2,1)} custom-call(s32[1]{0:T(128)} %bitcast.core, bf16[128,512]{1,0:T(8,128)(2,1)} %copy-done, bf16[16,4,208,128]{3,2,1,0:T(8,128)(2,1)} %bitcast.26), custom_call_target="tpu_custom_call" | custom-call | tf_op jit(solution)/shard_map/pallas_call | solution.py:256
  116.7 11.8 %all_to_all.32 = bf16[8,64,256]{2,1,0:T(8,128)(2,1)S(1)} all-to-all(bf16[8,64,256]{2,1,0:T(8,128)(2,1)} %shard_map.116), channel_id=1, replica_groups=mesh['z'=16,'yh'=2,'yl'=2,'c'=2,'x'=4] {'c','x'}, dimensions={0} | all-to-all | bytes 524288 | tf_op jit(solution)/shard_map/all_to_all | solution.py:270
  128.5 0.0 copy-done.3
  128.5 0.0 copy-done.4
  128.5 0.6 fusion.1
  129.1 0.8 broadcast_in_dim.20
  129.9 3.6 %all-to-all-start.4 = ((bf16[8,64,512]{2,1,0:T(8,128)(2,1)}), bf16[8,64,512]{2,1,0:T(8,128)(2,1)S(1)}, u32[]{:S(2)}, u32[]{:S(2)}) async-start(bf16[8,64,512]{2,1,0:T(8,128)(2,1)} %broadcast_in_dim.20), calls=%async_computation.4 | async-start | bytes 1048576 | tf_op jit(solution)/shard_map/all_to_all | solution.py:285
  133.5 8.8 %all-gather.9.cloned.1.call-done = bf16[32,4,208,128]{3,2,1,0:T(8,128)(2,1)} async-done(((bf16[16,4,208,128]{3,2,1,0:T(8,128)(2,1)}), bf16[32,4,208,128]{3,2,1,0:T(8,128)(2,1)}) %all-gather.9.cloned.1.call-update) | async-done | bytes 6815760 | tf_op jit(solution)/shard_map/all_gather | solution.py:269
  142.3 5.0 %shard_map.117 = (bf16[2048,768]{1,0:T(8,128)(2,1)}, bf16[2048,384]{1,0:T(8,128)(2,1)}) custom-call(bf16[2,16,4,208,128]{4,3,2,1,0:T(8,128)(2,1)} %bitcast.27), custom_call_target="tpu_custom_call" | custom-call | tf_op jit(solution)/shard_map/pallas_call | solution.py:271
  147.4 0.0 all-to-all-done.4.whole
  147.4 0.0 copy-start.2
  147.4 0.8 copy-done.2
  148.2 5.1 %shard_map.118 = bf16[8,64,512]{2,1,0:T(8,128)(2,1)} custom-call(bf16[8,64,512]{2,1,0:T(8,128)(2,1)} %copy-done.2, f32[1,2048]{1,0:T(1,128)} %bitcast.31, bf16[2048,768]{1,0:T(8,128)(2,1)} %get-tuple-element.17.far1, bf16[2048,384]{1,0:T(8,128)(2,1)} %get-tuple-element.18.far2), custom_call_target="tpu_custom_call" | custom-call | tf_op jit(solution)/shard_map/pallas_call | solution.py:286
  153.3 14.1 %all_to_all.33 = bf16[8,64,512]{2,1,0:T(8,128)(2,1)S(1)} all-to-all(bf16[8,64,512]{2,1,0:T(8,128)(2,1)} %shard_map.118), channel_id=1, replica_groups=mesh['z'=16,'yh'=2,'yl'=2,'c'=2,'x'=4] {'yl','x'}, dimensions={0} | all-to-all | bytes 1048576 | tf_op jit(solution)/shard_map/all_to_all | solution.py:299
  167.4 0.1 convert_reduce_fusion
  167.5 0.6 add_convert_fusion
  (2 shorter events, 0.1 us)
Async XLA Ops:
  6.5 71.5 %copy-start.1 = (bf16[64,512]{1,0:T(8,128)(2,1)S(1)}, bf16[64,512]{1,0:T(8,128)(2,1)}, u32[]{:S(2)}) copy-start(bf16[64,512]{1,0:T(8,128)(2,1)} %mine.1) | copy-start | bytes 196612
  6.5 107.0 %all-gather.7.cloned.1.call-start = ((), (), s32[]{:S(2)}) async-start(), calls=%async_computation.6 | async-start | bytes 3620864 | tf_op jit(solution)/shard_map/all_gather | solution.py:230
  20.4 9.7 %collective-permute-start = (bf16[4,400,128]{2,1,0:T(8,128)(2,1)S(1)}, bf16[4,400,128]{2,1,0:T(8,128)(2,1)S(1)}, u32[]{:S(2)}, u32[]{:S(2)}) collective-permute-start(bf16[4,400,128]{2,1,0:T(8,128)(2,1)S(1)} %all_to_all.30.mine), channel_id=1, source_target_pairs={{0,4},{4,0},{1,5},{5,1},{2,6},{6,2},{3,7},{7,3},{8,12},{12,8},{9,1... | collective-permute-start | bytes 1228808 | tf_op jit(solution)/shard_map/ppermute | solution.py:231
  71.0 29.6 %all-to-all-start.1 = ((f32[16,40,128]{2,1,0:T(8,128)}), f32[16,40,128]{2,1,0:T(8,128)S(1)}, u32[]{:S(2)}, u32[]{:S(2)}) async-start(f32[16,40,128]{2,1,0:T(8,128)} %shard_map.111), calls=%async_computation.1 | async-start | bytes 655360 | tf_op jit(solution)/shard_map/all_to_all | solution.py:240
  78.0 64.3 %all-gather.9.cloned.1.call-start = ((), (), s32[]{:S(2)}) async-start(), calls=%async_computation.7 | async-start | bytes 10223616 | tf_op jit(solution)/shard_map/all_gather | solution.py:269
  78.1 17.7 %collective-permute-start.1 = (bf16[64,512]{1,0:T(8,128)(2,1)S(1)}, bf16[64,512]{1,0:T(8,128)(2,1)S(1)}, u32[]{:S(2)}, u32[]{:S(2)}) collective-permute-start(bf16[64,512]{1,0:T(8,128)(2,1)S(1)} %copy-done.1), channel_id=1, source_target_pairs={{0,4},{4,0},{1,5},{5,1},{2,6},{6,2},{3,7},{7,3},{8,12},{12,8},{9,1... | collective-permute-start | bytes 196616 | tf_op jit(solution)/shard_map/ppermute | solution.py:248
  113.5 0.7 copy-start
  113.5 15.0 %copy-start.3 = (bf16[64,512]{1,0:T(8,128)(2,1)S(1)}, bf16[64,512]{1,0:T(8,128)(2,1)}, u32[]{:S(2)}) copy-start(bf16[64,512]{1,0:T(8,128)(2,1)} %param.14) | copy-start | bytes 196612
  113.5 15.0 %copy-start.4 = (s32[2,256]{1,0:T(2,128)S(1)}, s32[2,256]{1,0:T(2,128)}, u32[]{:S(2)}) copy-start(s32[2,256]{1,0:T(2,128)} %constant.25) | copy-start | bytes 6148
  129.9 17.5 %all-to-all-start.4 = ((bf16[8,64,512]{2,1,0:T(8,128)(2,1)}), bf16[8,64,512]{2,1,0:T(8,128)(2,1)S(1)}, u32[]{:S(2)}, u32[]{:S(2)}) async-start(bf16[8,64,512]{2,1,0:T(8,128)(2,1)} %broadcast_in_dim.20), calls=%async_computation.4 | async-start | bytes 1048576 | tf_op jit(solution)/shard_map/all_to_all | solution.py:285
  147.4 0.8 copy-start.2
Sparse Core Ops, SparseCore 0:
  20.5 87.1 all-gather.6
  113.7 28.6 all-gather.8
